TPU v7x, 32 devices: a whole 2x2x4 slice. The times are simulated.
32 devices in a mesh: ctx: 8 (over z, core), fsdp: 4 (over y, x).
Axes of the slice: x: 2, y: 2, z: 4, core: 2. Of those that a mesh axis runs over, the one named last changes fastest.
Arguments:
- tokens: bfloat16 [4, 2048, 2048], P('fsdp', 'ctx'), may hold values from -6 to 6
- seq_ids: int32 [4, 2048], P('fsdp', 'ctx'), may hold values from 0 to 1, as said below
- positions: int32 [4, 2048], P('fsdp', 'ctx'), may hold values from 0 to 1791, as said below
- block_ids: int32 [4, 2048], P('fsdp', 'ctx'), may hold values from 0 to 6, as said below
- gain_attn: float32 [2048], P(('ctx', 'fsdp')), may hold values from 0.5 to 1.5
- w_query: float32 [2048, 2048], P(('ctx', 'fsdp')), may hold values from -0.4375 to 0.4375
- key_weight_matrix: float32 [2048, 512], P(('ctx', 'fsdp')), may hold values from -0.4375 to 0.4375
- value_weight_matrix: float32 [2048, 512], P(('ctx', 'fsdp')), may hold values from -0.125 to 0.125
- w_out: float32 [2048, 2048], P(('ctx', 'fsdp')), may hold values from -4 to 4
- gain_mlp: float32 [2048], P(('ctx', 'fsdp')), may hold values from 0.5 to 1.5
- w_gate: float32 [2048, 8192], P(('ctx', 'fsdp')), may hold values from -0.125 to 0.125
- w_up: float32 [2048, 8192], P(('ctx', 'fsdp')), may hold values from -0.125 to 0.125
- w_down: float32 [2048, 8192], P(('ctx', 'fsdp')), may hold values from -0.625 to 0.625
- out_grad: bfloat16 [4, 2048, 2048], P('fsdp', 'ctx'), may hold values from -6 to 6
Outputs:
- layer_out: bfloat16 [4, 2048, 2048], P('fsdp', 'ctx')
- input_grad: float32 [4, 2048, 2048], P('fsdp', 'ctx')
- grad_gain_attn: float32 [2048], P(('ctx', 'fsdp'))
- grad_query: float32 [2048, 2048], P(('ctx', 'fsdp'))
- grad_key: float32 [2048, 512], P(('ctx', 'fsdp'))
- grad_value: float32 [2048, 512], P(('ctx', 'fsdp'))
- grad_out: float32 [2048, 2048], P(('ctx', 'fsdp'))
- grad_gain_mlp: float32 [2048], P(('ctx', 'fsdp'))
- grad_gate: float32 [2048, 8192], P(('ctx', 'fsdp'))
- grad_up: float32 [2048, 8192], P(('ctx', 'fsdp'))
- grad_down: float32 [2048, 8192], P(('ctx', 'fsdp'))
Inputs may be any that keep to these rules, and one draw needn't show every extreme that they name: `seq_ids`: each row of 2048 tokens holds two sequences, ids 0 then 1, each of 256 tokens or more. `positions`: A token's place within its sequence, counted from 0. `block_ids`: the token's position divided by 256, rounded down.
All inputs are finite; a program needn't handle non-finite values.
Results may differ from a plain program's by a relative error of at most 0.025.
Values may be sent and summed in bfloat16 or wider, within the bound.
A program may use at most 1.125 GiB of HBM per device.

v0:
```python
import math

import jax
import jax.numpy as jnp
from jax import lax
from jax.sharding import PartitionSpec as P

MODEL_WIDTH = 2048
QUERY_HEADS = 32
KEY_VALUE_HEADS = 8
HEAD_SIZE = 64
FF = 8192


eps_norm = 1e-05
rope_base = 10000000.0
attention_score_scale = 0.015625
residual_scale = 0.22
negative_filler = -1e30


def from_behind(value, axis, by):
    length = lax.axis_size(axis)
    return lax.ppermute(value, axis, [(i, (i + by) % length) for i in range(length)])


def rms_parts(values):
    inverse = lax.rsqrt(jnp.mean(values * values, axis=-1, keepdims=True) + eps_norm)
    return (values * inverse, inverse)


def rms_backward(normalized_input, inverse, grad_normed):
    return inverse * (
        grad_normed
        - normalized_input * jnp.mean(grad_normed * normalized_input, axis=-1, keepdims=True)
    )


def rope_tables(places):
    frequency = rope_base ** (-(jnp.arange(HEAD_SIZE // 2, dtype=jnp.float32) * 2.0) / HEAD_SIZE)
    angles = places.astype(jnp.float32)[:, None] * frequency[None, :]
    return (jnp.cos(angles)[:, None, :], jnp.sin(angles)[:, None, :])


def apply_rotation(values, cosine_table, sine_table):
    middle = values.shape[-1] // 2
    first_half = values[..., :middle]
    second = values[..., middle:]
    return jnp.concatenate(
        [
            first_half * cosine_table - second * sine_table,
            second * cosine_table + first_half * sine_table,
        ],
        axis=-1,
    )


def rotation_backward(grad_rot, cosine_table, sine_table):
    middle = grad_rot.shape[-1] // 2
    first_half = grad_rot[..., :middle]
    second = grad_rot[..., middle:]
    return jnp.concatenate(
        [
            first_half * cosine_table + second * sine_table,
            second * cosine_table - first_half * sine_table,
        ],
        axis=-1,
    )


def contract_rows(left, right):
    return lax.dot_general(
        left, right, (((0,), (0,)), ((), ())), preferred_element_type=jnp.float32
    )


def contract_cols(left, right):
    return lax.dot_general(
        left, right, (((1,), (1,)), ((), ())), preferred_element_type=jnp.float32
    )


def local(
    tokens,
    seq_ids,
    positions,
    block_ids,
    gain_attn,
    w_query,
    key_weight_matrix,
    value_weight_matrix,
    w_out,
    gain_mlp,
    w_gate,
    w_up,
    w_down,
    out_grad,
):
    inputs = tokens[0].astype(jnp.float32)
    seq_here = seq_ids[0]
    block_here = block_ids[0]
    local_row_count = inputs.shape[0]
    heads_per_group = QUERY_HEADS // KEY_VALUE_HEADS
    query_stop_index = QUERY_HEADS * HEAD_SIZE
    key_stop_index = query_stop_index + KEY_VALUE_HEADS * HEAD_SIZE
    value_stop_index = key_stop_index + KEY_VALUE_HEADS * HEAD_SIZE
    cosine_table, sine_table = rope_tables(positions[0])
    attn_pack = (
        w_query.astype(jnp.bfloat16),
        key_weight_matrix.astype(jnp.bfloat16),
        value_weight_matrix.astype(jnp.bfloat16),
        gain_attn.astype(jnp.bfloat16),
    )
    mlp_pack = (
        w_gate.astype(jnp.bfloat16),
        w_up.astype(jnp.bfloat16),
        gain_mlp.astype(jnp.bfloat16),
    )
    out_rows = w_out.astype(jnp.bfloat16)
    down_rows = w_down.astype(jnp.bfloat16)

    def fold_attn(update, initial):
        return update(
            initial,
            (
                lax.all_gather(attn_pack[0], ("ctx", "fsdp"), axis=0, tiled=True),
                lax.all_gather(attn_pack[1], ("ctx", "fsdp"), axis=0, tiled=True),
                lax.all_gather(attn_pack[2], ("ctx", "fsdp"), axis=0, tiled=True),
                lax.all_gather(attn_pack[3], ("ctx", "fsdp"), axis=0, tiled=True),
            ),
            jnp.int32(0),
        )

    def fold_out(update, initial):
        return update(
            initial, lax.all_gather(out_rows, ("ctx", "fsdp"), axis=0, tiled=True), jnp.int32(0)
        )

    def fold_mlp(update, initial):
        return update(
            initial,
            (
                lax.all_gather(mlp_pack[0], ("ctx", "fsdp"), axis=0, tiled=True),
                lax.all_gather(mlp_pack[1], ("ctx", "fsdp"), axis=0, tiled=True),
                lax.all_gather(mlp_pack[2], ("ctx", "fsdp"), axis=0, tiled=True),
            ),
            jnp.int32(0),
        )

    def fold_down(update, initial):
        return update(
            initial, lax.all_gather(down_rows, ("ctx", "fsdp"), axis=0, tiled=True), jnp.int32(0)
        )

    normed_one, inverse_one = rms_parts(inputs)

    def project_in(running, pieces, offset):
        scaled = (normed_one * pieces[3].astype(jnp.float32)[None, :]).astype(jnp.bfloat16)
        joined = jnp.concatenate([pieces[0], pieces[1], pieces[2]], axis=1)
        return (jnp.dot(scaled, joined, preferred_element_type=jnp.float32), scaled)

    projected_output, normed_attn = fold_attn(
        project_in,
        (
            jnp.zeros((local_row_count, value_stop_index), jnp.float32),
            jnp.zeros((local_row_count, MODEL_WIDTH), jnp.bfloat16),
        ),
    )
    query_block_slice = apply_rotation(
        projected_output[:, :query_stop_index].reshape(local_row_count, QUERY_HEADS, HEAD_SIZE),
        cosine_table,
        sine_table,
    ).astype(jnp.bfloat16)
    query_grouped = query_block_slice.reshape(
        local_row_count, KEY_VALUE_HEADS, heads_per_group, HEAD_SIZE
    )
    key_b = (
        apply_rotation(
            projected_output[:, query_stop_index:key_stop_index].reshape(
                local_row_count, KEY_VALUE_HEADS, HEAD_SIZE
            ),
            cosine_table,
            sine_table,
        )
        .astype(jnp.bfloat16)
        .reshape(local_row_count, KEY_VALUE_HEADS * HEAD_SIZE)
    )
    value_b = projected_output[:, key_stop_index:].astype(jnp.bfloat16)

    def visible(seg_keys, blk_keys):
        return (seq_here[:, None] == seg_keys[None, :]) & (blk_keys[None, :] <= block_here[:, None])

    start_state = (
        jnp.full((KEY_VALUE_HEADS, heads_per_group, local_row_count), negative_filler, jnp.float32),
        jnp.zeros((KEY_VALUE_HEADS, heads_per_group, local_row_count), jnp.float32),
        jnp.zeros((KEY_VALUE_HEADS, heads_per_group, local_row_count, HEAD_SIZE), jnp.float32),
    )
    key_row_slice = lax.all_gather(key_b, "ctx", axis=0, tiled=True)
    value_row_slice = lax.all_gather(value_b, "ctx", axis=0, tiled=True)
    seg_keys = lax.all_gather(seq_here, "ctx", axis=0, tiled=True)
    blk_keys = lax.all_gather(block_here, "ctx", axis=0, tiled=True)
    key_total_count = key_row_slice.shape[0]
    block_row_count = math.gcd(key_total_count, 512)

    def attend_one_block(current, block_index):
        first_row = block_index * block_row_count
        key_block_slice = lax.dynamic_slice_in_dim(
            key_row_slice, first_row, block_row_count, 0
        ).reshape(block_row_count, KEY_VALUE_HEADS, HEAD_SIZE)
        value_block_slice = lax.dynamic_slice_in_dim(
            value_row_slice, first_row, block_row_count, 0
        ).reshape(block_row_count, KEY_VALUE_HEADS, HEAD_SIZE)
        allowed = visible(
            lax.dynamic_slice_in_dim(seg_keys, first_row, block_row_count, 0),
            lax.dynamic_slice_in_dim(blk_keys, first_row, block_row_count, 0),
        )

        def attend_compute(state_now):
            row_max, row_sum, weighted = state_now
            scores = (
                jnp.einsum(
                    "tkgd,skd->kgts",
                    query_grouped,
                    key_block_slice,
                    preferred_element_type=jnp.float32,
                )
                * attention_score_scale
            )
            scores = jnp.where(allowed[None, None], scores, negative_filler)
            new_max = jnp.maximum(row_max, jnp.max(scores, axis=-1))
            weights = jnp.where(allowed[None, None], jnp.exp(scores - new_max[..., None]), 0.0)
            shrink = jnp.exp(row_max - new_max)
            row_sum = row_sum * shrink + jnp.sum(weights, axis=-1)
            weighted = weighted * shrink[..., None] + jnp.einsum(
                "kgts,skd->kgtd",
                weights.astype(jnp.bfloat16),
                value_block_slice,
                preferred_element_type=jnp.float32,
            )
            return (new_max, row_sum, weighted)

        def unchanged(state_now):
            return state_now

        return (lax.cond(jnp.any(allowed), attend_compute, unchanged, current), None)

    result, unused = lax.scan(
        attend_one_block, start_state, jnp.arange(key_total_count // block_row_count)
    )
    row_max, row_sum, weighted = result
    attention_result = jnp.transpose(weighted / row_sum[..., None], (2, 0, 1, 3))
    log_sum = row_max + jnp.log(row_sum)
    attended_b = attention_result.reshape(local_row_count, QUERY_HEADS * HEAD_SIZE).astype(
        jnp.bfloat16
    )

    def out_columns(running, pieces, offset):
        return contract_cols(attended_b, pieces)

    attn_branch = fold_out(out_columns, jnp.zeros((local_row_count, MODEL_WIDTH), jnp.float32))
    hidden = inputs + residual_scale * attn_branch
    normed_two, inverse_two = rms_parts(hidden)

    def mlp_in(running, pieces, offset):
        scaled = (normed_two * pieces[2].astype(jnp.float32)[None, :]).astype(jnp.bfloat16)
        joined = jnp.concatenate([pieces[0], pieces[1]], axis=1)
        return (jnp.dot(scaled, joined, preferred_element_type=jnp.float32), scaled)

    gate_up, normed_mlp = fold_mlp(
        mlp_in,
        (
            jnp.zeros((local_row_count, 2 * FF), jnp.float32),
            jnp.zeros((local_row_count, MODEL_WIDTH), jnp.bfloat16),
        ),
    )
    gate = gate_up[:, :FF]
    up_vals = gate_up[:, FF:]
    sigmoid_gate = jax.nn.sigmoid(gate)
    act_b = (gate * sigmoid_gate * up_vals).astype(jnp.bfloat16)

    def down_columns(running, pieces, offset):
        return contract_cols(act_b, pieces)

    mlp_branch = fold_down(down_columns, jnp.zeros((local_row_count, MODEL_WIDTH), jnp.float32))
    layer_out = (hidden + residual_scale * mlp_branch).astype(jnp.bfloat16)[None]
    upstream = out_grad[0].astype(jnp.float32)
    mlp_grad_b = (residual_scale * upstream).astype(jnp.bfloat16)

    def down_back(running, pieces, offset):
        return jnp.dot(mlp_grad_b, pieces, preferred_element_type=jnp.float32)

    act_grad = fold_down(down_back, jnp.zeros((local_row_count, FF), jnp.float32))
    gate_grad_b = (act_grad * up_vals * sigmoid_gate * (1.0 + gate * (1.0 - sigmoid_gate))).astype(
        jnp.bfloat16
    )
    up_grad_b = (act_grad * gate * sigmoid_gate).astype(jnp.bfloat16)
    gate_up_grad = jnp.concatenate([gate_grad_b, up_grad_b], axis=1)

    def mlp_back(running, pieces, offset):
        joined = jnp.concatenate([pieces[0], pieces[1]], axis=1)
        spread = contract_cols(gate_up_grad, joined)
        gain_rows = pieces[2].astype(jnp.float32)
        return (spread * gain_rows[None, :], jnp.sum(normed_two * spread, axis=0))

    normed_grad_two, gain_grad_mlp = fold_mlp(
        mlp_back,
        (
            jnp.zeros((local_row_count, MODEL_WIDTH), jnp.float32),
            jnp.zeros((MODEL_WIDTH,), jnp.float32),
        ),
    )
    hidden_grad = upstream + rms_backward(normed_two, inverse_two, normed_grad_two)
    row_shard = lax.psum_scatter(
        jnp.concatenate(
            [contract_rows(normed_mlp, gate_up_grad), contract_rows(mlp_grad_b, act_b)], axis=1
        ).astype(jnp.bfloat16),
        "ctx",
        scatter_dimension=0,
        tiled=True,
    )
    mlp_shard = lax.psum_scatter(row_shard, "fsdp", scatter_dimension=0, tiled=True).astype(
        jnp.float32
    )
    attn_grad_b = (residual_scale * hidden_grad).astype(jnp.bfloat16)

    def out_back(running, pieces, offset):
        return jnp.dot(attn_grad_b, pieces, preferred_element_type=jnp.float32)

    attention_result_gradient = fold_out(
        out_back, jnp.zeros((local_row_count, QUERY_HEADS * HEAD_SIZE), jnp.float32)
    ).astype(jnp.bfloat16)
    gradient_grouped = attention_result_gradient.reshape(
        local_row_count, KEY_VALUE_HEADS, heads_per_group, HEAD_SIZE
    )
    delta = jnp.transpose(
        jnp.sum(gradient_grouped.astype(jnp.float32) * attention_result, axis=-1), (1, 2, 0)
    )

    def key_pass(key_row_slice, value_row_slice, seg_keys, blk_keys, query_grad):
        key_total_count = key_row_slice.shape[0]
        block_row_count = math.gcd(key_total_count, 512)

        def key_one_block(query_now, block_index):
            first_row = block_index * block_row_count
            key_block_slice = key_row_slice.reshape(block_row_count, KEY_VALUE_HEADS, HEAD_SIZE)
            value_block_slice = value_row_slice.reshape(block_row_count, KEY_VALUE_HEADS, HEAD_SIZE)
            allowed = visible(seg_keys, blk_keys)

            def key_compute(query_acc):
                scores = (
                    jnp.einsum(
                        "tkgd,skd->kgts",
                        query_grouped,
                        key_block_slice,
                        preferred_element_type=jnp.float32,
                    )
                    * attention_score_scale
                )
                weights = jnp.exp(
                    jnp.where(allowed[None, None], scores - log_sum[..., None], negative_filler)
                )
                weight_grad = jnp.einsum(
                    "tkgd,skd->kgts",
                    gradient_grouped,
                    value_block_slice,
                    preferred_element_type=jnp.float32,
                )
                score_grad = (weights * (weight_grad - delta[..., None])).astype(jnp.bfloat16)
                query_acc = query_acc + jnp.einsum(
                    "kgts,skd->tkgd",
                    score_grad,
                    key_block_slice,
                    preferred_element_type=jnp.float32,
                )
                key_gradient = jnp.einsum(
                    "kgts,tkgd->skd", score_grad, query_grouped, preferred_element_type=jnp.float32
                )
                value_gradient = jnp.einsum(
                    "kgts,tkgd->skd",
                    weights.astype(jnp.bfloat16),
                    gradient_grouped,
                    preferred_element_type=jnp.float32,
                )
                return (
                    query_acc,
                    key_gradient.reshape(block_row_count, KEY_VALUE_HEADS * HEAD_SIZE),
                    value_gradient.reshape(block_row_count, KEY_VALUE_HEADS * HEAD_SIZE),
                )

            def skipped(query_acc):
                return (
                    query_acc,
                    jnp.zeros((block_row_count, KEY_VALUE_HEADS * HEAD_SIZE), jnp.float32),
                    jnp.zeros((block_row_count, KEY_VALUE_HEADS * HEAD_SIZE), jnp.float32),
                )

            query_now, key_gradient, value_gradient = lax.cond(
                jnp.any(allowed), key_compute, skipped, query_now
            )
            return (query_now, (key_gradient, value_gradient))

        query_grad, key_pieces_list = lax.scan(
            key_one_block, query_grad, jnp.arange(key_total_count // block_row_count)
        )
        return (
            query_grad,
            key_pieces_list[0].reshape(key_total_count, KEY_VALUE_HEADS * HEAD_SIZE),
            key_pieces_list[1].reshape(key_total_count, KEY_VALUE_HEADS * HEAD_SIZE),
        )

    query_begin_index = jnp.zeros(
        (local_row_count, KEY_VALUE_HEADS, heads_per_group, HEAD_SIZE), jnp.float32
    )

    def cycle_step(step_index, current):
        key_row_slice, value_row_slice, seg_keys, blk_keys, key_acc, value_acc, query_grad = current
        query_grad, key_part, value_part = key_pass(
            key_row_slice, value_row_slice, seg_keys, blk_keys, query_grad
        )
        key_acc = key_acc + key_part
        value_acc = value_acc + value_part
        key_row_slice, value_row_slice, seg_keys, blk_keys = from_behind(
            (key_row_slice, value_row_slice, seg_keys, blk_keys), "ctx", 1
        )
        key_acc, value_acc = (
            from_behind(key_acc.astype(jnp.bfloat16), "ctx", 1).astype(key_acc.dtype),
            from_behind(value_acc.astype(jnp.bfloat16), "ctx", 1).astype(value_acc.dtype),
        )
        return (key_row_slice, value_row_slice, seg_keys, blk_keys, key_acc, value_acc, query_grad)

    blank_gradient = jnp.zeros((local_row_count, KEY_VALUE_HEADS * HEAD_SIZE), jnp.float32)
    final = lax.fori_loop(
        0,
        lax.axis_size("ctx"),
        cycle_step,
        (key_b, value_b, seq_here, block_here, blank_gradient, blank_gradient, query_begin_index),
    )
    key_gradient_total = final[4]
    value_grad_sum = final[5]
    query_grad = final[6]
    query_grad_b = (
        rotation_backward(
            (query_grad * attention_score_scale).reshape(local_row_count, QUERY_HEADS, HEAD_SIZE),
            cosine_table,
            sine_table,
        )
        .astype(jnp.bfloat16)
        .reshape(local_row_count, QUERY_HEADS * HEAD_SIZE)
    )
    key_grad_b = (
        rotation_backward(
            (key_gradient_total * attention_score_scale).reshape(
                local_row_count, KEY_VALUE_HEADS, HEAD_SIZE
            ),
            cosine_table,
            sine_table,
        )
        .astype(jnp.bfloat16)
        .reshape(local_row_count, KEY_VALUE_HEADS * HEAD_SIZE)
    )
    value_grad_b = value_grad_sum.astype(jnp.bfloat16)
    proj_grad = jnp.concatenate([query_grad_b, key_grad_b, value_grad_b], axis=1)

    def attn_back(running, pieces, offset):
        joined = jnp.concatenate([pieces[0], pieces[1], pieces[2]], axis=1)
        spread = contract_cols(proj_grad, joined)
        gain_rows = pieces[3].astype(jnp.float32)
        return (spread * gain_rows[None, :], jnp.sum(normed_one * spread, axis=0))

    normed_grad_one, gain_grad_attn = fold_attn(
        attn_back,
        (
            jnp.zeros((local_row_count, MODEL_WIDTH), jnp.float32),
            jnp.zeros((MODEL_WIDTH,), jnp.float32),
        ),
    )
    input_grad = hidden_grad + rms_backward(normed_one, inverse_one, normed_grad_one)
    attn_term = jnp.concatenate(
        [contract_rows(normed_attn, proj_grad), contract_rows(attn_grad_b, attended_b)], axis=1
    )
    attn_shard, gain_shard_attn, gain_shard_mlp = (
        lax.psum_scatter(attn_term, ("ctx", "fsdp"), scatter_dimension=0, tiled=True),
        lax.psum_scatter(gain_grad_attn, ("ctx", "fsdp"), scatter_dimension=0, tiled=True),
        lax.psum_scatter(gain_grad_mlp, ("ctx", "fsdp"), scatter_dimension=0, tiled=True),
    )
    return (
        layer_out,
        input_grad[None],
        gain_shard_attn,
        attn_shard[:, :query_stop_index],
        attn_shard[:, query_stop_index:key_stop_index],
        attn_shard[:, key_stop_index:value_stop_index],
        attn_shard[:, value_stop_index:],
        gain_shard_mlp,
        mlp_shard[:, :FF],
        mlp_shard[:, FF : 2 * FF],
        mlp_shard[:, 2 * FF :],
    )


def solution(mesh):
    return jax.shard_map(
        local,
        mesh=mesh,
        in_specs=(
            P("fsdp", "ctx", None),
            P("fsdp", "ctx"),
            P("fsdp", "ctx"),
            P("fsdp", "ctx"),
            P(("ctx", "fsdp")),
            P(("ctx", "fsdp"), None),
            P(("ctx", "fsdp"), None),
            P(("ctx", "fsdp"), None),
            P(("ctx", "fsdp"), None),
            P(("ctx", "fsdp")),
            P(("ctx", "fsdp"), None),
            P(("ctx", "fsdp"), None),
            P(("ctx", "fsdp"), None),
            P("fsdp", "ctx", None),
        ),
        out_specs=(
            P("fsdp", "ctx", None),
            P("fsdp", "ctx", None),
            P(("ctx", "fsdp")),
            P(("ctx", "fsdp"), None),
            P(("ctx", "fsdp"), None),
            P(("ctx", "fsdp"), None),
            P(("ctx", "fsdp"), None),
            P(("ctx", "fsdp")),
            P(("ctx", "fsdp"), None),
            P(("ctx", "fsdp"), None),
            P(("ctx", "fsdp"), None),
        ),
        check_vma=False,
    )
```

profile of v0, /device:TPU:0, one launch (start us, length us, event | category | flops | bytes accessed | tf_op | source)
XLA Modules:
  0.0 3155.2 jit_solution(6662788961164335775)
XLA Ops:
  14.0 42.4 %all-reduce.6 = (bf16[2048]{0:T(1024)(128)(2,1)S(1)}, bf16[2048]{0:T(1024)(128)(2,1)S(1)}) all-reduce(bf16[2048]{0:T(1024)(128)(2,1)S(1)} %dynamic-update-slice, bf16[2048]{0:T(1024)(128)(2,1)S(1)} %dynamic-update-slice.1), channel_id=1, replica_groups=mesh['ctx'=8,'fsdp'=4] {'ctx','fsdp'}, use_global_device_ids=true, to_apply=%add | all-reduce | flops 4096 | bytes 16384
  58.0 33.9 %all-gather.12.cloned.1.call-done = bf16[2048,2048]{1,0:T(8,128)(2,1)} async-done(((bf16[64,2048]{1,0:T(8,128)(2,1)}), bf16[2048,2048]{1,0:T(8,128)(2,1)}) %all-gather.12.cloned.1.call-update) | async-done | bytes 8388624 | tf_op jit(solution)/shard_map/all_gather | solution.py:126
  100.3 50.0 %all-gather.14.cloned.1.call-done = bf16[2048,512]{1,0:T(8,128)(2,1)} async-done(((bf16[64,512]{1,0:T(8,128)(2,1)}), bf16[2048,512]{1,0:T(8,128)(2,1)}) %all-gather.14.cloned.1.call-update) | async-done | bytes 2097168 | tf_op jit(solution)/shard_map/all_gather | solution.py:127
  153.5 55.6 %all-gather.16.cloned.1.call-done = bf16[2048,512]{1,0:T(8,128)(2,1)} async-done(((bf16[64,512]{1,0:T(8,128)(2,1)}), bf16[2048,512]{1,0:T(8,128)(2,1)}) %all-gather.16.cloned.1.call-update) | async-done | bytes 2097168 | tf_op jit(solution)/shard_map/all_gather | solution.py:128
  260.2 20.9 all-gather.18.cloned.1.call-done
  281.4 24.8 while.46
  284.3 13.1 conditional.5
  307.7 53.4 %all-gather.22.cloned.1.call-done = bf16[2048,2048]{1,0:T(8,128)(2,1)} async-done(((bf16[64,2048]{1,0:T(8,128)(2,1)}), bf16[2048,2048]{1,0:T(8,128)(2,1)}) %all-gather.22.cloned.1.call-update) | async-done | bytes 8388624 | tf_op jit(solution)/shard_map/all_gather | solution.py:136
  369.0 189.0 %all-gather.24.cloned.1.call-done = bf16[2048,8192]{1,0:T(8,128)(2,1)} async-done(((bf16[64,8192]{1,0:T(8,128)(2,1)}), bf16[2048,8192]{1,0:T(8,128)(2,1)}) %all-gather.24.cloned.1.call-update) | async-done | bytes 33554448 | tf_op jit(solution)/shard_map/all_gather | solution.py:143
  558.0 23.6 constant_dynamic-update-slice_fusion.4
  581.6 172.8 %all-gather.26.cloned.1.call-done = bf16[2048,8192]{1,0:T(8,128)(2,1)} async-done(((bf16[64,8192]{1,0:T(8,128)(2,1)}), bf16[2048,8192]{1,0:T(8,128)(2,1)}) %all-gather.26.cloned.1.call-update) | async-done | bytes 33554448 | tf_op jit(solution)/shard_map/all_gather | solution.py:144
  754.4 23.8 constant_dynamic-update-slice_fusion.3
  778.3 32.7 %fusion.58 = f32[256,16384]{1,0:T(8,128)} fusion(bf16[2048,16384]{1,0:T(8,128)(2,1)} %constant_dynamic-update-slice_fusion.3, f32[256,2048]{1,0:T(8,128)S(1)} %copy-done.9, f32[2048]{0:T(1024)S(1)} %copy-done.24, f32[256]{0:T(256)S(1)} %add_rsqrt_fusion), kind=kOutput, calls=%fused_computation.118 | convolution fusion | flops 17181442048 | bytes 85992448 | tf_op jit(solution)/shard_map/dot_general | solution.py:267
  811.0 139.3 %all-gather.28.cloned.1.call-done = bf16[2048,8192]{1,0:T(8,128)(2,1)} async-done(((bf16[64,8192]{1,0:T(8,128)(2,1)}), bf16[2048,8192]{1,0:T(8,128)(2,1)}) %all-gather.28.cloned.1.call-update) | async-done | bytes 33554448 | tf_op jit(solution)/shard_map/all_gather | solution.py:152
  950.3 28.6 multiply_convert_fusion.1
  978.9 16.0 convolution_convert_fusion.1
  994.9 29.1 convolution_convert_fusion
  1024.0 66.8 %pad_maximum_fusion = bf16[2048,24576]{1,0:T(8,128)(2,1)} fusion(bf16[2048,8192]{1,0:T(8,128)(2,1)} %convolution_convert_fusion.1, bf16[2048,16384]{1,0:T(8,128)(2,1)} %convolution_convert_fusion), kind=kLoop, calls=%fused_computation.33 | loop fusion | flops 201326592 | bytes 201326592 | tf_op jit(solution)/shard_map/concatenate | solution.py:314
  1094.1 31.2 multiply_reduce_fusion
  1140.7 405.4 %while.47 = (s32[]{:T(128)}, bf16[256,512]{0,1:T(8,128)(2,1)}, bf16[256,512]{0,1:T(8,128)(2,1)}, s32[256]{0:T(256)}, s32[256]{0:T(256)S(1)}, /*index=5*/f32[256,...) while((s32[]{:T(128)}, bf16[256,512]{0,1:T(8,128)(2,1)}, ...), condition=%wide.region_15.16_spmd.clone, body=%wide.region_11.15_spmd.clone.sunk | while | flops 1364983808 | bytes 63226456 | solution.py:432
  1180.6 15.1 collective-permute-done.2
  1231.2 15.1 collective-permute-done.2
  1281.9 15.1 collective-permute-done.2
  1332.5 15.1 collective-permute-done.2
  1383.9 14.3 collective-permute-done.2
  1486.2 13.3 collective-permute-done.2
  1570.0 28.5 pad_maximum_fusion.1
  1598.6 535.7 %reduce-scatter.10.cloned.1.call-done = bf16[256,24576]{1,0:T(8,128)(2,1)} async-done(((bf16[2048,24576]{1,0:T(8,128)(2,1)}), bf16[256,24576]{1,0:T(8,128)(2,1)}) %reduce-scatter.10.cloned.1.call-update) | async-done | bytes 12582928
  2144.5 47.4 %all-reduce.5 = (f32[2048]{0:T(1024)S(1)}, f32[2048]{0:T(1024)S(1)}) all-reduce(f32[2048]{0:T(1024)S(1)} %get-tuple-element.431, f32[2048]{0:T(1024)S(1)} %copy-done.40), channel_id=4, replica_groups=mesh['ctx'=8,'fsdp'=4] {'ctx','fsdp'}, use_global_device_ids=true, to_apply=%region_18.19.clone | all-reduce | flops 4096 | bytes 32768
  2196.6 17.4 fusion.30
  2214.0 805.0 %reduce-scatter.6.cloned.1.call-done = f32[64,5120]{1,0:T(8,128)} async-done(((f32[2048,5120]{1,0:T(8,128)}), f32[64,5120]{1,0:T(8,128)}) %reduce-scatter.6.cloned.1.call-update) | async-done | bytes 1310736 | tf_op jit(solution)/shard_map/reduce_scatter | solution.py:482
  3022.9 120.5 %reduce-scatter.8.cloned.1.call-done = bf16[64,24576]{1,0:T(8,128)(2,1)} async-done(((bf16[256,24576]{1,0:T(8,128)(2,1)}), bf16[64,24576]{1,0:T(8,128)(2,1)}) %reduce-scatter.8.cloned.1.call-update) | async-done | bytes 3145744 | tf_op jit(solution)/shard_map/reduce_scatter | solution.py:321
  (396 shorter events, 499.1 us)
Async XLA Ops:
  7.2 84.7 %all-gather.12.cloned.1.call-start = ((), (), s32[]{:S(2)}) async-start(), calls=%async_computation.3 | async-start | bytes 8650752 | tf_op jit(solution)/shard_map/all_gather | solution.py:126
  9.0 141.3 %all-gather.14.cloned.1.call-start = ((), (), s32[]{:S(2)}) async-start(), calls=%async_computation.4 | async-start | bytes 2162688 | tf_op jit(solution)/shard_map/all_gather | solution.py:127
  10.6 198.4 %all-gather.16.cloned.1.call-start = ((), (), s32[]{:S(2)}) async-start(), calls=%async_computation.5 | async-start | bytes 2162688 | tf_op jit(solution)/shard_map/all_gather | solution.py:128
  12.3 244.0 %all-gather.20.cloned.1.call-start = ((), (), s32[]{:S(2)}) async-start(), calls=%async_computation.7 | async-start | bytes 2359296 | tf_op jit(solution)/shard_map/all_gather | solution.py:199
  221.1 60.0 %all-gather.18.cloned.1.call-start = ((), (), s32[]{:S(2)}) async-start(), calls=%async_computation.6 | async-start | bytes 2359296 | tf_op jit(solution)/shard_map/all_gather | solution.py:198
  223.6 137.5 %all-gather.22.cloned.1.call-start = ((), (), s32[]{:S(2)}) async-start(), calls=%async_computation.8 | async-start | bytes 8650752 | tf_op jit(solution)/shard_map/all_gather | solution.py:136
  225.4 332.6 %all-gather.24.cloned.1.call-start = ((), (), s32[]{:S(2)}) async-start(), calls=%async_computation.9 | async-start | bytes 34603008 | tf_op jit(solution)/shard_map/all_gather | solution.py:143
  226.6 527.8 %all-gather.26.cloned.1.call-start = ((), (), s32[]{:S(2)}) async-start(), calls=%async_computation.10 | async-start | bytes 34603008 | tf_op jit(solution)/shard_map/all_gather | solution.py:144
  229.6 720.7 %all-gather.28.cloned.1.call-start = ((), (), s32[]{:S(2)}) async-start(), calls=%async_computation.11 | async-start | bytes 34603008 | tf_op jit(solution)/shard_map/all_gather | solution.py:152
  232.3 1902.0 %reduce-scatter.10.cloned.1.call-start = ((), (), s32[]{:S(2)}) async-start(), calls=%async_computation.14 | async-start | bytes 113246208
  1090.9 1928.1 %reduce-scatter.6.cloned.1.call-start = ((), (), s32[]{:S(2)}) async-start(), calls=%async_computation.12 | async-start | bytes 43253760 | tf_op jit(solution)/shard_map/reduce_scatter | solution.py:482
  1158.8 36.8 %collective-permute-start = (bf16[256,512]{0,1:T(8,128)(2,1)S(1)}, bf16[256,512]{0,1:T(8,128)(2,1)}, u32[]{:S(2)}, u32[]{:S(2)}) collective-permute-start(bf16[256,512]{0,1:T(8,128)(2,1)S(1)} %copy.111), channel_id=1, source_target_pairs={{0,4},{4,8},{8,12},{12,16},{16,20},{20,24},{24,28},{28,0},{1,5},{5... | collective-permute-start | bytes 786440 | tf_op jit(solution)/shard_map/while/body/eval_jaxpr/ppermute | solution.py:24
  1158.8 36.8 %collective-permute-start.1 = (bf16[256,512]{0,1:T(8,128)(2,1)}, bf16[256,512]{0,1:T(8,128)(2,1)}, u32[]{:S(2)}, u32[]{:S(2)}) collective-permute-start(bf16[256,512]{0,1:T(8,128)(2,1)} %copy.112), channel_id=1, source_target_pairs={{0,4},{4,8},{8,12},{12,16},{16,20},{20,24},{24,28},{28,0},{1,5},{5... | collective-permute-start | bytes 786440 | tf_op jit(solution)/shard_map/while/body/eval_jaxpr/ppermute | solution.py:24
  1160.8 34.8 %collective-permute-start.2 = (s32[256]{0:T(256)S(1)}, s32[256]{0:T(256)}, u32[]{:S(2)}, u32[]{:S(2)}) collective-permute-start(s32[256]{0:T(256)S(1)} %copy.113), channel_id=1, source_target_pairs={{0,4},{4,8},{8,12},{12,16},{16,20},{20,24},{24,28},{28,0},{1,5},{5... | collective-permute-start | bytes 3080 | tf_op jit(solution)/shard_map/while/body/eval_jaxpr/ppermute | solution.py:24
  1212.1 34.2 %collective-permute-start = (bf16[256,512]{0,1:T(8,128)(2,1)S(1)}, bf16[256,512]{0,1:T(8,128)(2,1)}, u32[]{:S(2)}, u32[]{:S(2)}) collective-permute-start(bf16[256,512]{0,1:T(8,128)(2,1)S(1)} %copy.111), channel_id=1, source_target_pairs={{0,4},{4,8},{8,12},{12,16},{16,20},{20,24},{24,28},{28,0},{1,5},{5... | collective-permute-start | bytes 786440 | tf_op jit(solution)/shard_map/while/body/eval_jaxpr/ppermute | solution.py:24
  1212.2 34.1 %collective-permute-start.1 = (bf16[256,512]{0,1:T(8,128)(2,1)}, bf16[256,512]{0,1:T(8,128)(2,1)}, u32[]{:S(2)}, u32[]{:S(2)}) collective-permute-start(bf16[256,512]{0,1:T(8,128)(2,1)} %copy.112), channel_id=1, source_target_pairs={{0,4},{4,8},{8,12},{12,16},{16,20},{20,24},{24,28},{28,0},{1,5},{5... | collective-permute-start | bytes 786440 | tf_op jit(solution)/shard_map/while/body/eval_jaxpr/ppermute | solution.py:24
  1214.2 32.1 %collective-permute-start.2 = (s32[256]{0:T(256)S(1)}, s32[256]{0:T(256)}, u32[]{:S(2)}, u32[]{:S(2)}) collective-permute-start(s32[256]{0:T(256)S(1)} %copy.113), channel_id=1, source_target_pairs={{0,4},{4,8},{8,12},{12,16},{16,20},{20,24},{24,28},{28,0},{1,5},{5... | collective-permute-start | bytes 3080 | tf_op jit(solution)/shard_map/while/body/eval_jaxpr/ppermute | solution.py:24
  1256.8 40.1 %collective-permute-start = (bf16[256,512]{0,1:T(8,128)(2,1)S(1)}, bf16[256,512]{0,1:T(8,128)(2,1)}, u32[]{:S(2)}, u32[]{:S(2)}) collective-permute-start(bf16[256,512]{0,1:T(8,128)(2,1)S(1)} %copy.111), channel_id=1, source_target_pairs={{0,4},{4,8},{8,12},{12,16},{16,20},{20,24},{24,28},{28,0},{1,5},{5... | collective-permute-start | bytes 786440 | tf_op jit(solution)/shard_map/while/body/eval_jaxpr/ppermute | solution.py:24
  1264.5 32.5 %collective-permute-start.1 = (bf16[256,512]{0,1:T(8,128)(2,1)}, bf16[256,512]{0,1:T(8,128)(2,1)}, u32[]{:S(2)}, u32[]{:S(2)}) collective-permute-start(bf16[256,512]{0,1:T(8,128)(2,1)} %copy.112), channel_id=1, source_target_pairs={{0,4},{4,8},{8,12},{12,16},{16,20},{20,24},{24,28},{28,0},{1,5},{5... | collective-permute-start | bytes 786440 | tf_op jit(solution)/shard_map/while/body/eval_jaxpr/ppermute | solution.py:24
  1306.7 40.9 %collective-permute-start = (bf16[256,512]{0,1:T(8,128)(2,1)S(1)}, bf16[256,512]{0,1:T(8,128)(2,1)}, u32[]{:S(2)}, u32[]{:S(2)}) collective-permute-start(bf16[256,512]{0,1:T(8,128)(2,1)S(1)} %copy.111), channel_id=1, source_target_pairs={{0,4},{4,8},{8,12},{12,16},{16,20},{20,24},{24,28},{28,0},{1,5},{5... | collective-permute-start | bytes 786440 | tf_op jit(solution)/shard_map/while/body/eval_jaxpr/ppermute | solution.py:24
  1311.9 35.7 %collective-permute-start.1 = (bf16[256,512]{0,1:T(8,128)(2,1)}, bf16[256,512]{0,1:T(8,128)(2,1)}, u32[]{:S(2)}, u32[]{:S(2)}) collective-permute-start(bf16[256,512]{0,1:T(8,128)(2,1)} %copy.112), channel_id=1, source_target_pairs={{0,4},{4,8},{8,12},{12,16},{16,20},{20,24},{24,28},{28,0},{1,5},{5... | collective-permute-start | bytes 786440 | tf_op jit(solution)/shard_map/while/body/eval_jaxpr/ppermute | solution.py:24
  1357.4 40.9 %collective-permute-start = (bf16[256,512]{0,1:T(8,128)(2,1)S(1)}, bf16[256,512]{0,1:T(8,128)(2,1)}, u32[]{:S(2)}, u32[]{:S(2)}) collective-permute-start(bf16[256,512]{0,1:T(8,128)(2,1)S(1)} %copy.111), channel_id=1, source_target_pairs={{0,4},{4,8},{8,12},{12,16},{16,20},{20,24},{24,28},{28,0},{1,5},{5... | collective-permute-start | bytes 786440 | tf_op jit(solution)/shard_map/while/body/eval_jaxpr/ppermute | solution.py:24
  1368.7 29.6 collective-permute-start.1
  1408.0 29.7 collective-permute-start.5
  1408.0 40.9 %collective-permute-start = (bf16[256,512]{0,1:T(8,128)(2,1)S(1)}, bf16[256,512]{0,1:T(8,128)(2,1)}, u32[]{:S(2)}, u32[]{:S(2)}) collective-permute-start(bf16[256,512]{0,1:T(8,128)(2,1)S(1)} %copy.111), channel_id=1, source_target_pairs={{0,4},{4,8},{8,12},{12,16},{16,20},{20,24},{24,28},{28,0},{1,5},{5... | collective-permute-start | bytes 786440 | tf_op jit(solution)/shard_map/while/body/eval_jaxpr/ppermute | solution.py:24
  1416.2 32.7 %collective-permute-start.1 = (bf16[256,512]{0,1:T(8,128)(2,1)}, bf16[256,512]{0,1:T(8,128)(2,1)}, u32[]{:S(2)}, u32[]{:S(2)}) collective-permute-start(bf16[256,512]{0,1:T(8,128)(2,1)} %copy.112), channel_id=1, source_target_pairs={{0,4},{4,8},{8,12},{12,16},{16,20},{20,24},{24,28},{28,0},{1,5},{5... | collective-permute-start | bytes 786440 | tf_op jit(solution)/shard_map/while/body/eval_jaxpr/ppermute | solution.py:24
  1419.1 29.8 collective-permute-start.2
  1458.6 40.9 %collective-permute-start = (bf16[256,512]{0,1:T(8,128)(2,1)S(1)}, bf16[256,512]{0,1:T(8,128)(2,1)}, u32[]{:S(2)}, u32[]{:S(2)}) collective-permute-start(bf16[256,512]{0,1:T(8,128)(2,1)S(1)} %copy.111), channel_id=1, source_target_pairs={{0,4},{4,8},{8,12},{12,16},{16,20},{20,24},{24,28},{28,0},{1,5},{5... | collective-permute-start | bytes 786440 | tf_op jit(solution)/shard_map/while/body/eval_jaxpr/ppermute | solution.py:24
  1465.7 33.9 %collective-permute-start.1 = (bf16[256,512]{0,1:T(8,128)(2,1)}, bf16[256,512]{0,1:T(8,128)(2,1)}, u32[]{:S(2)}, u32[]{:S(2)}) collective-permute-start(bf16[256,512]{0,1:T(8,128)(2,1)} %copy.112), channel_id=1, source_target_pairs={{0,4},{4,8},{8,12},{12,16},{16,20},{20,24},{24,28},{28,0},{1,5},{5... | collective-permute-start | bytes 786440 | tf_op jit(solution)/shard_map/while/body/eval_jaxpr/ppermute | solution.py:24
  1468.5 31.0 collective-permute-start.2
  1509.3 36.8 %collective-permute-start = (bf16[256,512]{0,1:T(8,128)(2,1)S(1)}, bf16[256,512]{0,1:T(8,128)(2,1)}, u32[]{:S(2)}, u32[]{:S(2)}) collective-permute-start(bf16[256,512]{0,1:T(8,128)(2,1)S(1)} %copy.111), channel_id=1, source_target_pairs={{0,4},{4,8},{8,12},{12,16},{16,20},{20,24},{24,28},{28,0},{1,5},{5... | collective-permute-start | bytes 786440 | tf_op jit(solution)/shard_map/while/body/eval_jaxpr/ppermute | solution.py:24
  1598.6 1544.8 %reduce-scatter.8.cloned.1.call-start = ((), (), s32[]{:S(2)}) async-start(), calls=%async_computation.13 | async-start | bytes 15728640 | tf_op jit(solution)/shard_map/reduce_scatter | solution.py:321
  (70 other events, 2972.5 us)
Sparse Core Ops, SparseCore 0:
  11.5 80.3 all-gather.11
  95.3 54.9 all-gather.13
  153.8 55.2 all-gather.15
  221.2 28.0 all-gather.19
  250.8 30.3 all-gather.17
  284.5 76.6 all-gather.21
  364.6 193.3 all-gather.23
  561.4 192.9 all-gather.25
  757.3 192.9 all-gather.27
  1091.0 1043.2 reduce-scatter.9
  2136.7 882.2 reduce-scatter.5
  3022.2 121.1 reduce-scatter.7
where the time goes:
time: 3160 us
  waiting for transfers between devices  2330 us (74%)
  matrix products  223 us (7%)
  other arithmetic  195 us (6%)
  starting transfers between devices  137 us (4%)
  local copies, waits for them, and re-layouts  134 us (4%)
  blocking collectives  109 us (3%)
    reduce_scatter x1, waiting for transfers between devices, local(): lax.psum_scatter(attn_term, ('ctx', 'fsdp'), scatter_dimension=0, tiled=T...  805 us
    unnamed x13, waiting for transfers between devices  536 us
    all_gather x1, waiting for transfers between devices, fold_mlp(): lax.all_gather(mlp_pack[0], ('ctx', 'fsdp'), axis=0, tiled=True)  189 us
    all_gather x1, waiting for transfers between devices, fold_mlp(): lax.all_gather(mlp_pack[1], ('ctx', 'fsdp'), axis=0, tiled=True)  173 us
    ppermute x48, waiting for transfers between devices, from_behind(): lax.ppermute(value, axis, [(i, (i + by) % length) for i in range(length)])  154 us
    all_gather x1, waiting for transfers between devices, fold_down(): lax.all_gather(down_rows, ('ctx', 'fsdp'), axis=0, tiled=True)  139 us
    ppermute x48, starting transfers between devices, from_behind(): lax.ppermute(value, axis, [(i, (i + by) % length) for i in range(length)])  137 us
    reduce_scatter x1, waiting for transfers between devices, local(): lax.psum_scatter(row_shard, 'fsdp', scatter_dimension=0, tiled=True)  120 us
  transfers between devices with their start and end apart: 60, of which 26 were waited for; matrix products, arithmetic and copies ran while one was open for 12% of the time, Pallas kernels for 0%

commit v1 on v0

v1 whole, which is shorter than its diff:
```python
import functools

import jax
import jax.numpy as jnp
from jax import lax
from jax.experimental import pallas as pl
from jax.experimental.pallas import tpu as pltpu
from jax.sharding import PartitionSpec as P

QUERY_HEADS = 32
KEY_VALUE_HEADS = 8
HD = 64
BLOCK = 256
EPS = 1e-05
ROPE_BASE = 10000000.0
SCALE = 0.015625
RES = 0.22
NEG = -1e30
bf16 = jnp.bfloat16
f32 = jnp.float32


def dg(a, b, ca, cb):
    return lax.dot_general(a, b, (((ca,), (cb,)), ((), ())), preferred_element_type=f32)


def attn_fwd_kernel(nh, tq, tk, q_ref, k_ref, v_ref, st_ref, en_ref, o_ref, ob_ref, l_ref):
    st = st_ref[...]
    en = en_ref[...]
    lo = jnp.min(st) // tk
    hi = (jnp.max(en) + tk - 1) // tk
    qs = [q_ref[h * HD : (h + 1) * HD, :] for h in range(nh)]

    def body(j, c):
        off = pl.multiple_of(j * tk, tk)
        kb = k_ref[pl.ds(off, tk), :]
        vb = v_ref[:, pl.ds(off, tk)]
        jj = off + lax.broadcasted_iota(jnp.int32, (tk, tq), 0)
        vis = (jj >= st) & (jj < en)
        out = []
        for h in range(nh):
            m, l, a = c[h]
            s = dg(kb, qs[h], 1, 0) * SCALE
            s = jnp.where(vis, s, NEG)
            mn = jnp.maximum(m, jnp.max(s, axis=0, keepdims=True))
            p = jnp.where(vis, jnp.exp(s - mn), 0.0)
            sh = jnp.exp(m - mn)
            l = l * sh + jnp.sum(p, axis=0, keepdims=True)
            a = a * sh + dg(vb, p.astype(bf16), 1, 0)
            out.append((mn, l, a))
        return tuple(out)

    init = tuple(
        (jnp.full((1, tq), NEG, f32), jnp.zeros((1, tq), f32), jnp.zeros((HD, tq), f32))
        for _ in range(nh)
    )
    res = lax.fori_loop(lo, hi, body, init)
    for h in range(nh):
        m, l, a = res[h]
        o = a / l
        o_ref[h * HD : (h + 1) * HD, :] = o
        ob_ref[h * HD : (h + 1) * HD, :] = o.astype(bf16)
        l_ref[h : h + 1, :] = m + jnp.log(l)


def attn_fwd(qT, k, vT, st, en, tq=256, tk=256):
    n, S = qT.shape
    nh = n // HD
    blk = lambda r: pl.BlockSpec((r, tq), lambda i: (0, i))
    full = lambda s: pl.BlockSpec(s, lambda i: (0, 0))
    return pl.pallas_call(
        functools.partial(attn_fwd_kernel, nh, tq, tk),
        grid=(S // tq,),
        in_specs=[blk(n), full((S, HD)), full((HD, S)), blk(1), blk(1)],
        out_specs=[blk(n), blk(n), blk(nh)],
        out_shape=[
            jax.ShapeDtypeStruct((n, S), f32),
            jax.ShapeDtypeStruct((n, S), bf16),
            jax.ShapeDtypeStruct((nh, S), f32),
        ],
        cost_estimate=pl.CostEstimate(
            flops=2 * S * S * n, bytes_accessed=8 * n * S, transcendentals=S * S * nh // 2
        ),
        name="attn_fwd",
    )(qT, k, vT, st, en)


def attn_bwd_kernel(
    nh, tq, tk, q_ref, do_ref, o_ref, lse_ref, st_ref, en_ref, k_ref, kT_ref, v_ref, dq_ref, dk_ref, dv_ref
):
    i = pl.program_id(0)

    @pl.when(i == 0)
    def _():
        dk_ref[...] = jnp.zeros_like(dk_ref)
        dv_ref[...] = jnp.zeros_like(dv_ref)

    st = st_ref[...]
    en = en_ref[...]
    lo = jnp.min(st) // tk
    hi = (jnp.max(en) + tk - 1) // tk
    qs = [q_ref[h * HD : (h + 1) * HD, :] for h in range(nh)]
    dos = [do_ref[h * HD : (h + 1) * HD, :] for h in range(nh)]
    dl = [
        jnp.sum(dos[h].astype(f32) * o_ref[h * HD : (h + 1) * HD, :], axis=0, keepdims=True)
        for h in range(nh)
    ]
    ls = [lse_ref[h : h + 1, :] for h in range(nh)]
    dq_ref[...] = jnp.zeros_like(dq_ref)

    def body(j, _):
        off = pl.multiple_of(j * tk, tk)
        kb = k_ref[pl.ds(off, tk), :]
        kT = kT_ref[:, pl.ds(off, tk)]
        vb = v_ref[pl.ds(off, tk), :]
        jj = off + lax.broadcasted_iota(jnp.int32, (tk, tq), 0)
        vis = (jj >= st) & (jj < en)
        dk = jnp.zeros((HD, tk), f32)
        dv = jnp.zeros((HD, tk), f32)
        for h in range(nh):
            s = dg(kb, qs[h], 1, 0) * SCALE
            p = jnp.exp(jnp.where(vis, s - ls[h], NEG))
            dp = dg(vb, dos[h], 1, 0)
            dsc = (p * (dp - dl[h])).astype(bf16)
            dq_ref[h * HD : (h + 1) * HD, :] += dg(kT, dsc, 1, 0)
            dk = dk + dg(qs[h], dsc, 1, 1)
            dv = dv + dg(dos[h], p.astype(bf16), 1, 1)
        dk_ref[:, pl.ds(off, tk)] += dk
        dv_ref[:, pl.ds(off, tk)] += dv
        return 0

    lax.fori_loop(lo, hi, body, 0)


def attn_bwd(qT, doT, oT, lse, st, en, k, kT, v, tq=256, tk=256):
    n, S = qT.shape
    nh = n // HD
    blk = lambda r: pl.BlockSpec((r, tq), lambda i: (0, i))
    full = lambda s: pl.BlockSpec(s, lambda i: (0, 0))
    return pl.pallas_call(
        functools.partial(attn_bwd_kernel, nh, tq, tk),
        grid=(S // tq,),
        in_specs=[
            blk(n), blk(n), blk(n), blk(nh), blk(1), blk(1),
            full((S, HD)), full((HD, S)), full((S, HD)),
        ],
        out_specs=[blk(n), full((HD, S)), full((HD, S))],
        out_shape=[
            jax.ShapeDtypeStruct((n, S), f32),
            jax.ShapeDtypeStruct((HD, S), f32),
            jax.ShapeDtypeStruct((HD, S), f32),
        ],
        cost_estimate=pl.CostEstimate(
            flops=5 * S * S * n, bytes_accessed=10 * n * S, transcendentals=S * S * nh // 2
        ),
        name="attn_bwd",
    )(qT, doT, oT, lse, st, en, k, kT, v)


def rms(v):
    inv = lax.rsqrt(jnp.mean(v * v, axis=-1, keepdims=True) + EPS)
    return v * inv, inv


def rms_back(x, inv, e):
    return inv * (e - x * jnp.mean(e * x, axis=-1, keepdims=True))


def rotate(v, cos, sin, sign):
    heads = v.shape[0] // HD
    v = v.reshape(heads, 2, HD // 2, v.shape[1])
    a, b = v[:, 0], v[:, 1]
    s = sign * sin
    return jnp.stack([a * cos - b * s, b * cos + a * s], axis=1).reshape(heads * HD, -1)


def local(
    tokens, seq_ids, positions, block_ids, gain_attn, w_query, w_key, w_value, w_out,
    gain_mlp, w_gate, w_up, w_down, out_grad,
):
    nc = lax.axis_size("ctx")
    nf = lax.axis_size("fsdp")
    T, E = tokens.shape[1:]
    R = w_query.shape[0]
    S = T * nc
    FFL = w_gate.shape[1] // nc
    nh = QUERY_HEADS // nc
    rep = nc // KEY_VALUE_HEADS
    QW = nh * HD
    KO, VO, OO = QW, QW + HD, QW + 2 * HD
    AW = 2 * QW + 2 * HD

    def cols(w):
        return w.astype(bf16).reshape(R, nc, -1)

    def kv_cols(w):
        return jnp.repeat(w.astype(bf16).reshape(R, KEY_VALUE_HEADS, HD), rep, axis=1)

    def spread(parts):
        w = jnp.transpose(jnp.concatenate(parts, axis=2), (1, 0, 2))
        w = lax.all_to_all(w, "ctx", 0, 0, tiled=True)
        w = lax.all_gather(w, "fsdp", axis=0)
        return jnp.transpose(w, (1, 0, 2, 3)).reshape(E, -1)

    def collect(g):
        g = g.astype(bf16).reshape(nc, nf, R, -1)
        g = jnp.transpose(g, (1, 0, 2, 3)).reshape(E, -1)
        g = lax.psum_scatter(g, "fsdp", scatter_dimension=0, tiled=True)
        return lax.all_to_all(g.reshape(nc, R, -1), "ctx", 0, 0, tiled=True)

    def gather(v):
        return lax.all_gather(v, "ctx", axis=0, tiled=True)

    def scatter(v):
        return lax.psum_scatter(v.astype(bf16), "ctx", scatter_dimension=0, tiled=True).astype(f32)

    both = ("ctx", "fsdp")
    g_attn, g_mlp = lax.all_gather(
        jnp.stack([gain_attn, gain_mlp]).astype(bf16), both, axis=1, tiled=True
    ).astype(f32)
    ids = lax.all_gather(
        jnp.concatenate([seq_ids, positions, block_ids], axis=0), "ctx", axis=1, tiled=True
    )
    row_tok = gather(tokens[0])
    wa = spread([cols(w_query), kv_cols(w_key), kv_cols(w_value), cols(w_out)])

    seq, pos, blk = ids[0], ids[1], ids[2]
    place = jnp.arange(S, dtype=jnp.int32)
    cut = jnp.sum((seq == 0).astype(jnp.int32))
    first = place - pos
    last = jnp.minimum(first + BLOCK * (blk + 1), jnp.where(seq == 0, cut, S))
    st, en = first[None], last[None]
    freq = ROPE_BASE ** (-(jnp.arange(HD // 2, dtype=f32) * 2.0) / HD)
    ang = freq[:, None] * pos.astype(f32)[None, :]
    cos, sin = jnp.cos(ang), jnp.sin(ang)

    x1r, _ = rms(row_tok.astype(f32))
    n1 = (x1r * g_attn[None]).astype(bf16)
    w_qkv, w_o = wa[:, :OO], wa[:, OO:]
    qkv = dg(w_qkv, n1, 0, 1)
    qkT = rotate(qkv[:VO], cos, sin, 1.0).astype(bf16)
    qT, kT = qkT[:QW], qkT[QW:]
    vT = qkv[VO:].astype(bf16)
    k, v = kT.T, vT.T
    oT, oTb, lse = attn_fwd(qT, k, vT, st, en)
    attn = scatter(dg(oTb, w_o, 0, 1))

    wm = spread([cols(w_gate), cols(w_up), cols(w_down)])
    w_gu, w_d = wm[:, : 2 * FFL], wm[:, 2 * FFL :]
    up_grad = out_grad[0].astype(f32)
    dm = gather((RES * up_grad).astype(bf16))

    tok = tokens[0].astype(f32)
    hidden = tok + RES * attn
    x2, r2 = rms(hidden)
    n2 = gather((x2 * g_mlp[None]).astype(bf16))
    gu = dg(n2, w_gu, 1, 0)
    gate, up = gu[:, :FFL], gu[:, FFL:]
    sg = jax.nn.sigmoid(gate)
    act = (gate * sg * up).astype(bf16)
    d_act = dg(dm, w_d, 1, 0)
    d_gate = (d_act * up * sg * (1.0 + gate * (1.0 - sg))).astype(bf16)
    d_up = (d_act * gate * sg).astype(bf16)
    d_gu = jnp.concatenate([d_gate, d_up], axis=1)
    dn2 = scatter(dg(d_gu, w_gu, 1, 1))
    mlp = scatter(dg(act, w_d, 1, 1))
    layer_out = (hidden + RES * mlp).astype(bf16)
    gm = collect(jnp.concatenate([dg(n2, d_gu, 0, 0), dg(dm, act, 0, 0)], axis=1))

    gg_mlp = jnp.sum(x2 * dn2, axis=0)
    dh = up_grad + rms_back(x2, r2, dn2 * g_mlp[None])
    da = gather((RES * dh).astype(bf16))
    doT = dg(w_o, da, 0, 1).astype(bf16)
    dqT, dkT, dvT = attn_bwd(qT, doT, oT, lse, st, en, k, kT, v)
    dqk = rotate(jnp.concatenate([dqT, dkT], axis=0) * SCALE, cos, sin, -1.0).astype(bf16)
    dqkv = jnp.concatenate([dqk, dvT.astype(bf16)], axis=0)
    dn1 = scatter(dg(dqkv, w_qkv, 0, 1))
    x1, r1 = rms(tok)
    gg_attn = jnp.sum(x1 * dn1, axis=0)
    input_grad = dh + rms_back(x1, r1, dn1 * g_attn[None])
    ga = collect(jnp.concatenate([dg(n1, dqkv, 0, 1), dg(da, oTb, 0, 1)], axis=1))
    gains = lax.psum_scatter(
        jnp.stack([gg_attn, gg_mlp], axis=1), both, scatter_dimension=0, tiled=True
    )

    def rows(g):
        return jnp.transpose(g.astype(f32), (1, 0, 2)).reshape(R, -1)

    def kv_rows(g):
        g = g.astype(f32).reshape(KEY_VALUE_HEADS, rep, R, HD)
        return jnp.transpose(jnp.sum(g, axis=1), (1, 0, 2)).reshape(R, -1)

    return (
        layer_out[None],
        input_grad[None],
        gains[:, 0],
        rows(ga[:, :, :KO]),
        kv_rows(ga[:, :, KO:VO]),
        kv_rows(ga[:, :, VO:OO]),
        rows(ga[:, :, OO:]),
        gains[:, 1],
        rows(gm[:, :, :FFL]),
        rows(gm[:, :, FFL : 2 * FFL]),
        rows(gm[:, :, 2 * FFL :]),
    )


def solution(mesh):
    w1, w2 = P(("ctx", "fsdp")), P(("ctx", "fsdp"), None)
    act, ids = P("fsdp", "ctx", None), P("fsdp", "ctx")
    return jax.shard_map(
        local,
        mesh=mesh,
        in_specs=(act, ids, ids, ids, w1, w2, w2, w2, w2, w1, w2, w2, w2, act),
        out_specs=(act, act, w1, w2, w2, w2, w2, w1, w2, w2, w2),
        check_vma=False,
    )
```

time: 3160 us -> 1430 us (0.45)
  waiting for transfers between devices: 2330 us -> 711 us
  blocking collectives: 109 us -> 344 us
  other arithmetic: 195 us -> 51.2 us
  starting transfers between devices: 137 us -> 5.87 us
  local copies, waits for them, and re-layouts: 134 us -> 45.8 us
  Pallas kernels: 0 us -> 85 us
  matrix products: 223 us -> 164 us
    reduce_scatter x2 -> x6, waiting for transfers between devices: 925 us -> 234 us  [the longest x4 206 us: scatter(): lax.psum_scatter(v.astype(bf16), 'ctx', scatter_dimension=0, tiled=True)]
    unnamed x13 -> x14, waiting for transfers between devices: 536 us -> 131 us
    all_gather x9 -> x6, waiting for transfers between devices: 715 us -> 325 us  [the longest x4 195 us: gather(): return lax.all_gather(v, 'ctx', axis=0, tiled=True)]
    all_to_all x0 -> x3, blocking collectives: none -> 264 us  [the longest x2 151 us: spread(): w = lax.all_to_all(w, 'ctx', 0, 0, tiled=True)]
    ppermute x48 -> x0, waiting for transfers between devices: 154 us -> none  [from_behind(): lax.ppermute(value, axis, [(i, (i + by) % length) for i in range(length)])]
    ppermute x48 -> x0, starting transfers between devices: 137 us -> none  [from_behind(): lax.ppermute(value, axis, [(i, (i + by) % length) for i in range(length)])]
    unnamed x2 -> x0, blocking collectives: 89.8 us -> none
    concatenate x6 -> x3, other arithmetic: 96.2 us -> 8.18 us  [the longest x1 7.82 us: local(): jnp.concatenate([dg(n2, d_gu, 0, 0), dg(dm, act, 0, 0)], axis=1)]
  transfers between devices with their start and end apart: 60 -> 14, of which waited for: 26 -> 12; matrix products, arithmetic and copies ran while one was open for 12% -> 13% of each run, Pallas kernels for 0% -> 3%
where the time goes in v1:
time: 1430 us; the launch traced here: 1420 us
  waiting for transfers between devices  711 us (50%)
  blocking collectives  344 us (24%)
  matrix products  164 us (11%)
  Pallas kernels  85 us (6%)
  other arithmetic  51.2 us (4%)
  local copies, waits for them, and re-layouts  45.8 us (3%)
  between operations  14.8 us (1%)
    reduce_scatter x4, waiting for transfers between devices, scatter(): lax.psum_scatter(v.astype(bf16), 'ctx', scatter_dimension=0, tiled=True)  206 us
    all_gather x4, waiting for transfers between devices, gather(): return lax.all_gather(v, 'ctx', axis=0, tiled=True)  195 us
    dot_general x12, matrix products, dg(): lax.dot_general(a, b, (((ca,), (cb,)), ((), ())), preferred_element_type=...  164 us
    all_to_all x2, blocking collectives, spread(): w = lax.all_to_all(w, 'ctx', 0, 0, tiled=True)  151 us
    unnamed x14, waiting for transfers between devices  131 us
    all_gather x2, waiting for transfers between devices, spread(): w = lax.all_gather(w, 'fsdp', axis=0)  130 us
    all_to_all x1, blocking collectives, collect(): return lax.all_to_all(g.reshape(nc, R, -1), 'ctx', 0, 0, tiled=True)  113 us
    all_gather x1, blocking collectives, local(): lax.all_gather(jnp.stack([gain_attn, gain_mlp]).astype(bf16), both, axis=...  66 us
  transfers between devices with their start and end apart: 14, of which 12 were waited for; matrix products, arithmetic and copies ran while one was open for 13% of the time, Pallas kernels for 3%

profile of v1, /device:TPU:0, one launch (start us, length us, event | category | flops | bytes accessed | tf_op | source)
XLA Modules:
  0.0 1422.3 jit_solution(12652503483226215886)
XLA Ops:
  11.9 24.4 %all_to_all.20 = bf16[8,64,640]{2,1,0:T(8,128)(2,1)} all-to-all(bf16[8,64,640]{2,1,0:T(8,128)(2,1)S(1)} %copy.116), channel_id=1, replica_groups=mesh['ctx'=8,'fsdp'=4] {'ctx'}, dimensions={0} | all-to-all | bytes 1310720 | tf_op jit(solution)/shard_map/all_to_all | solution.py:201
  37.2 66.0 %all-gather.3 = bf16[32,64,2]{1,2,0:T(2,128)(2,1)S(1)} all-gather(bf16[1,64,2]{1,2,0:T(2,128)(2,1)S(1)} %maximum_bitcast_fusion.2), channel_id=1, replica_groups=mesh['ctx'=8,'fsdp'=4] {'ctx','fsdp'}, dimensions={0}, use_global_device_ids=true | all-gather | bytes 8448 | tf_op jit(solution)/shard_map/all_gather | solution.py:218
  103.3 14.3 %all_gather.34 = s32[3,2048]{1,0:T(4,128)S(1)} all-gather(s32[3,256]{1,0:T(4,128)S(1)} %pad_add_fusion), channel_id=1, replica_groups=mesh['ctx'=8,'fsdp'=4] {'ctx'}, dimensions={1}, use_global_device_ids=true | all-gather | bytes 27648 | tf_op jit(solution)/shard_map/all_gather | solution.py:221
  124.9 34.1 %all-gather.19.cloned.1.call-done = bf16[1,2048,2048]{2,1,0:T(8,128)(2,1)} async-done(((bf16[1,256,2048]{2,1,0:T(8,128)(2,1)}), bf16[1,2048,2048]{2,1,0:T(8,128)(2,1)}) %all-gather.19.cloned.1.call-update) | async-done | bytes 8388624 | tf_op jit(solution)/shard_map/all_gather | solution.py:212
  164.8 5.5 fusion.16
  174.3 41.3 %attn_fwd.1 = (f32[256,2048]{1,0:T(8,128)}, bf16[256,2048]{1,0:T(8,128)(2,1)}, f32[4,2048]{1,0:T(4,128)}) custom-call(bf16[256,2048]{1,0:T(8,128)(2,1)} %bitcast.171, bf16[2048,64]{1,0:T(8,128)(2,1)} %copy.120.k_ref, bf16[64,2048]{1,0:T(8,128)(2,1)} %copy.121.v_ref, s32[1,2048]{1,0:T(1,128)} %get-tuple-element.47.st_ref, s32[1,2048]{1,0:T(1,128)} %get-tuple-element.46.en_ref), custom_call_target="tpu_custom_call" | custom-call | flops 2147483648 | bytes 4194304 | tf_op jit(solution)/shard_map/attn_fwd/pallas_call | solution.py:71
  215.6 7.2 convolution_convert_fusion.4
  230.0 126.3 %all_to_all.21 = bf16[8,64,3072]{2,1,0:T(8,128)(2,1)} all-to-all(bf16[8,64,3072]{2,1,0:T(8,128)(2,1)S(1)} %copy.122), channel_id=1, replica_groups=mesh['ctx'=8,'fsdp'=4] {'ctx'}, dimensions={0} | all-to-all | bytes 6291456 | tf_op jit(solution)/shard_map/all_to_all | solution.py:201
  356.4 17.3 %reduce-scatter.10.cloned.1.call-done = bf16[256,2048]{1,0:T(8,128)(2,1)} async-done(((bf16[2048,2048]{1,0:T(8,128)(2,1)}), bf16[256,2048]{1,0:T(8,128)(2,1)}) %reduce-scatter.10.cloned.1.call-update) | async-done | bytes 1048592 | tf_op jit(solution)/shard_map/reduce_scatter | solution.py:215
  378.4 129.9 %all-gather.21.cloned.1.call-done = bf16[32,64,3072]{2,1,0:T(8,128)(2,1)} async-done(((bf16[8,64,3072]{2,1,0:T(8,128)(2,1)}), bf16[32,64,3072]{2,1,0:T(8,128)(2,1)}) %all-gather.21.cloned.1.call-update) | async-done | bytes 12582928 | tf_op jit(solution)/shard_map/all_gather | solution.py:202
  508.2 10.9 copy.123
  519.1 73.2 %all-gather.11.cloned.1.call-done = bf16[2048,2048]{1,0:T(8,128)(2,1)} async-done(((bf16[256,2048]{1,0:T(8,128)(2,1)}), bf16[2048,2048]{1,0:T(8,128)(2,1)}) %all-gather.11.cloned.1.call-update) | async-done | bytes 8388624 | tf_op jit(solution)/shard_map/all_gather | solution.py:212
  592.3 24.3 %fusion.4 = f32[2048,2048]{0,1:T(8,128)} fusion(bf16[2048,2048]{1,0:T(8,128)(2,1)} %all-gather.11.cloned.1.call-done, bf16[2048,3072]{1,0:T(8,128)(2,1)} %bitcast.137), kind=kOutput, calls=%fused_computation.17 | convolution fusion | flops 17179869184 | bytes 33554432 | tf_op jit(solution)/shard_map/dot_general | solution.py:24
  616.6 58.3 %all-gather.13.cloned.1.call-done = bf16[2048,2048]{1,0:T(8,128)(2,1)} async-done(((bf16[256,2048]{1,0:T(8,128)(2,1)}), bf16[2048,2048]{1,0:T(8,128)(2,1)}) %all-gather.13.cloned.1.call-update) | async-done | bytes 8388624 | tf_op jit(solution)/shard_map/all_gather | solution.py:212
  675.0 22.7 %multiply_convert_fusion.1 = (bf16[2048,1024]{0,1:T(8,128)(2,1)}, bf16[2048,1024]{0,1:T(8,128)(2,1)}, bf16[2048,1024]{0,1:T(8,128)(2,1)}) fusion(f32[2048,2048]{0,1:T(8,128)} %fusion.4, bf16[2048,2048]{1,0:T(8,128)(2,1)} %all-gather.13.cloned.1.call-done, bf16[2048,3072]{1,0:T(8,128)(2,1)} %bitcast.138), kind=kOutput, calls=%fused_computation.8 | convolution fusion | flops 8623489024 | bytes 41943040 | tf_op jit(solution)/shard_map/dot_general | solution.py:24
  697.7 23.8 %convolution_convert_fusion.2 = bf16[2048,2048]{1,0:T(8,128)(2,1)} fusion(bf16[2048,3072]{1,0:T(8,128)(2,1)} %bitcast.139, bf16[2048,1024]{0,1:T(8,128)(2,1)} %get-tuple-element.29, bf16[2048,1024]{0,1:T(8,128)(2,1)} %get-tuple-element.28), kind=kOutput, calls=%fused_computation.13 | convolution fusion | flops 17200840704 | bytes 25165824 | tf_op jit(solution)/shard_map/dot_general | solution.py:24
  721.6 88.3 %reduce-scatter.14.cloned.1.call-done = bf16[256,2048]{1,0:T(8,128)(2,1)} async-done(((bf16[2048,2048]{1,0:T(8,128)(2,1)}), bf16[256,2048]{1,0:T(8,128)(2,1)}) %reduce-scatter.14.cloned.1.call-update) | async-done | bytes 1048592 | tf_op jit(solution)/shard_map/reduce_scatter | solution.py:215
  815.7 14.1 convolution_convert_fusion.5
  829.8 23.0 %convolution_convert_fusion = bf16[2048,2048]{1,0:T(8,128)(2,1)S(1)} fusion(bf16[2048,2048]{1,0:T(8,128)(2,1)} %all-gather.11.cloned.1.call-done, bf16[2048,1024]{0,1:T(8,128)(2,1)} %get-tuple-element.29, bf16[2048,1024]{0,1:T(8,128)(2,1)} %get-tuple-element.28), kind=kOutput, calls=%fused_computation.11 | convolution fusion | flops 17200840704 | bytes 25165824 | tf_op jit(solution)/shard_map/dot_general | solution.py:24
  852.8 7.8 pad_maximum_fusion
  860.7 5.8 copy.137
  866.9 29.3 %all-gather.15.cloned.1.call-done = bf16[2048,2048]{1,0:T(8,128)(2,1)} async-done(((bf16[256,2048]{1,0:T(8,128)(2,1)}), bf16[2048,2048]{1,0:T(8,128)(2,1)}) %all-gather.15.cloned.1.call-update) | async-done | bytes 8388624 | tf_op jit(solution)/shard_map/all_gather | solution.py:212
  896.2 7.1 convolution_convert_fusion.8.do_ref
  903.3 43.8 %attn_bwd.1 = (f32[256,2048]{1,0:T(8,128)}, f32[64,2048]{1,0:T(8,128)}, f32[64,2048]{1,0:T(8,128)}) custom-call(bf16[256,2048]{1,0:T(8,128)(2,1)} %bitcast.172, bf16[256,2048]{1,0:T(8,128)(2,1)} %convolution_convert_fusion.8.do_ref, f32[256,2048]{1,0:T(8,128)} %get-tuple-element.18.o_ref, f32[4,2048]{1,0:T(4,128)} %get-tuple-element.19.lse_ref, ...), custom_call_target="tpu_custom_call" | custom-call | flops 5368709120 | bytes 5242880 | tf_op jit(solution)/shard_map/attn_bwd/pallas_call | solution.py:140
  951.7 7.2 convolution_convert_fusion.7
  966.5 9.8 convolution_convert_fusion.1
  976.4 14.1 convolution_convert_fusion.3
  990.5 28.1 %reduce-scatter.20.cloned.1.call-done = bf16[512,3072]{1,0:T(8,128)(2,1)} async-done(((bf16[2048,3072]{1,0:T(8,128)(2,1)}), bf16[512,3072]{1,0:T(8,128)(2,1)}) %reduce-scatter.20.cloned.1.call-update) | async-done | bytes 3145744 | tf_op jit(solution)/shard_map/reduce_scatter | solution.py:208
  1018.6 113.2 %all_to_all.22 = bf16[8,64,3072]{2,1,0:T(8,128)(2,1)} all-to-all(bf16[8,64,3072]{2,1,0:T(8,128)(2,1)} %bitcast.159), channel_id=1, replica_groups=mesh['ctx'=8,'fsdp'=4] {'ctx'}, dimensions={0} | all-to-all | bytes 6291456 | tf_op jit(solution)/shard_map/all_to_all | solution.py:209
  1143.7 21.2 %all-to-all-done.2 = bf16[8,64,640]{2,1,0:T(8,128)(2,1)} async-done(((bf16[8,64,640]{2,1,0:T(8,128)(2,1)}), bf16[8,64,640]{2,1,0:T(8,128)(2,1)}, u32[]{:S(2)}, u32[]{:S(2)}) %all-to-all-start.2) | async-done | bytes 655392 | tf_op jit(solution)/shard_map/all_to_all | solution.py:209
  1181.4 96.2 %reduce-scatter.12.cloned.1.call-done = bf16[256,2048]{1,0:T(8,128)(2,1)} async-done(((bf16[2048,2048]{1,0:T(8,128)(2,1)}), bf16[256,2048]{1,0:T(8,128)(2,1)}) %reduce-scatter.12.cloned.1.call-update) | async-done | bytes 1048592 | tf_op jit(solution)/shard_map/reduce_scatter | solution.py:215
  1283.0 130.5 %reduce-scatter.22.cloned.1.call-done = f32[64,2]{1,0:T(8,128)} async-done(((f32[2048,2]{1,0:T(8,128)}), f32[64,2]{1,0:T(8,128)}) %reduce-scatter.22.cloned.1.call-update) | async-done | bytes 528
  (155 shorter events, 88.5 us)
Async XLA Ops:
  7.2 114.1 %all-gather.17.cloned.1.call-start = ((), (), s32[]{:S(2)}) async-start(), calls=%async_computation.20 | async-start | bytes 3276800 | tf_op jit(solution)/shard_map/all_gather | solution.py:202
  11.6 25.5 %copy-start.21 = (f32[64]{0:T(128)S(1)}, f32[64]{0:T(128)}, u32[]{:S(2)}) copy-start(f32[64]{0:T(128)} %param.23) | copy-start | bytes 772
  11.6 25.5 %copy-start.22 = (f32[64]{0:T(128)S(1)}, f32[64]{0:T(128)}, u32[]{:S(2)}) copy-start(f32[64]{0:T(128)} %param.18) | copy-start | bytes 772
  11.6 91.7 %copy-start.18 = (s32[1,256]{1,0:T(1,128)S(1)}, s32[1,256]{1,0:T(1,128)}, u32[]{:S(2)}) copy-start(s32[1,256]{1,0:T(1,128)} %param.17) | copy-start | bytes 3076
  11.6 91.7 %copy-start.19 = (s32[1,256]{1,0:T(1,128)S(1)}, s32[1,256]{1,0:T(1,128)}, u32[]{:S(2)}) copy-start(s32[1,256]{1,0:T(1,128)} %param.16) | copy-start | bytes 3076
  11.6 91.7 %copy-start.20 = (s32[1,256]{1,0:T(1,128)S(1)}, s32[1,256]{1,0:T(1,128)}, u32[]{:S(2)}) copy-start(s32[1,256]{1,0:T(1,128)} %param.15) | copy-start | bytes 3076
  36.3 122.7 %all-gather.19.cloned.1.call-start = ((), (), s32[]{:S(2)}) async-start(), calls=%async_computation.21 | async-start | bytes 9437184 | tf_op jit(solution)/shard_map/all_gather | solution.py:212
  37.1 336.6 %reduce-scatter.10.cloned.1.call-start = ((), (), s32[]{:S(2)}) async-start(), calls=%async_computation.11 | async-start | bytes 9437184 | tf_op jit(solution)/shard_map/reduce_scatter | solution.py:215
  118.3 46.0 %copy-start.14 = (f32[1,2048]{1,0:T(1,128)}, f32[1,2048]{1,0:T(1,128)S(1)}, u32[]{:S(2)}) copy-start(f32[1,2048]{1,0:T(1,128)S(1)} %get-tuple-element.49) | copy-start | bytes 24580
  121.3 49.2 %copy-start.5 = (f32[32,2048]{1,0:T(8,128)}, f32[32,2048]{1,0:T(8,128)S(1)}, u32[]{:S(2)}) copy-start(f32[32,2048]{1,0:T(8,128)S(1)} %get-tuple-element.53) | copy-start | bytes 786436
  159.0 5.8 copy-start.4
  171.0 44.6 %copy-start.13 = (bf16[1,2,32,2048]{3,2,1,0:T(8,128)(2,1)}, bf16[1,2,32,2048]{3,2,1,0:T(8,128)(2,1)S(1)}, u32[]{:S(2)}) copy-start(bf16[1,2,32,2048]{3,2,1,0:T(8,128)(2,1)S(1)} %pad_maximum_fusion.9) | copy-start | bytes 786436
  172.3 43.3 %copy-start.9 = (bf16[64,2048]{0,1:T(8,128)(2,1)}, bf16[64,2048]{0,1:T(8,128)(2,1)S(1)}, u32[]{:S(2)}) copy-start(bf16[64,2048]{0,1:T(8,128)(2,1)S(1)} %copy.142) | copy-start | bytes 786436
  222.8 285.4 %all-gather.21.cloned.1.call-start = ((), (), s32[]{:S(2)}) async-start(), calls=%async_computation.22 | async-start | bytes 15728640 | tf_op jit(solution)/shard_map/all_gather | solution.py:202
  223.2 2.5 copy-start.7
  356.3 17.4 %copy-start = (bf16[1,256,2048]{2,1,0:T(8,128)(2,1)S(1)}, bf16[1,256,2048]{2,1,0:T(8,128)(2,1)}, u32[]{:S(2)}) copy-start(bf16[1,256,2048]{2,1,0:T(8,128)(2,1)} %param.14) | copy-start | bytes 3145732
  356.3 236.0 %all-gather.11.cloned.1.call-start = ((), (), s32[]{:S(2)}) async-start(), calls=%async_computation.12 | async-start | bytes 9437184 | tf_op jit(solution)/shard_map/all_gather | solution.py:212
  377.0 297.9 %all-gather.13.cloned.1.call-start = ((), (), s32[]{:S(2)}) async-start(), calls=%async_computation.14 | async-start | bytes 9437184 | tf_op jit(solution)/shard_map/all_gather | solution.py:212
  378.3 431.6 %reduce-scatter.14.cloned.1.call-start = ((), (), s32[]{:S(2)}) async-start(), calls=%async_computation.15 | async-start | bytes 9437184 | tf_op jit(solution)/shard_map/reduce_scatter | solution.py:215
  721.6 174.6 %all-gather.15.cloned.1.call-start = ((), (), s32[]{:S(2)}) async-start(), calls=%async_computation.16 | async-start | bytes 9437184 | tf_op jit(solution)/shard_map/all_gather | solution.py:212
  809.9 2.4 copy-start.2
  815.7 202.9 %reduce-scatter.20.cloned.1.call-start = ((), (), s32[]{:S(2)}) async-start(), calls=%async_computation.19 | async-start | bytes 15728640 | tf_op jit(solution)/shard_map/reduce_scatter | solution.py:208
  866.4 265.4 %reduce-scatter.18.cloned.1.call-start = ((), (), s32[]{:S(2)}) async-start(), calls=%async_computation.18 | async-start | bytes 3276800 | tf_op jit(solution)/shard_map/reduce_scatter | solution.py:208
  950.3 8.5 slice-start
  951.6 7.2 copy-start.11
  951.6 7.2 slice-start.1
  951.7 7.2 copy-start.15
  951.7 7.2 copy-start.17
  966.3 211.7 %reduce-scatter.16.cloned.1.call-start = ((), (), s32[]{:S(2)}) async-start(), calls=%async_computation.17 | async-start | bytes 9437184 | tf_op jit(solution)/shard_map/reduce_scatter | solution.py:215
  976.4 301.3 %reduce-scatter.12.cloned.1.call-start = ((), (), s32[]{:S(2)}) async-start(), calls=%async_computation.13 | async-start | bytes 9437184 | tf_op jit(solution)/shard_map/reduce_scatter | solution.py:215
  1131.9 33.1 %all-to-all-start.2 = ((bf16[8,64,640]{2,1,0:T(8,128)(2,1)}), bf16[8,64,640]{2,1,0:T(8,128)(2,1)}, u32[]{:S(2)}, u32[]{:S(2)}) async-start(bf16[8,64,640]{2,1,0:T(8,128)(2,1)} %bitcast.177), calls=%async_computation.7 | async-start | bytes 1310720 | tf_op jit(solution)/shard_map/all_to_all | solution.py:209
  1136.1 277.4 %reduce-scatter.22.cloned.1.call-start = ((), (), s32[]{:S(2)}) async-start(), calls=%async_computation.23 | async-start | bytes 1081344
  (7 other events, 11.2 us)
Sparse Core Ops, SparseCore 0:
  36.5 38.6 all-gather.16
  76.7 82.2 all-gather.18
  222.9 150.7 reduce-scatter.9
  375.4 132.7 all-gather.20
  510.2 82.0 all-gather.10
  594.4 80.5 all-gather.12
  721.7 88.1 reduce-scatter.13
  815.8 80.3 all-gather.14
  899.3 119.2 reduce-scatter.19
  1021.5 39.5 reduce-scatter.17
  1063.4 114.5 reduce-scatter.15
  1180.1 97.5 reduce-scatter.11
  1279.9 133.5 reduce-scatter.21

commit v2 on v1

--- a/solution.py
+++ b/solution.py
@@ -157,6 +157,681 @@
     )(qT, doT, oT, lse, st, en, k, kT, v)
 
 
+MESH = pl.DeviceIdType.MESH
+CH = 16
+
+
+class Place:
+    def __init__(self, nc, nf):
+        self.nc, self.nf, self.nz = nc, nf, nc // 2
+        self.c = lax.axis_index("ctx")
+        self.f = lax.axis_index("fsdp")
+        self.z = self.c // 2
+        self.j = self.c % 2
+        self.sib = self.z * 2 + (1 - self.j)
+        self.low = self.z > 0
+        self.high = self.z < self.nz - 1
+
+
+def remote(src, dst, ss, rs, axis, idx):
+    return pltpu.make_async_remote_copy(
+        src_ref=src, dst_ref=dst, send_sem=ss, recv_sem=rs, device_id={axis: idx}, device_id_type=MESH
+    )
+
+
+def greet(p, line=True, ctx=False, fsdp=False):
+    sem = pltpu.get_barrier_semaphore()
+    count = 0
+
+    def tell(axis, idx):
+        pl.semaphore_signal(sem, inc=1, device_id={axis: idx}, device_id_type=MESH)
+
+    if ctx:
+        for k in range(1, p.nc):
+            tell("ctx", lax.rem(p.c + k, p.nc))
+        count = p.nc - 1
+    elif line:
+        tell("ctx", p.sib)
+
+        @pl.when(p.low)
+        def _():
+            tell("ctx", p.c - 2)
+
+        @pl.when(p.high)
+        def _():
+            tell("ctx", p.c + 2)
+
+        count = 1 + p.low.astype(jnp.int32) + p.high.astype(jnp.int32)
+    if fsdp:
+        for k in range(1, p.nf):
+            tell("fsdp", lax.rem(p.f + k, p.nf))
+        count = count + p.nf - 1
+    pl.semaphore_wait(sem, count)
+
+
+def each(fn, start, size, step=CH):
+    def body(r, _):
+        fn(pl.ds(pl.multiple_of(start + r * step, step), step))
+        return 0
+
+    lax.fori_loop(0, size // step, body, 0)
+
+
+class Gather:
+    def __init__(self, p, own, full, rows, ss, rs, ls):
+        self.p, self.own, self.full, self.rows, self.ss, self.rs, self.ls = p, own, full, rows, ss, rs, ls
+
+    def slot(self, k):
+        return self.full.at[k, self.rows]
+
+    def copy(self, way, k, to, src=None):
+        return remote(self.slot(k) if src is None else src, self.slot(k), self.ss.at[way, k], self.rs.at[k], "ctx", to)
+
+    def first(self):
+        p = self.p
+        src = self.own.at[self.rows]
+
+        @pl.when(p.high)
+        def _():
+            self.copy(0, p.c, p.c + 2, src).start()
+
+        @pl.when(p.low)
+        def _():
+            self.copy(1, p.c, p.c - 2, src).start()
+
+        self.copy(2, p.c, p.sib, src).start()
+        pltpu.make_async_copy(src, self.slot(p.c), self.ls).start()
+
+    def step(self, t):
+        p = self.p
+
+        @pl.when(p.z - t >= 0)
+        def _():
+            k = p.c - 2 * t
+            self.copy(2, k, p.sib).wait_recv()
+
+            @pl.when(p.high)
+            def _():
+                self.copy(0, k, p.c + 2).start()
+
+            self.copy(2, k, p.sib).start()
+
+        @pl.when(p.z + t < p.nz)
+        def _():
+            k = p.c + 2 * t
+            self.copy(2, k, p.sib).wait_recv()
+
+            @pl.when(p.low)
+            def _():
+                self.copy(1, k, p.c - 2).start()
+
+            self.copy(2, k, p.sib).start()
+
+    def finish(self):
+        p = self.p
+        src = self.own.at[self.rows]
+        for y in range(p.nz):
+            self.copy(2, 2 * y + 1 - p.j, p.sib).wait_recv()
+        for y in range(p.nz):
+            k = 2 * y + p.j
+            self.copy(2, k, p.sib).wait_send()
+
+            @pl.when(p.high & (y <= p.z))
+            def _(k=k):
+                self.copy(0, k, p.c + 2).wait_send()
+
+            @pl.when(p.low & (y >= p.z))
+            def _(k=k):
+                self.copy(1, k, p.c - 2).wait_send()
+
+        pltpu.make_async_copy(src, self.slot(p.c), self.ls).wait()
+
+    def all_steps(self):
+        return [self.first] + [functools.partial(self.step, t) for t in range(1, self.p.nz)]
+
+
+class Scatter:
+    def __init__(self, p, part, a, x, u, d, acc, start, size, sems):
+        self.p, self.part, self.a, self.x, self.u, self.d, self.acc = p, part, a, x, u, d, acc
+        self.start, self.size, self.rows, self.sems = start, size, pl.ds(start, size), sems
+
+    def cross(self, y):
+        p = self.p
+        return remote(
+            self.part.at[2 * y + 1 - p.j, self.rows], self.x.at[y, self.rows],
+            self.sems.at[0, y], self.sems.at[1, y], "ctx", p.sib,
+        )
+
+    def load(self, y):
+        return pltpu.make_async_copy(
+            self.part.at[2 * y + self.p.j, self.rows], self.a.at[y, self.rows], self.sems.at[2, y]
+        )
+
+    def go_up(self, y):
+        return remote(
+            self.a.at[y, self.rows], self.u.at[y, self.rows], self.sems.at[3, y], self.sems.at[4, y], "ctx", self.p.c + 2
+        )
+
+    def go_down(self, y):
+        return remote(
+            self.a.at[y, self.rows], self.d.at[y, self.rows], self.sems.at[5, y], self.sems.at[6, y], "ctx", self.p.c - 2
+        )
+
+    def begin(self):
+        nz = self.p.nz
+        order = []
+        for i in range(nz):
+            order += [y for y in (nz - 1 - i, i) if y not in order]
+        for y in order:
+            self.cross(y).start()
+            self.load(y).start()
+
+    def add(self, y, extra):
+        def fn(r):
+            v = self.a[y, r].astype(f32) + self.x[y, r].astype(f32)
+            if extra is not None:
+                v = v + extra[y, r].astype(f32)
+            self.a[y, r] = v.astype(bf16)
+
+        each(fn, self.start, self.size)
+
+    def step(self, i):
+        p = self.p
+        up, down = p.nz - 1 - i, i
+
+        @pl.when(p.z < up)
+        def _():
+            self.load(up).wait()
+            self.cross(up).wait_recv()
+
+            @pl.when(p.low)
+            def _():
+                self.go_up(up).wait_recv()
+                self.add(up, self.u)
+
+            @pl.when(p.z == 0)
+            def _():
+                self.add(up, None)
+
+            self.go_up(up).start()
+
+        @pl.when(p.z > down)
+        def _():
+            self.load(down).wait()
+            self.cross(down).wait_recv()
+
+            @pl.when(p.high)
+            def _():
+                self.go_down(down).wait_recv()
+                self.add(down, self.d)
+
+            @pl.when(p.z == p.nz - 1)
+            def _():
+                self.add(down, None)
+
+            self.go_down(down).start()
+
+    def total(self):
+        p = self.p
+        z = p.z
+        self.load(z).wait()
+        self.cross(z).wait_recv()
+
+        def both(r):
+            self.acc[r] = self.a[z, r].astype(f32) + self.x[z, r].astype(f32)
+
+        each(both, self.start, self.size)
+
+        @pl.when(p.low)
+        def _():
+            self.go_up(z).wait_recv()
+
+            def fn(r):
+                self.acc[r] += self.u[z, r].astype(f32)
+
+            each(fn, self.start, self.size)
+
+        @pl.when(p.high)
+        def _():
+            self.go_down(z).wait_recv()
+
+            def fn(r):
+                self.acc[r] += self.d[z, r].astype(f32)
+
+            each(fn, self.start, self.size)
+
+    def finish(self):
+        p = self.p
+        for y in range(p.nz):
+            self.cross(y).wait_send()
+
+            @pl.when(p.z < y)
+            def _(y=y):
+                self.go_up(y).wait_send()
+
+            @pl.when(p.z > y)
+            def _(y=y):
+                self.go_down(y).wait_send()
+
+    def all_steps(self):
+        return [functools.partial(self.step, i) for i in range(self.p.nz - 1)]
+
+
+def interleave(first, second):
+    for i in range(max(len(first), len(second))):
+        if i < len(first):
+            first[i]()
+        if i < len(second):
+            second[i]()
+
+
+class Peers:
+    def __init__(self, p, pick, ss, rs, keep, ls):
+        self.p, self.pick, self.ss, self.rs, self.keep, self.ls = p, pick, ss, rs, keep, ls
+
+    def copy(self, k):
+        p = self.p
+        to = lax.rem(p.f + k, p.nf)
+        src, dst = self.pick(to)
+        return remote(src, dst, self.ss.at[k], self.rs.at[k], "fsdp", to)
+
+    def start(self):
+        for k in range(1, self.p.nf):
+            self.copy(k).start()
+        if self.keep is not None:
+            pltpu.make_async_copy(*self.keep, self.ls).start()
+
+    def wait(self):
+        for k in range(1, self.p.nf):
+            self.copy(k).wait()
+        if self.keep is not None:
+            pltpu.make_async_copy(*self.keep, self.ls).wait()
+
+
+DMA = pltpu.SemaphoreType.DMA
+
+
+def gather_sems(nc):
+    return [DMA((3, nc)), DMA((nc,)), DMA]
+
+
+def scatter_scratch(nz, T, E):
+    return [pltpu.VMEM((nz, T, E), bf16)] * 4 + [pltpu.VMEM((T, E), f32)]
+
+
+def params(cid):
+    return pltpu.CompilerParams(collective_id=cid, has_side_effects=True, vmem_limit_bytes=60 * 1024 * 1024)
+
+
+ANY = pl.BlockSpec(memory_space=pl.ANY)
+VM = pl.BlockSpec(memory_space=pltpu.VMEM)
+
+
+def open_kernel(nc, nf, tok, ids, wl, row, ids_row, w, gss, grs, gls, iss, irs, ils, ass, ars, fss, frs, als):
+    p = Place(nc, nf)
+    greet(p, ctx=True, fsdp=True)
+    T = tok.shape[0]
+    g = Gather(p, tok, row, pl.ds(0, T), gss, grs, gls)
+
+    def id_copy(k):
+        to = lax.rem(p.c + k, nc)
+        return remote(ids, ids_row.at[p.c], iss.at[k], irs.at[k], "ctx", to)
+
+    def block(k):
+        to = lax.rem(p.c + k, nc)
+        return remote(wl.at[to], w.at[p.c, p.f], ass.at[k], ars.at[k], "ctx", to)
+
+    def onward(c, k, m):
+        to = lax.rem(p.f + m, nf)
+        return remote(w.at[c, p.f], w.at[c, p.f], fss.at[k, m], frs.at[k, m], "fsdp", to)
+
+    def source(k):
+        return lax.rem(p.c + nc - k, nc)
+
+    keep_ids = pltpu.make_async_copy(ids, ids_row.at[p.c], ils)
+    keep_w = pltpu.make_async_copy(wl.at[p.c], w.at[p.c, p.f], als)
+    keep_w.start()
+    keep_ids.start()
+    for k in range(1, nc):
+        block(k).start()
+        id_copy(k).start()
+    g.first()
+    keep_w.wait()
+
+    def spread(k):
+        for m in range(1, nf):
+            onward(source(k), k, m).start()
+
+    spread(0)
+    for k in range(1, nc):
+        block(k).wait_recv()
+        spread(k)
+    for t in range(1, p.nz):
+        g.step(t)
+    g.finish()
+    keep_ids.wait()
+    for k in range(1, nc):
+        block(k).wait_send()
+        id_copy(k).wait()
+    for k in range(nc):
+        for m in range(1, nf):
+            onward(source(k), k, m).wait()
+
+
+def open_call(nc, nf, tok, ids, wl):
+    T, E = tok.shape
+    _, R, A = wl.shape
+    return pl.pallas_call(
+        functools.partial(open_kernel, nc, nf),
+        in_specs=[ANY, ANY, ANY],
+        out_specs=[ANY, ANY, ANY],
+        out_shape=[
+            jax.ShapeDtypeStruct((nc, T, E), bf16),
+            jax.ShapeDtypeStruct((nc,) + ids.shape, jnp.int32),
+            jax.ShapeDtypeStruct((nc, nf, R, A), bf16),
+        ],
+        scratch_shapes=gather_sems(nc)
+        + [DMA((nc,)), DMA((nc,)), DMA, DMA((nc,)), DMA((nc,)), DMA((nc, nf)), DMA((nc, nf)), DMA],
+        compiler_params=params(1),
+        name="open_row",
+    )(tok, ids, wl)
+
+
+def middle_kernel(
+    nc, nf, parts, part, tok, og, g, wl, hid, n2, dm, w,
+    a, x, u, d, acc, own, dmo, rsem, nss, nrs, nls, dss, drs, dls, fss, frs, fls,
+):
+    p = Place(nc, nf)
+    greet(p, fsdp=True)
+    T = tok.shape[0]
+    size = T // parts
+    rs = [Scatter(p, part, a, x, u, d, acc, q * size, size, rsem.at[q]) for q in range(parts)]
+    ag = [
+        Gather(p, own, n2, pl.ds(q * size, size), nss.at[q], nrs.at[q], nls.at[q]) for q in range(parts)
+    ]
+    dg_ = Gather(p, dmo, dm, pl.ds(0, T), dss, drs, dls)
+    peers = Peers(p, lambda to: (wl, w.at[:, p.f]), fss, frs, (wl, w.at[:, p.f]), fls)
+
+    rs[0].begin()
+
+    def dm_rows(r):
+        dmo[r] = (RES * og[r].astype(f32)).astype(bf16)
+
+    each(dm_rows, 0, T)
+    peers.start()
+    for q in range(1, parts):
+        rs[q].begin()
+
+    def close(q):
+        rs[q].total()
+
+        def fn(r):
+            h = tok[r].astype(f32) + RES * acc[r]
+            hid[r] = h
+            own[r] = (h * lax.rsqrt(jnp.mean(h * h, axis=-1, keepdims=True) + EPS) * g[...]).astype(bf16)
+
+        each(fn, q * size, size)
+        ag[q].first()
+
+    pending = dg_.all_steps()
+    for q in range(parts):
+        interleave(pending, rs[q].all_steps())
+        close(q)
+        pending = ag[q].all_steps()[1:]
+    for s in pending:
+        s()
+    for q in range(parts):
+        ag[q].finish()
+        rs[q].finish()
+    dg_.finish()
+    peers.wait()
+
+
+def middle_call(nc, nf, parts, part, tok, og, g, wl):
+    T, E = tok.shape
+    _, R, M = wl.shape
+    nz = nc // 2
+    return pl.pallas_call(
+        functools.partial(middle_kernel, nc, nf, parts),
+        in_specs=[ANY, VM, VM, VM, ANY],
+        out_specs=[VM, ANY, ANY, ANY],
+        out_shape=[
+            jax.ShapeDtypeStruct((T, E), f32),
+            jax.ShapeDtypeStruct((nc, T, E), bf16),
+            jax.ShapeDtypeStruct((nc, T, E), bf16),
+            jax.ShapeDtypeStruct((nc, nf, R, M), bf16),
+        ],
+        scratch_shapes=scatter_scratch(nz, T, E)
+        + [pltpu.VMEM((T, E), bf16), pltpu.VMEM((T, E), bf16), DMA((parts, 7, nz))]
+        + [DMA((parts, 3, nc)), DMA((parts, nc)), DMA((parts,))]
+        + gather_sems(nc)
+        + [DMA((nf,)), DMA((nf,)), DMA],
+        compiler_params=params(2),
+        name="attn_to_mlp",
+    )(part, tok, og, g, wl)
+
+
+def turn_kernel(nc, nf, parts, fold, *refs):
+    it = iter(refs)
+    take = lambda n: [next(it) for _ in range(n)]
+    (part,) = take(1)
+    mpart = next(it) if fold else None
+    hid, og, g, gw, dh, da = take(6)
+    lay = next(it) if fold else None
+    gg, y = take(2)
+    a, x, u, d, acc, own, rsem = take(7)
+    nss, nrs, nls, fss, frs, fls = take(6)
+    p = Place(nc, nf)
+    greet(p, fsdp=True)
+    T, E = hid.shape
+    size = T // parts
+    rs = [Scatter(p, part, a, x, u, d, acc, q * size, size, rsem.at[q]) for q in range(parts)]
+    ag = [
+        Gather(p, own, da, pl.ds(q * size, size), nss.at[q], nrs.at[q], nls.at[q]) for q in range(parts)
+    ]
+    peers = Peers(p, lambda to: (gw.at[:, to], y.at[p.f]), fss, frs, (gw.at[:, p.f], y.at[p.f]), fls)
+    for q in range(parts):
+        rs[q].begin()
+    peers.start()
+    gg[...] = jnp.zeros_like(gg)
+    if fold:
+        a2, x2, u2, d2, msem = take(5)
+        ms = Scatter(p, mpart, a2, x2, u2, d2, acc, 0, T, msem)
+
+    def close(q):
+        rs[q].total()
+
+        def fn(r):
+            h = hid[r]
+            inv = lax.rsqrt(jnp.mean(h * h, axis=-1, keepdims=True) + EPS)
+            xn = h * inv
+            dn = acc[r]
+            e = dn * g[...]
+            v = og[r].astype(f32) + inv * (e - xn * jnp.mean(e * xn, axis=-1, keepdims=True))
+            dh[r] = v
+            own[r] = (RES * v).astype(bf16)
+            gg[...] += jnp.sum((xn * dn).reshape(CH // 8, 8, E), axis=0)
+
+        each(fn, q * size, size)
+        ag[q].first()
+
+    pending = []
+    for q in range(parts):
+        interleave(pending, rs[q].all_steps())
+        if fold and q == parts - 1:
+            ms.begin()
+        close(q)
+        pending = ag[q].all_steps()[1:]
+    interleave(pending, ms.all_steps() if fold else [])
+    if fold:
+        ms.total()
+
+        def out(r):
+            lay[r] = (hid[r] + RES * acc[r]).astype(bf16)
+
+        each(out, 0, T)
+        ms.finish()
+    for q in range(parts):
+        ag[q].finish()
+        rs[q].finish()
+    peers.wait()
+
+
+def turn_call(nc, nf, parts, part, mpart, hid, og, g, gw):
+    T, E = hid.shape
+    _, _, R, M = gw.shape
+    nz = nc // 2
+    fold = mpart is not None
+    return pl.pallas_call(
+        functools.partial(turn_kernel, nc, nf, parts, fold),
+        in_specs=[ANY] * (1 + fold) + [VM, VM, VM, ANY],
+        out_specs=[VM, ANY] + [VM] * fold + [VM, ANY],
+        out_shape=[jax.ShapeDtypeStruct((T, E), f32), jax.ShapeDtypeStruct((nc, T, E), bf16)]
+        + [jax.ShapeDtypeStruct((T, E), bf16)] * fold
+        + [jax.ShapeDtypeStruct((8, E), f32), jax.ShapeDtypeStruct((nf, nc, R, M), bf16)],
+        scratch_shapes=scatter_scratch(nz, T, E)
+        + [pltpu.VMEM((T, E), bf16), DMA((parts, 7, nz))]
+        + [DMA((parts, 3, nc)), DMA((parts, nc)), DMA((parts,))]
+        + [DMA((nf,)), DMA((nf,)), DMA]
+        + ([pltpu.VMEM((nz, T, E), bf16)] * 4 + [DMA((7, nz))]) * fold,
+        compiler_params=params(3),
+        name="mlp_to_attn",
+    )(*([part, mpart] if fold else [part]), hid, og, g, gw)
+
+
+def close_kernel(
+    nc, nf, parts, part, tok, dh, g, gw, ggm, dx, gout, ggout,
+    a, x, u, d, acc, y, zb, gg, gbuf, gsum, gfin, rsem, fss, frs, fls, css, crs, cls, s1, r1, s2, r2, l2,
+):
+    p = Place(nc, nf)
+    greet(p, ctx=True, fsdp=True)
+    T, E = tok.shape
+    R = gw.shape[2]
+    size = T // parts
+    rs = [Scatter(p, part, a, x, u, d, acc, q * size, size, rsem.at[q]) for q in range(parts)]
+    peers = Peers(p, lambda to: (gw.at[:, to], y.at[p.f]), fss, frs, (gw.at[:, p.f], y.at[p.f]), fls)
+    for q in range(parts):
+        rs[q].begin()
+    peers.start()
+    gg[...] = jnp.zeros_like(gg)
+
+    def piece(k):
+        to = lax.rem(p.c + k, nc)
+        return remote(zb.at[to], gout.at[p.c], css.at[k], crs.at[k], "ctx", to)
+
+    mine = pltpu.make_async_copy(zb.at[p.c], gout.at[p.c], cls)
+
+    def grads():
+        peers.wait()
+        for c in range(nc):
+
+            def fn(r):
+                v = y[0, c, r].astype(f32)
+                for m in range(1, nf):
+                    v = v + y[m, c, r].astype(f32)
+                zb[c, r] = v.astype(bf16)
+
+            each(fn, 0, R)
+        for k in range(1, nc):
+            piece(k).start()
+        mine.start()
+
+    def close(q):
+        rs[q].total()
+
+        def fn(r):
+            t = tok[r].astype(f32)
+            inv = lax.rsqrt(jnp.mean(t * t, axis=-1, keepdims=True) + EPS)
+            xn = t * inv
+            dn = acc[r]
+            e = dn * g[...]
+            dx[r] = dh[r] + inv * (e - xn * jnp.mean(e * xn, axis=-1, keepdims=True))
+            gg[...] += jnp.sum((xn * dn).reshape(CH // 8, 8, E), axis=0)
+
+        each(fn, q * size, size)
+
+    for q in range(parts):
+        steps = rs[q].all_steps()
+        for s in steps:
+            s()
+        if q == 0:
+            grads()
+        close(q)
+
+    groups = E // 128
+    sa = jnp.sum(gg[...], axis=0, keepdims=True)
+    sm = jnp.sum(ggm[...], axis=0, keepdims=True)
+    for i in range(groups):
+        gbuf[p.f, i] = jnp.concatenate(
+            [sa[:, i * 128 : (i + 1) * 128], sm[:, i * 128 : (i + 1) * 128], jnp.zeros((6, 128), f32)], axis=0
+        )
+
+    def over(k):
+        to = lax.rem(p.f + k, nf)
+        return remote(gbuf.at[p.f], gbuf.at[p.f], s1.at[k], r1.at[k], "fsdp", to)
+
+    for k in range(1, nf):
+        over(k).start()
+    for k in range(1, nf):
+        over(k).wait()
+    v = gbuf[0]
+    for m in range(1, nf):
+        v = v + gbuf[m]
+    gsum[...] = v
+    per = 128 // R
+
+    def along(k):
+        to = lax.rem(p.c + k, nc)
+        return remote(gsum.at[(to * nf + p.f) // per], gfin.at[p.c], s2.at[k], r2.at[k], "ctx", to)
+
+    for k in range(1, nc):
+        along(k).start()
+    own = pltpu.make_async_copy(gsum.at[(p.c * nf + p.f) // per], gfin.at[p.c], l2)
+    own.start()
+    own.wait()
+    for k in range(1, nc):
+        along(k).wait()
+    t = gfin[0]
+    for m in range(1, nc):
+        t = t + gfin[m]
+    ggout[...] = t
+    for k in range(1, nc):
+        piece(k).wait()
+    mine.wait()
+    for q in range(parts):
+        rs[q].finish()
+
+
+def close_call(nc, nf, parts, part, tok, dh, g, gw, ggm):
+    T, E = tok.shape
+    _, _, R, A = gw.shape
+    nz = nc // 2
+    return pl.pallas_call(
+        functools.partial(close_kernel, nc, nf, parts),
+        in_specs=[ANY, VM, VM, VM, ANY, VM],
+        out_specs=[VM, ANY, VM],
+        out_shape=[
+            jax.ShapeDtypeStruct((T, E), f32),
+            jax.ShapeDtypeStruct((nc, R, A), bf16),
+            jax.ShapeDtypeStruct((8, 128), f32),
+        ],
+        scratch_shapes=scatter_scratch(nz, T, E)
+        + [
+            pltpu.VMEM((nf, nc, R, A), bf16),
+            pltpu.VMEM((nc, R, A), bf16),
+            pltpu.VMEM((8, E), f32),
+            pltpu.VMEM((nf, E // 128, 8, 128), f32),
+            pltpu.VMEM((E // 128, 8, 128), f32),
+            pltpu.VMEM((nc, 8, 128), f32),
+            DMA((parts, 7, nz)),
+        ]
+        + [DMA((nf,)), DMA((nf,)), DMA, DMA((nc,)), DMA((nc,)), DMA]
+        + [DMA((nf,)), DMA((nf,)), DMA((nc,)), DMA((nc,)), DMA],
+        compiler_params=params(4),
+        name="close_row",
+    )(part, tok, dh, g, gw, ggm)
+
+
 def rms(v):
     inv = lax.rsqrt(jnp.mean(v * v, axis=-1, keepdims=True) + EPS)
     return v * inv, inv
@@ -180,6 +855,7 @@
 ):
     nc = lax.axis_size("ctx")
     nf = lax.axis_size("fsdp")
+    nz = nc // 2
     T, E = tokens.shape[1:]
     R = w_query.shape[0]
     S = T * nc
@@ -187,8 +863,8 @@
     nh = QUERY_HEADS // nc
     rep = nc // KEY_VALUE_HEADS
     QW = nh * HD
-    KO, VO, OO = QW, QW + HD, QW + 2 * HD
-    AW = 2 * QW + 2 * HD
+    KO, VO, OO, GO = QW, QW + HD, QW + 2 * HD, 2 * QW + 2 * HD
+    tok, og = tokens[0], out_grad[0]
 
     def cols(w):
         return w.astype(bf16).reshape(R, nc, -1)
@@ -196,35 +872,23 @@
     def kv_cols(w):
         return jnp.repeat(w.astype(bf16).reshape(R, KEY_VALUE_HEADS, HD), rep, axis=1)
 
-    def spread(parts):
-        w = jnp.transpose(jnp.concatenate(parts, axis=2), (1, 0, 2))
-        w = lax.all_to_all(w, "ctx", 0, 0, tiled=True)
-        w = lax.all_gather(w, "fsdp", axis=0)
-        return jnp.transpose(w, (1, 0, 2, 3)).reshape(E, -1)
-
-    def collect(g):
-        g = g.astype(bf16).reshape(nc, nf, R, -1)
-        g = jnp.transpose(g, (1, 0, 2, 3)).reshape(E, -1)
-        g = lax.psum_scatter(g, "fsdp", scatter_dimension=0, tiled=True)
-        return lax.all_to_all(g.reshape(nc, R, -1), "ctx", 0, 0, tiled=True)
-
-    def gather(v):
-        return lax.all_gather(v, "ctx", axis=0, tiled=True)
-
-    def scatter(v):
-        return lax.psum_scatter(v.astype(bf16), "ctx", scatter_dimension=0, tiled=True).astype(f32)
-
-    both = ("ctx", "fsdp")
-    g_attn, g_mlp = lax.all_gather(
-        jnp.stack([gain_attn, gain_mlp]).astype(bf16), both, axis=1, tiled=True
-    ).astype(f32)
-    ids = lax.all_gather(
-        jnp.concatenate([seq_ids, positions, block_ids], axis=0), "ctx", axis=1, tiled=True
-    )
-    row_tok = gather(tokens[0])
-    wa = spread([cols(w_query), kv_cols(w_key), kv_cols(w_value), cols(w_out)])
-
-    seq, pos, blk = ids[0], ids[1], ids[2]
+    def blocks(parts):
+        return jnp.transpose(jnp.concatenate(parts, axis=2), (1, 0, 2))
+
+    def exchange(w):
+        return lax.all_to_all(w, "ctx", 0, 0, tiled=True)
+
+    gains = jnp.stack([gain_attn, gain_mlp], axis=1).astype(bf16)
+    gains = jnp.broadcast_to(jnp.pad(gains, ((0, 0), (0, 126)))[:, None], (R, nc, 128))
+    wl = blocks([cols(w_query), kv_cols(w_key), kv_cols(w_value), cols(w_out), gains])
+    ids = jnp.pad(jnp.concatenate([seq_ids, positions, block_ids], axis=0), ((0, 5), (0, 0)))
+    row_tok, ids, wa = open_call(nc, nf, tok, ids, wl)
+    wa = wa.reshape(E, -1)
+    g_attn, g_mlp = wa[:, GO].astype(f32)[None], wa[:, GO + 1].astype(f32)[None]
+
+    wm = exchange(blocks([cols(w_gate), cols(w_up), cols(w_down)]))
+
+    seq, pos, blk = (ids[:, i].reshape(S) for i in range(3))
     place = jnp.arange(S, dtype=jnp.int32)
     cut = jnp.sum((seq == 0).astype(jnp.int32))
     first = place - pos
@@ -234,26 +898,20 @@
     ang = freq[:, None] * pos.astype(f32)[None, :]
     cos, sin = jnp.cos(ang), jnp.sin(ang)
 
-    x1r, _ = rms(row_tok.astype(f32))
-    n1 = (x1r * g_attn[None]).astype(bf16)
-    w_qkv, w_o = wa[:, :OO], wa[:, OO:]
+    x1r, _ = rms(row_tok.reshape(S, E).astype(f32))
+    n1 = (x1r * g_attn).astype(bf16)
+    w_qkv, w_o = wa[:, :OO], wa[:, OO:GO]
     qkv = dg(w_qkv, n1, 0, 1)
     qkT = rotate(qkv[:VO], cos, sin, 1.0).astype(bf16)
     qT, kT = qkT[:QW], qkT[QW:]
     vT = qkv[VO:].astype(bf16)
     k, v = kT.T, vT.T
     oT, oTb, lse = attn_fwd(qT, k, vT, st, en)
-    attn = scatter(dg(oTb, w_o, 0, 1))
-
-    wm = spread([cols(w_gate), cols(w_up), cols(w_down)])
+    attn = dg(oTb, w_o, 0, 1).astype(bf16).reshape(nc, T, E)
+
+    hidden, n2, dm, wm = middle_call(nc, nf, 1, attn, tok, og, g_mlp, wm)
+    n2, dm, wm = n2.reshape(S, E), dm.reshape(S, E), wm.reshape(E, -1)
     w_gu, w_d = wm[:, : 2 * FFL], wm[:, 2 * FFL :]
-    up_grad = out_grad[0].astype(f32)
-    dm = gather((RES * up_grad).astype(bf16))
-
-    tok = tokens[0].astype(f32)
-    hidden = tok + RES * attn
-    x2, r2 = rms(hidden)
-    n2 = gather((x2 * g_mlp[None]).astype(bf16))
     gu = dg(n2, w_gu, 1, 0)
     gate, up = gu[:, :FFL], gu[:, FFL:]
     sg = jax.nn.sigmoid(gate)
@@ -262,26 +920,29 @@
     d_gate = (d_act * up * sg * (1.0 + gate * (1.0 - sg))).astype(bf16)
     d_up = (d_act * gate * sg).astype(bf16)
     d_gu = jnp.concatenate([d_gate, d_up], axis=1)
-    dn2 = scatter(dg(d_gu, w_gu, 1, 1))
-    mlp = scatter(dg(act, w_d, 1, 1))
-    layer_out = (hidden + RES * mlp).astype(bf16)
-    gm = collect(jnp.concatenate([dg(n2, d_gu, 0, 0), dg(dm, act, 0, 0)], axis=1))
-
-    gg_mlp = jnp.sum(x2 * dn2, axis=0)
-    dh = up_grad + rms_back(x2, r2, dn2 * g_mlp[None])
-    da = gather((RES * dh).astype(bf16))
+    dn2 = dg(d_gu, w_gu, 1, 1).astype(bf16).reshape(nc, T, E)
+    mlp = dg(act, w_d, 1, 1).astype(bf16).reshape(nc, T, E)
+    gm = jnp.concatenate([dg(n2, d_gu, 0, 0), dg(dm, act, 0, 0)], axis=1).astype(bf16)
+    gm = gm.reshape(nc, nf, R, -1)
+
+    if nz <= 4:
+        dh, da, layer_out, ggm, gm = turn_call(nc, nf, 1, dn2, mlp, hidden, og, g_mlp, gm)
+    else:
+        dh, da, ggm, gm = turn_call(nc, nf, 1, dn2, None, hidden, og, g_mlp, gm)
+        mlp = lax.psum_scatter(mlp.reshape(S, E), "ctx", scatter_dimension=0, tiled=True)
+        layer_out = (hidden + RES * mlp.astype(f32)).astype(bf16)
+    da = da.reshape(S, E)
+    gm = exchange(jnp.sum(gm.astype(f32), axis=0).astype(bf16))
+
     doT = dg(w_o, da, 0, 1).astype(bf16)
     dqT, dkT, dvT = attn_bwd(qT, doT, oT, lse, st, en, k, kT, v)
     dqk = rotate(jnp.concatenate([dqT, dkT], axis=0) * SCALE, cos, sin, -1.0).astype(bf16)
     dqkv = jnp.concatenate([dqk, dvT.astype(bf16)], axis=0)
-    dn1 = scatter(dg(dqkv, w_qkv, 0, 1))
-    x1, r1 = rms(tok)
-    gg_attn = jnp.sum(x1 * dn1, axis=0)
-    input_grad = dh + rms_back(x1, r1, dn1 * g_attn[None])
-    ga = collect(jnp.concatenate([dg(n1, dqkv, 0, 1), dg(da, oTb, 0, 1)], axis=1))
-    gains = lax.psum_scatter(
-        jnp.stack([gg_attn, gg_mlp], axis=1), both, scatter_dimension=0, tiled=True
-    )
+    dn1 = dg(dqkv, w_qkv, 0, 1).astype(bf16).reshape(nc, T, E)
+    ga = jnp.concatenate([dg(n1, dqkv, 0, 1), dg(da, oTb, 0, 1)], axis=1).astype(bf16)
+    input_grad, ga, gains = close_call(nc, nf, 1, dn1, tok, dh, g_attn, ga.reshape(nc, nf, R, -1), ggm)
+    at = lax.rem((lax.axis_index("ctx") * nf + lax.axis_index("fsdp")) * R, 128)
+    gains = lax.dynamic_slice_in_dim(gains, at, R, 1)
 
     def rows(g):
         return jnp.transpose(g.astype(f32), (1, 0, 2)).reshape(R, -1)
@@ -293,12 +954,12 @@
     return (
         layer_out[None],
         input_grad[None],
-        gains[:, 0],
+        gains[0],
         rows(ga[:, :, :KO]),
         kv_rows(ga[:, :, KO:VO]),
         kv_rows(ga[:, :, VO:OO]),
         rows(ga[:, :, OO:]),
-        gains[:, 1],
+        gains[1],
         rows(gm[:, :, :FFL]),
         rows(gm[:, :, FFL : 2 * FFL]),
         rows(gm[:, :, 2 * FFL :]),

time: 1430 us -> 1190 us (0.83)
  Pallas kernels: 85 us -> 876 us
  waiting for transfers between devices: 711 us -> 0.01 us
  blocking collectives: 344 us -> 0 us
  local copies, waits for them, and re-layouts: 45.8 us -> 86.8 us
    pallas_call x0 -> x4, Pallas kernels: none -> 791 us  [the longest x1 255 us: turn_call(): pl.pallas_call(functools.partial(turn_kernel, nc, nf, parts, fold), in_sp...]
    all_gather x6 -> x0, waiting for transfers between devices: 325 us -> none  [the longest x4 195 us: gather(): return lax.all_gather(v, 'ctx', axis=0, tiled=True)]
    all_to_all x3 -> x0, blocking collectives: 264 us -> none  [the longest x2 151 us: spread(): w = lax.all_to_all(w, 'ctx', 0, 0, tiled=True)]
    reduce_scatter x6 -> x0, waiting for transfers between devices: 234 us -> none  [the longest x4 206 us: scatter(): lax.psum_scatter(v.astype(bf16), 'ctx', scatter_dimension=0, tiled=True)]
    unnamed x14 -> x0, waiting for transfers between devices: 131 us -> none
    all_gather x2 -> x0, blocking collectives: 80.3 us -> none  [the longest x1 66 us: local(): lax.all_gather(jnp.stack([gain_attn, gain_mlp]).astype(bf16), both, axis=...]
    dot_general x0 -> x4, local copies, waits for them, and re-layouts: none -> 49.3 us  [dg(): lax.dot_general(a, b, (((ca,), (cb,)), ((), ())), preferred_element_type=...]
    all_to_all x1 -> x2, waiting for transfers between devices: 21.2 us -> 0.01 us  [exchange(): return lax.all_to_all(w, 'ctx', 0, 0, tiled=True)]
  transfers between devices with their start and end apart: 14 -> 2, of which waited for: 12 -> 0; matrix products, arithmetic and copies ran while one was open for 13% -> 10% of each run, Pallas kernels for 3% -> 31%
where the time goes in v2:
time: 1190 us
  Pallas kernels  876 us (74%)
  matrix products  151 us (13%)
  local copies, waits for them, and re-layouts  86.8 us (7%)
  other arithmetic  61.3 us (5%)
    pallas_call x1, Pallas kernels, turn_call(): pl.pallas_call(functools.partial(turn_kernel, nc, nf, parts, fold), in_sp...  255 us
    pallas_call x1, Pallas kernels, middle_call(): pl.pallas_call(functools.partial(middle_kernel, nc, nf, parts), in_specs=...  248 us
    dot_general x12, matrix products, dg(): lax.dot_general(a, b, (((ca,), (cb,)), ((), ())), preferred_element_type=...  151 us
    pallas_call x1, Pallas kernels, open_call(): pl.pallas_call(functools.partial(open_kernel, nc, nf), in_specs=[ANY, ANY...  150 us
    pallas_call x1, Pallas kernels, close_call(): pl.pallas_call(functools.partial(close_kernel, nc, nf, parts), in_specs=[...  138 us
    dot_general x4, local copies, waits for them, and re-layouts, dg(): lax.dot_general(a, b, (((ca,), (cb,)), ((), ())), preferred_element_type=...  49.3 us
    pallas_call x1, Pallas kernels, attn_bwd(): pl.pallas_call(functools.partial(attn_bwd_kernel, nh, tq, tk), grid=(S //...  43.2 us
    pallas_call x1, Pallas kernels, attn_fwd(): pl.pallas_call(functools.partial(attn_fwd_kernel, nh, tq, tk), grid=(S //...  41.6 us
  transfers between devices with their start and end apart: 2, of which 0 were waited for; matrix products, arithmetic and copies ran while one was open for 10% of the time, Pallas kernels for 31%

profile of v2, /device:TPU:0, one launch (start us, length us, event | category | flops | bytes accessed | tf_op | source)
XLA Modules:
  0.0 1187.3 jit_solution(16448308695455302682)
XLA Ops:
  5.7 6.5 all-to-all-start
  23.8 2.1 concatenate.29
  25.9 150.4 %open_row.1 = (bf16[8,256,2048]{2,1,0:T(8,128)(2,1)}, s32[8,8,256]{2,1,0:T(8,128)}, bf16[8,4,64,768]{3,2,1,0:T(8,128)(2,1)}) custom-call(bf16[256,2048]{1,0:T(8,128)(2,1)} %bitcast.135, s32[8,256]{1,0:T(8,128)} %pad.8.ids, bf16[8,64,768]{2,1,0:T(8,128)(2,1)} %bitcast.161), custom_call_target="tpu_custom_call" | custom-call | tf_op jit(solution)/shard_map/open_row/pallas_call | solution.py:524
  176.3 2.7 fusion.31
  180.5 5.1 multiply_reduce_fusion
  185.6 8.7 fusion.1
  194.3 6.4 fusion.20
  212.8 2.3 fusion.22
  215.7 41.6 %attn_fwd.1 = (f32[256,2048]{1,0:T(8,128)}, bf16[256,2048]{1,0:T(8,128)(2,1)}, f32[4,2048]{1,0:T(4,128)}) custom-call(bf16[256,2048]{1,0:T(8,128)(2,1)} %bitcast.175, bf16[2048,64]{1,0:T(8,128)(2,1)} %copy.91.k_ref, bf16[64,2048]{1,0:T(8,128)(2,1)} %copy.92.v_ref, s32[1,2048]{1,0:T(1,128)} %get-tuple-element.77.st_ref, s32[1,2048]{1,0:T(1,128)} %get-tuple-element.76.en_ref), custom_call_target="tpu_custom_call" | custom-call | flops 2147483648 | bytes 4194304 | tf_op jit(solution)/shard_map/attn_fwd/pallas_call | solution.py:71
  257.9 7.2 convolution_convert_fusion.3
  266.7 247.8 %attn_to_mlp.1 = (f32[256,2048]{1,0:T(8,128)}, bf16[8,256,2048]{2,1,0:T(8,128)(2,1)}, bf16[8,256,2048]{2,1,0:T(8,128)(2,1)}, bf16[8,4,64,3072]{3,2,1,0:T(8,128)(2,1)}) custom-call(bf16[8,256,2048]{2,1,0:T(8,128)(2,1)} %bitcast.131, bf16[256,2048]{1,0:T(8,128)(2,1)} %bitcast.136, bf16[256,2048]{1,0:T(8,128)(2,1)} %bitcast.155, ...), custom_call_target="tpu_custom_call" | custom-call | tf_op jit(solution)/shard_map/attn_to_mlp/pallas_call | solution.py:594
  514.5 12.3 %copy.97 = bf16[2048,2048]{1,0:T(8,128)(2,1)} copy(bf16[2048,2048]{0,1:T(8,128)(2,1)} %bitcast.152) | data formatting | bytes 16777216 | tf_op jit(solution)/shard_map/dot_general | solution.py:24
  526.9 24.3 %fusion.5 = f32[2048,2048]{0,1:T(8,128)} fusion(bf16[2048,2048]{1,0:T(8,128)(2,1)} %bitcast.153, bf16[2048,3072]{1,0:T(8,128)(2,1)} %bitcast.190), kind=kOutput, calls=%fused_computation.17 | convolution fusion | flops 17179869184 | bytes 33554432 | tf_op jit(solution)/shard_map/dot_general | solution.py:24
  551.2 22.7 %multiply_convert_fusion.2 = (bf16[2048,1024]{0,1:T(8,128)(2,1)}, bf16[2048,1024]{0,1:T(8,128)(2,1)}, bf16[2048,1024]{0,1:T(8,128)(2,1)}) fusion(f32[2048,2048]{0,1:T(8,128)} %fusion.5, bf16[2048,2048]{1,0:T(8,128)(2,1)} %bitcast.147, bf16[2048,3072]{1,0:T(8,128)(2,1)} %bitcast.191), kind=kOutput, calls=%fused_computation.10 | convolution fusion | flops 8623489024 | bytes 41943040 | tf_op jit(solution)/shard_map/dot_general | solution.py:24
  573.9 24.0 %convolution_convert_fusion.2 = bf16[2048,2048]{1,0:T(8,128)(2,1)} fusion(bf16[2048,3072]{1,0:T(8,128)(2,1)} %bitcast.192, bf16[2048,1024]{0,1:T(8,128)(2,1)} %get-tuple-element.54, bf16[2048,1024]{0,1:T(8,128)(2,1)} %get-tuple-element.53), kind=kOutput, calls=%fused_computation.14 | convolution fusion | flops 17200840704 | bytes 25165824 | tf_op jit(solution)/shard_map/dot_general | solution.py:24
  597.9 20.7 %fusion.7 = bf16[8,4,64,2048]{3,2,1,0:T(8,128)(2,1)} fusion(bf16[8,4,64,2048]{3,2,1,0:T(8,128)(2,1)S(1)} %bitcast.151, bf16[2048,1024]{0,1:T(8,128)(2,1)} %get-tuple-element.54, bf16[2048,1024]{0,1:T(8,128)(2,1)S(1)} %copy-done.22), kind=kOutput, calls=%fused_computation.19 | convolution fusion | flops 17200840704 | bytes 25165824 | tf_op jit(solution)/shard_map/dot_general | solution.py:24
  618.7 12.3 %copy.99 = bf16[2048,2048]{1,0:T(8,128)(2,1)} copy(bf16[2048,2048]{0,1:T(8,128)(2,1)} %bitcast.148) | data formatting | bytes 16777216 | tf_op jit(solution)/shard_map/dot_general | solution.py:24
  631.0 14.7 %convolution_convert_fusion.1 = bf16[2048,2048]{1,0:T(8,128)(2,1)} fusion(bf16[2048,1024]{0,1:T(8,128)(2,1)} %get-tuple-element.55, bf16[2048,3072]{1,0:T(8,128)(2,1)} %bitcast.193), kind=kOutput, calls=%fused_computation.13 | convolution fusion | flops 8594128896 | bytes 16777216 | tf_op jit(solution)/shard_map/dot_general | solution.py:24
  645.6 9.2 fusion.15
  654.9 9.1 pad_maximum_fusion.refs_5_
  664.0 254.8 %mlp_to_attn.1 = (f32[256,2048]{1,0:T(8,128)}, bf16[8,256,2048]{2,1,0:T(8,128)(2,1)}, bf16[256,2048]{1,0:T(8,128)(2,1)}, f32[8,2048]{1,0:T(8,128)}, bf16[4,8,64,3072]{3,2,1,0:T(8,128)(2,1)}) custom-call(bf16[8,256,2048]{2,1,0:T(8,128)(2,1)} %bitcast.138, bf16[8,256,2048]{2,1,0:T(8,128)(2,1)} %bitcast.139, f32[256,2048]{1,0:T(8,128)} %get-tuple-element.39.refs_2_, ...), custom_call_target="tpu_custom_call" | custom-call | tf_op jit(solution)/shard_map/mlp_to_attn/pallas_call | solution.py:685
  918.8 9.9 reduce_sum.40
  928.7 4.8 all-to-all-start.1
  933.5 12.3 %copy.102 = bf16[2048,2048]{1,0:T(8,128)(2,1)} copy(bf16[2048,2048]{0,1:T(8,128)(2,1)} %bitcast.132) | data formatting | bytes 16777216 | tf_op jit(solution)/shard_map/dot_general | solution.py:24
  945.8 7.1 convolution_convert_fusion.4.do_ref
  952.9 43.2 %attn_bwd.1 = (f32[256,2048]{1,0:T(8,128)}, f32[64,2048]{1,0:T(8,128)}, f32[64,2048]{1,0:T(8,128)}) custom-call(bf16[256,2048]{1,0:T(8,128)(2,1)} %bitcast.176, bf16[256,2048]{1,0:T(8,128)(2,1)} %convolution_convert_fusion.4.do_ref, f32[256,2048]{1,0:T(8,128)} %get-tuple-element.42.o_ref, f32[4,2048]{1,0:T(4,128)} %get-tuple-element.43.lse_ref, ...), custom_call_target="tpu_custom_call" | custom-call | flops 5368709120 | bytes 5242880 | tf_op jit(solution)/shard_map/attn_bwd/pallas_call | solution.py:140
  997.2 12.3 %copy.103 = bf16[2048,2048]{1,0:T(8,128)(2,1)} copy(bf16[2048,2048]{0,1:T(8,128)(2,1)} %bitcast.143) | data formatting | bytes 16777216 | tf_op jit(solution)/shard_map/dot_general | solution.py:24
  1009.5 2.2 maximum_multiply_fusion
  1014.3 2.5 convolution_convert_fusion.6
  1016.8 4.7 convolution_convert_fusion.5
  1024.4 7.1 convolution_convert_fusion
  1031.5 138.2 %close_row.1 = (f32[256,2048]{1,0:T(8,128)}, bf16[8,64,640]{2,1,0:T(8,128)(2,1)}, f32[8,128]{1,0:T(8,128)}) custom-call(bf16[8,256,2048]{2,1,0:T(8,128)(2,1)} %bitcast.150, bf16[256,2048]{1,0:T(8,128)(2,1)} %bitcast.137, f32[256,2048]{1,0:T(8,128)} %get-tuple-element.47.dh, f32[1,2048]{1,0:T(1,128)} %bitcast.184, ...), custom_call_target="tpu_custom_call" | custom-call | tf_op jit(solution)/shard_map/close_row/pallas_call | solution.py:809
  (117 shorter events, 56.9 us)
Async XLA Ops:
  0.6 2.2 copy-start.8
  0.7 2.8 copy-start.9
  5.7 6.5 copy-start.19
  5.7 6.5 copy-start.20
  5.7 9.5 copy-start.15
  5.7 259.4 %all-to-all-start = ((bf16[8,64,3072]{2,1,0:T(8,128)(2,1)}), bf16[8,64,3072]{2,1,0:T(8,128)(2,1)S(1)}, u32[]{:S(2)}, u32[]{:S(2)}) async-start(bf16[8,64,3072]{2,1,0:T(8,128)(2,1)} %maximum_bitcast_fusion), calls=%async_computation | async-start | bytes 6291456 | tf_op jit(solution)/shard_map/all_to_all | solution.py:879
  180.5 5.1 copy-start.16
  200.7 0.8 copy-start.17
  204.6 2.0 copy-start.6
  205.0 0.8 copy-start.4
  205.0 1.6 copy-start.5
  265.1 1.6 copy-start
  573.9 24.0 %copy-start.2 = (bf16[2048,2048]{1,0:T(8,128)(2,1)S(1)}, bf16[2048,2048]{1,0:T(8,128)(2,1)}, u32[]{:S(2)}) copy-start(bf16[2048,2048]{1,0:T(8,128)(2,1)} %copy.97) | copy-start | bytes 25165828
  573.9 24.0 %copy-start.22 = (bf16[2048,1024]{0,1:T(8,128)(2,1)S(1)}, bf16[2048,1024]{0,1:T(8,128)(2,1)}, u32[]{:S(2)}) copy-start(bf16[2048,1024]{0,1:T(8,128)(2,1)} %get-tuple-element.53) | copy-start | bytes 12582916
  631.0 14.7 %copy-start.3 = (bf16[2048,2048]{1,0:T(8,128)(2,1)S(1)}, bf16[2048,2048]{1,0:T(8,128)(2,1)}, u32[]{:S(2)}) copy-start(bf16[2048,2048]{1,0:T(8,128)(2,1)} %copy.99) | copy-start | bytes 25165828
  631.0 14.7 %copy-start.21 = (bf16[2048,1024]{0,1:T(8,128)(2,1)S(1)}, bf16[2048,1024]{0,1:T(8,128)(2,1)}, u32[]{:S(2)}) copy-start(bf16[2048,1024]{0,1:T(8,128)(2,1)} %get-tuple-element.55) | copy-start | bytes 12582916
  631.0 23.9 %slice-start = ((s8[8388608]{0:T(1024)(128)(4,1)}), s8[4194304]{0:T(1024)(128)(4,1)S(1)}, s32[]{:S(2)}) async-start(s8[8388608]{0:T(1024)(128)(4,1)} %bitcast.140), calls=%async_computation.2 | async-start | bytes 8388608
  645.6 9.2 slice-start.1
  928.7 250.7 %all-to-all-start.1 = ((bf16[8,64,3072]{2,1,0:T(8,128)(2,1)}), bf16[8,64,3072]{2,1,0:T(8,128)(2,1)S(1)}, u32[]{:S(2)}, u32[]{:S(2)}) async-start(bf16[8,64,3072]{2,1,0:T(8,128)(2,1)} %reduce_sum.40), calls=%async_computation.1 | async-start | bytes 6291456 | tf_op jit(solution)/shard_map/all_to_all | solution.py:879
  1009.5 2.2 copy-start.7
  1009.5 2.2 copy-start.14
  1009.5 4.4 copy-start.1
  1011.7 2.6 copy-start.11
  1012.1 4.7 slice-start.2
  1014.3 2.5 slice-start.3
  1021.5 2.8 copy-start.12
  1169.7 9.1 copy-start.18
  1181.7 3.1 copy-start.13
  1183.2 2.5 copy-start.10

commit v3 on v2

--- a/solution.py
+++ b/solution.py
@@ -291,8 +291,8 @@
 
 
 class Scatter:
-    def __init__(self, p, part, a, x, u, d, acc, start, size, sems):
-        self.p, self.part, self.a, self.x, self.u, self.d, self.acc = p, part, a, x, u, d, acc
+    def __init__(self, p, part, a, x, ud, start, size, sems):
+        self.p, self.part, self.a, self.x, self.ud = p, part, a, x, ud
         self.start, self.size, self.rows, self.sems = start, size, pl.ds(start, size), sems
 
     def cross(self, y):
@@ -309,22 +309,29 @@
 
     def go_up(self, y):
         return remote(
-            self.a.at[y, self.rows], self.u.at[y, self.rows], self.sems.at[3, y], self.sems.at[4, y], "ctx", self.p.c + 2
+            self.a.at[y, self.rows], self.ud.at[y, self.rows], self.sems.at[3, y], self.sems.at[4, y], "ctx", self.p.c + 2
         )
 
-    def go_down(self, y):
+    def go_down(self, y, last=False):
+        to = self.p.nz if last else y
         return remote(
-            self.a.at[y, self.rows], self.d.at[y, self.rows], self.sems.at[5, y], self.sems.at[6, y], "ctx", self.p.c - 2
+            self.a.at[y, self.rows], self.ud.at[to, self.rows], self.sems.at[5, y], self.sems.at[6, y], "ctx", self.p.c - 2
         )
 
-    def begin(self):
+    def begin(self, cross=True, load=True):
         nz = self.p.nz
         order = []
         for i in range(nz):
             order += [y for y in (nz - 1 - i, i) if y not in order]
         for y in order:
-            self.cross(y).start()
-            self.load(y).start()
+            if cross:
+                self.cross(y).start()
+            if load:
+                self.load(y).start()
+
+    def ready(self, y):
+        self.load(y).wait()
+        self.cross(y).wait_recv()
 
     def add(self, y, extra):
         def fn(r):
@@ -335,70 +342,68 @@
 
         each(fn, self.start, self.size)
 
-    def step(self, i):
+    def edges(self):
         p = self.p
-        up, down = p.nz - 1 - i, i
-
-        @pl.when(p.z < up)
+
+        @pl.when(p.z == 0)
         def _():
-            self.load(up).wait()
-            self.cross(up).wait_recv()
-
-            @pl.when(p.low)
-            def _():
-                self.go_up(up).wait_recv()
-                self.add(up, self.u)
-
-            @pl.when(p.z == 0)
-            def _():
-                self.add(up, None)
-
-            self.go_up(up).start()
-
-        @pl.when(p.z > down)
+            for y in range(p.nz - 1, 0, -1):
+                self.ready(y)
+                self.add(y, None)
+                self.go_up(y).start()
+
+        @pl.when(p.z == p.nz - 1)
         def _():
-            self.load(down).wait()
-            self.cross(down).wait_recv()
-
-            @pl.when(p.high)
-            def _():
-                self.go_down(down).wait_recv()
-                self.add(down, self.d)
-
-            @pl.when(p.z == p.nz - 1)
-            def _():
-                self.add(down, None)
-
-            self.go_down(down).start()
-
-    def total(self):
+            for y in range(p.nz - 1):
+                self.ready(y)
+                self.add(y, None)
+                self.go_down(y, y == p.nz - 2).start()
+
+    def step(self, t):
+        p = self.p
+
+        def upward():
+            y = p.nz - 1 - t + p.z
+            self.ready(y)
+            self.go_up(y).wait_recv()
+            self.add(y, self.ud)
+            self.go_up(y).start()
+
+        def downward():
+            y = t - (p.nz - 1 - p.z)
+            self.ready(y)
+            self.go_down(y).wait_recv()
+            self.add(y, self.ud)
+            self.go_down(y, t == p.nz - 2).start()
+
+        half = p.nz // 2
+        goes_up = p.low & p.high & (p.z <= t)
+        goes_down = p.low & p.high & (p.nz - 1 - p.z <= t)
+        pl.when(goes_up & (p.z < half))(upward)
+        pl.when(goes_down)(downward)
+        pl.when(goes_up & (p.z >= half))(upward)
+
+    def total(self, fn):
         p = self.p
         z = p.z
-        self.load(z).wait()
-        self.cross(z).wait_recv()
-
-        def both(r):
-            self.acc[r] = self.a[z, r].astype(f32) + self.x[z, r].astype(f32)
-
-        each(both, self.start, self.size)
-
-        @pl.when(p.low)
-        def _():
-            self.go_up(z).wait_recv()
-
-            def fn(r):
-                self.acc[r] += self.u[z, r].astype(f32)
-
-            each(fn, self.start, self.size)
-
-        @pl.when(p.high)
-        def _():
-            self.go_down(z).wait_recv()
-
-            def fn(r):
-                self.acc[r] += self.d[z, r].astype(f32)
-
-            each(fn, self.start, self.size)
+        self.ready(z)
+        pl.when(p.low)(lambda: self.go_up(z).wait_recv())
+        pl.when(p.high)(lambda: self.go_down(z, True).wait_recv())
+
+        def run(low, high):
+            def body(r):
+                v = self.a[z, r].astype(f32) + self.x[z, r].astype(f32)
+                if low:
+                    v = v + self.ud[z, r].astype(f32)
+                if high:
+                    v = v + self.ud[p.nz, r].astype(f32)
+                fn(r, v)
+
+            each(body, self.start, self.size)
+
+        pl.when(p.low & p.high)(lambda: run(True, True))
+        pl.when(p.z == 0)(lambda: run(False, p.nz > 1))
+        pl.when(p.z == p.nz - 1)(lambda: run(True, False))
 
     def finish(self):
         p = self.p
@@ -414,7 +419,7 @@
                 self.go_down(y).wait_send()
 
     def all_steps(self):
-        return [functools.partial(self.step, i) for i in range(self.p.nz - 1)]
+        return [functools.partial(self.step, i) for i in range(1, self.p.nz - 1)]
 
 
 def interleave(first, second):
@@ -456,7 +461,7 @@
 
 
 def scatter_scratch(nz, T, E):
-    return [pltpu.VMEM((nz, T, E), bf16)] * 4 + [pltpu.VMEM((T, E), f32)]
+    return [pltpu.VMEM((nz, T, E), bf16)] * 2 + [pltpu.VMEM((nz + 1, T, E), bf16)]
 
 
 def params(cid):
@@ -539,51 +544,48 @@
 
 def middle_kernel(
     nc, nf, parts, part, tok, og, g, wl, hid, n2, dm, w,
-    a, x, u, d, acc, own, dmo, rsem, nss, nrs, nls, dss, drs, dls, fss, frs, fls,
+    a, x, ud, own, dmo, rsem, nss, nrs, nls, dss, drs, dls, fss, frs, fls,
 ):
     p = Place(nc, nf)
     greet(p, fsdp=True)
     T = tok.shape[0]
     size = T // parts
-    rs = [Scatter(p, part, a, x, u, d, acc, q * size, size, rsem.at[q]) for q in range(parts)]
+    rs = [Scatter(p, part, a, x, ud, q * size, size, rsem.at[q]) for q in range(parts)]
     ag = [
         Gather(p, own, n2, pl.ds(q * size, size), nss.at[q], nrs.at[q], nls.at[q]) for q in range(parts)
     ]
-    dg_ = Gather(p, dmo, dm, pl.ds(0, T), dss, drs, dls)
+    dmg = Gather(p, dmo, dm, pl.ds(0, T), dss, drs, dls)
     peers = Peers(p, lambda to: (wl, w.at[:, p.f]), fss, frs, (wl, w.at[:, p.f]), fls)
-
-    rs[0].begin()
+    for q in range(parts):
+        rs[q].begin()
 
     def dm_rows(r):
         dmo[r] = (RES * og[r].astype(f32)).astype(bf16)
 
     each(dm_rows, 0, T)
+    dmg.first()
+    rs[0].edges()
     peers.start()
-    for q in range(1, parts):
-        rs[q].begin()
-
-    def close(q):
-        rs[q].total()
-
-        def fn(r):
-            h = tok[r].astype(f32) + RES * acc[r]
-            hid[r] = h
-            own[r] = (h * lax.rsqrt(jnp.mean(h * h, axis=-1, keepdims=True) + EPS) * g[...]).astype(bf16)
-
-        each(fn, q * size, size)
-        ag[q].first()
-
-    pending = dg_.all_steps()
+
+    def rows(r, v):
+        h = tok[r].astype(f32) + RES * v
+        hid[r] = h
+        own[r] = (h * lax.rsqrt(jnp.mean(h * h, axis=-1, keepdims=True) + EPS) * g[...]).astype(bf16)
+
+    pending = dmg.all_steps()[1:]
     for q in range(parts):
         interleave(pending, rs[q].all_steps())
-        close(q)
+        if q + 1 < parts:
+            rs[q + 1].edges()
+        rs[q].total(rows)
+        ag[q].first()
         pending = ag[q].all_steps()[1:]
     for s in pending:
         s()
     for q in range(parts):
         ag[q].finish()
         rs[q].finish()
-    dg_.finish()
+    dmg.finish()
     peers.wait()
 
 
@@ -611,104 +613,206 @@
     )(part, tok, og, g, wl)
 
 
-def turn_kernel(nc, nf, parts, fold, *refs):
+def turn_kernel(nc, nf, fold, *refs):
     it = iter(refs)
     take = lambda n: [next(it) for _ in range(n)]
-    (part,) = take(1)
+    part, n2, dm, dgu, act = take(5)
+    wd = next(it) if fold else None
+    hid, og, g, dh, da = take(5)
+    lay = next(it) if fold else None
+    gg, y, gbuf = take(3)
     mpart = next(it) if fold else None
-    hid, og, g, gw, dh, da = take(6)
-    lay = next(it) if fold else None
-    gg, y = take(2)
-    a, x, u, d, acc, own, rsem = take(7)
+    a, x, ud, own, rsem = take(5)
     nss, nrs, nls, fss, frs, fls = take(6)
+    dguv, actv, nb, db, nt, go, lsem, ssem = take(8)
     p = Place(nc, nf)
     greet(p, fsdp=True)
     T, E = hid.shape
-    size = T // parts
-    rs = [Scatter(p, part, a, x, u, d, acc, q * size, size, rsem.at[q]) for q in range(parts)]
-    ag = [
-        Gather(p, own, da, pl.ds(q * size, size), nss.at[q], nrs.at[q], nls.at[q]) for q in range(parts)
-    ]
-    peers = Peers(p, lambda to: (gw.at[:, to], y.at[p.f]), fss, frs, (gw.at[:, p.f], y.at[p.f]), fls)
-    for q in range(parts):
-        rs[q].begin()
-    peers.start()
+    S, F2 = dgu.shape
+    F = act.shape[1]
+    R = E // (nc * nf)
+    B = nf * R
+    rs = Scatter(p, part, a, x, ud, 0, T, rsem)
+    ag = Gather(p, own, da, pl.ds(0, T), nss, nrs, nls)
+    rs.begin()
+    big = [pltpu.make_async_copy(dgu, dguv, lsem.at[4]), pltpu.make_async_copy(act, actv, lsem.at[5])]
+    if fold:
+        x2, ud2, wdv, mp, msem, wsem, psem = take(7)
+        ms = Scatter(p, mpart, a, x2, ud2, 0, T, msem)
+        big.append(pltpu.make_async_copy(wd, wdv, wsem))
+    for cp in big:
+        cp.start()
+
+    def column(b, slot):
+        at = pl.ds(pl.multiple_of(b * B, B), B)
+        return (
+            pltpu.make_async_copy(n2.at[:, at], nb.at[slot], lsem.at[slot]),
+            pltpu.make_async_copy(dm.at[:, at], db.at[slot], lsem.at[2 + slot]),
+        )
+
+    def keep(b, slot):
+        return pltpu.make_async_copy(go.at[slot], gbuf.at[b], ssem.at[slot])
+
+    def peer(b, k):
+        to = lax.rem(p.f + k, nf)
+        at = pl.ds(pl.multiple_of(to * R, R), R)
+        return remote(gbuf.at[b, at], y.at[p.f, b], fss.at[k, b], frs.at[k, b], "fsdp", to)
+
+    def mine(b):
+        at = pl.ds(pl.multiple_of(p.f * R, R), R)
+        return pltpu.make_async_copy(gbuf.at[b, at], y.at[p.f, b], fls.at[b])
+
+    def send(b):
+        keep(b, b % 2).wait()
+        for k in range(1, nf):
+            peer(b, k).start()
+        mine(b).start()
+
+    def grads(b, _):
+        slot = b % 2
+
+        @pl.when(b + 1 < nc)
+        def _():
+            for cp in column(b + 1, 1 - slot):
+                cp.start()
+
+        now = column(b, slot)
+        for src, val, base, width, cp in ((nb, dguv, 0, F2, now[0]), (db, actv, F2, F, now[1])):
+            cp.wait()
+            nt[...] = src[slot].T
+            step = min(512, width)
+
+            def dots(i, _, val=val, base=base, step=step):
+                at = pl.multiple_of(i * step, step)
+                v = jnp.dot(nt[...], val[:, pl.ds(at, step)], preferred_element_type=f32)
+                go[slot, :, pl.ds(pl.multiple_of(base + at, step), step)] = v.astype(bf16)
+                return 0
+
+            lax.fori_loop(0, width // step, dots, 0)
+        keep(b, slot).start()
+
+        @pl.when(b > 0)
+        def _():
+            send(b - 1)
+
+        return 0
+
+    def mlp(b, _):
+        slot = b % 2
+        out = pltpu.make_async_copy(mp.at[slot], mpart.at[b], psem.at[slot])
+
+        @pl.when(b > 1)
+        def _():
+            out.wait()
+
+        tok = actv[pl.ds(pl.multiple_of(b * T, T), T), :]
+
+        def dots(i, _):
+            at = pl.ds(pl.multiple_of(i * 512, 512), 512)
+            mp[slot, :, at] = dg(tok, wdv[at, :], 1, 1).astype(bf16)
+            return 0
+
+        lax.fori_loop(0, E // 512, dots, 0)
+        out.start()
+        return 0
+
+    for cp in column(0, 0):
+        cp.start()
     gg[...] = jnp.zeros_like(gg)
+    rs.edges()
+    for cp in big:
+        cp.wait()
     if fold:
-        a2, x2, u2, d2, msem = take(5)
-        ms = Scatter(p, mpart, a2, x2, u2, d2, acc, 0, T, msem)
-
-    def close(q):
-        rs[q].total()
-
-        def fn(r):
-            h = hid[r]
-            inv = lax.rsqrt(jnp.mean(h * h, axis=-1, keepdims=True) + EPS)
-            xn = h * inv
-            dn = acc[r]
-            e = dn * g[...]
-            v = og[r].astype(f32) + inv * (e - xn * jnp.mean(e * xn, axis=-1, keepdims=True))
-            dh[r] = v
-            own[r] = (RES * v).astype(bf16)
-            gg[...] += jnp.sum((xn * dn).reshape(CH // 8, 8, E), axis=0)
-
-        each(fn, q * size, size)
-        ag[q].first()
-
-    pending = []
-    for q in range(parts):
-        interleave(pending, rs[q].all_steps())
-        if fold and q == parts - 1:
-            ms.begin()
-        close(q)
-        pending = ag[q].all_steps()[1:]
-    interleave(pending, ms.all_steps() if fold else [])
+        lax.fori_loop(0, nc, mlp, 0)
+        for slot in range(2):
+            pltpu.make_async_copy(mp.at[slot], mpart.at[slot], psem.at[slot]).wait()
+        ms.begin(load=False)
+    steps = rs.all_steps()
+    bounds = [nc * i // (len(steps) + 1) for i in range(len(steps) + 2)]
+    for i in range(len(steps) + 1):
+        lax.fori_loop(bounds[i], bounds[i + 1], grads, 0)
+        if i < len(steps):
+            steps[i]()
+    send(nc - 1)
+
+    def rows(r, dn):
+        h = hid[r]
+        inv = lax.rsqrt(jnp.mean(h * h, axis=-1, keepdims=True) + EPS)
+        xn = h * inv
+        e = dn * g[...]
+        v = og[r].astype(f32) + inv * (e - xn * jnp.mean(e * xn, axis=-1, keepdims=True))
+        dh[r] = v
+        own[r] = (RES * v).astype(bf16)
+        gg[...] += jnp.sum((xn * dn).reshape(CH // 8, 8, E), axis=0)
+
+    rs.total(rows)
+    ag.first()
+    rs.finish()
     if fold:
-        ms.total()
-
-        def out(r):
-            lay[r] = (hid[r] + RES * acc[r]).astype(bf16)
-
-        each(out, 0, T)
+        ms.begin(cross=False)
+        ms.edges()
+    interleave(ag.all_steps()[1:], ms.all_steps() if fold else [])
+    if fold:
+
+        def out(r, v):
+            lay[r] = (hid[r] + RES * v).astype(bf16)
+
+        ms.total(out)
         ms.finish()
-    for q in range(parts):
-        ag[q].finish()
-        rs[q].finish()
-    peers.wait()
-
-
-def turn_call(nc, nf, parts, part, mpart, hid, og, g, gw):
+    ag.finish()
+    for b in range(nc):
+        for k in range(1, nf):
+            peer(b, k).wait()
+        mine(b).wait()
+
+
+def turn_call(nc, nf, fold, part, n2, dm, dgu, act, wd, hid, og, g):
     T, E = hid.shape
-    _, _, R, M = gw.shape
+    S, F2 = dgu.shape
+    F = act.shape[1]
+    M = F2 + F
+    R = E // (nc * nf)
+    B = nf * R
     nz = nc // 2
-    fold = mpart is not None
+    VMEM = pltpu.VMEM
     return pl.pallas_call(
-        functools.partial(turn_kernel, nc, nf, parts, fold),
-        in_specs=[ANY] * (1 + fold) + [VM, VM, VM, ANY],
-        out_specs=[VM, ANY] + [VM] * fold + [VM, ANY],
+        functools.partial(turn_kernel, nc, nf, fold),
+        in_specs=[ANY] * (5 + fold) + [VM, VM, VM],
+        out_specs=[VM, ANY] + [VM] * fold + [VM, ANY, ANY] + [ANY] * fold,
         out_shape=[jax.ShapeDtypeStruct((T, E), f32), jax.ShapeDtypeStruct((nc, T, E), bf16)]
         + [jax.ShapeDtypeStruct((T, E), bf16)] * fold
-        + [jax.ShapeDtypeStruct((8, E), f32), jax.ShapeDtypeStruct((nf, nc, R, M), bf16)],
+        + [
+            jax.ShapeDtypeStruct((8, E), f32),
+            jax.ShapeDtypeStruct((nf, nc, R, M), bf16),
+            jax.ShapeDtypeStruct((nc, B, M), bf16),
+        ]
+        + [jax.ShapeDtypeStruct((nc, T, E), bf16)] * fold,
         scratch_shapes=scatter_scratch(nz, T, E)
-        + [pltpu.VMEM((T, E), bf16), DMA((parts, 7, nz))]
-        + [DMA((parts, 3, nc)), DMA((parts, nc)), DMA((parts,))]
-        + [DMA((nf,)), DMA((nf,)), DMA]
-        + ([pltpu.VMEM((nz, T, E), bf16)] * 4 + [DMA((7, nz))]) * fold,
+        + [VMEM((T, E), bf16), DMA((7, nz))]
+        + gather_sems(nc)
+        + [DMA((nf, nc)), DMA((nf, nc)), DMA((nc,))]
+        + [VMEM((S, F2), bf16), VMEM((S, F), bf16), VMEM((2, S, B), bf16), VMEM((2, S, B), bf16)]
+        + [VMEM((B, S), bf16), VMEM((2, B, M), bf16), DMA((6,)), DMA((2,))]
+        + [
+            VMEM((nz, T, E), bf16), VMEM((nz + 1, T, E), bf16), VMEM((E, F), bf16), VMEM((2, T, E), bf16),
+            DMA((7, nz)), DMA, DMA((2,)),
+        ]
+        * fold,
         compiler_params=params(3),
         name="mlp_to_attn",
-    )(*([part, mpart] if fold else [part]), hid, og, g, gw)
+    )(part, n2, dm, dgu, act, *([wd] if fold else []), hid, og, g)
 
 
 def close_kernel(
     nc, nf, parts, part, tok, dh, g, gw, ggm, dx, gout, ggout,
-    a, x, u, d, acc, y, zb, gg, gbuf, gsum, gfin, rsem, fss, frs, fls, css, crs, cls, s1, r1, s2, r2, l2,
+    a, x, ud, y, zb, gg, gbuf, gsum, gfin, rsem, fss, frs, fls, css, crs, cls, s1, r1, s2, r2, l2,
 ):
     p = Place(nc, nf)
     greet(p, ctx=True, fsdp=True)
     T, E = tok.shape
     R = gw.shape[2]
     size = T // parts
-    rs = [Scatter(p, part, a, x, u, d, acc, q * size, size, rsem.at[q]) for q in range(parts)]
+    rs = [Scatter(p, part, a, x, ud, q * size, size, rsem.at[q]) for q in range(parts)]
     peers = Peers(p, lambda to: (gw.at[:, to], y.at[p.f]), fss, frs, (gw.at[:, p.f], y.at[p.f]), fls)
     for q in range(parts):
         rs[q].begin()
@@ -736,27 +840,22 @@
             piece(k).start()
         mine.start()
 
-    def close(q):
-        rs[q].total()
-
-        def fn(r):
-            t = tok[r].astype(f32)
-            inv = lax.rsqrt(jnp.mean(t * t, axis=-1, keepdims=True) + EPS)
-            xn = t * inv
-            dn = acc[r]
-            e = dn * g[...]
-            dx[r] = dh[r] + inv * (e - xn * jnp.mean(e * xn, axis=-1, keepdims=True))
-            gg[...] += jnp.sum((xn * dn).reshape(CH // 8, 8, E), axis=0)
-
-        each(fn, q * size, size)
+    def rows(r, dn):
+        t = tok[r].astype(f32)
+        inv = lax.rsqrt(jnp.mean(t * t, axis=-1, keepdims=True) + EPS)
+        xn = t * inv
+        e = dn * g[...]
+        dx[r] = dh[r] + inv * (e - xn * jnp.mean(e * xn, axis=-1, keepdims=True))
+        gg[...] += jnp.sum((xn * dn).reshape(CH // 8, 8, E), axis=0)
 
     for q in range(parts):
-        steps = rs[q].all_steps()
-        for s in steps:
+        rs[q].edges()
+    for q in range(parts):
+        for s in rs[q].all_steps():
             s()
         if q == 0:
             grads()
-        close(q)
+        rs[q].total(rows)
 
     groups = E // 128
     sa = jnp.sum(gg[...], axis=0, keepdims=True)
@@ -849,6 +948,9 @@
     return jnp.stack([a * cos - b * s, b * cos + a * s], axis=1).reshape(heads * HD, -1)
 
 
+PB, PD = 1, 2
+
+
 def local(
     tokens, seq_ids, positions, block_ids, gain_attn, w_query, w_key, w_value, w_out,
     gain_mlp, w_gate, w_up, w_down, out_grad,
@@ -886,7 +988,9 @@
     wa = wa.reshape(E, -1)
     g_attn, g_mlp = wa[:, GO].astype(f32)[None], wa[:, GO + 1].astype(f32)[None]
 
-    wm = exchange(blocks([cols(w_gate), cols(w_up), cols(w_down)]))
+    wm = blocks([cols(w_gate), cols(w_up), cols(w_down)])
+    row_tok, wm = lax.optimization_barrier((row_tok, wm))
+    wm = exchange(wm)
 
     seq, pos, blk = (ids[:, i].reshape(S) for i in range(3))
     place = jnp.arange(S, dtype=jnp.int32)
@@ -909,7 +1013,7 @@
     oT, oTb, lse = attn_fwd(qT, k, vT, st, en)
     attn = dg(oTb, w_o, 0, 1).astype(bf16).reshape(nc, T, E)
 
-    hidden, n2, dm, wm = middle_call(nc, nf, 1, attn, tok, og, g_mlp, wm)
+    hidden, n2, dm, wm = middle_call(nc, nf, PB, attn, tok, og, g_mlp, wm)
     n2, dm, wm = n2.reshape(S, E), dm.reshape(S, E), wm.reshape(E, -1)
     w_gu, w_d = wm[:, : 2 * FFL], wm[:, 2 * FFL :]
     gu = dg(n2, w_gu, 1, 0)
@@ -921,15 +1025,12 @@
     d_up = (d_act * gate * sg).astype(bf16)
     d_gu = jnp.concatenate([d_gate, d_up], axis=1)
     dn2 = dg(d_gu, w_gu, 1, 1).astype(bf16).reshape(nc, T, E)
-    mlp = dg(act, w_d, 1, 1).astype(bf16).reshape(nc, T, E)
-    gm = jnp.concatenate([dg(n2, d_gu, 0, 0), dg(dm, act, 0, 0)], axis=1).astype(bf16)
-    gm = gm.reshape(nc, nf, R, -1)
-
     if nz <= 4:
-        dh, da, layer_out, ggm, gm = turn_call(nc, nf, 1, dn2, mlp, hidden, og, g_mlp, gm)
+        dh, da, layer_out, ggm, gm = turn_call(nc, nf, True, dn2, n2, dm, d_gu, act, w_d, hidden, og, g_mlp)[:5]
     else:
-        dh, da, ggm, gm = turn_call(nc, nf, 1, dn2, None, hidden, og, g_mlp, gm)
-        mlp = lax.psum_scatter(mlp.reshape(S, E), "ctx", scatter_dimension=0, tiled=True)
+        dh, da, ggm, gm = turn_call(nc, nf, False, dn2, n2, dm, d_gu, act, None, hidden, og, g_mlp)[:4]
+        mlp = dg(act, w_d, 1, 1).astype(bf16)
+        mlp = lax.psum_scatter(mlp, "ctx", scatter_dimension=0, tiled=True)
         layer_out = (hidden + RES * mlp.astype(f32)).astype(bf16)
     da = da.reshape(S, E)
     gm = exchange(jnp.sum(gm.astype(f32), axis=0).astype(bf16))
@@ -939,8 +1040,8 @@
     dqk = rotate(jnp.concatenate([dqT, dkT], axis=0) * SCALE, cos, sin, -1.0).astype(bf16)
     dqkv = jnp.concatenate([dqk, dvT.astype(bf16)], axis=0)
     dn1 = dg(dqkv, w_qkv, 0, 1).astype(bf16).reshape(nc, T, E)
-    ga = jnp.concatenate([dg(n1, dqkv, 0, 1), dg(da, oTb, 0, 1)], axis=1).astype(bf16)
-    input_grad, ga, gains = close_call(nc, nf, 1, dn1, tok, dh, g_attn, ga.reshape(nc, nf, R, -1), ggm)
+    ga = jnp.concatenate([dg(dqkv, n1, 1, 0), dg(oTb, da, 1, 0)], axis=0).astype(bf16).T
+    input_grad, ga, gains = close_call(nc, nf, PD, dn1, tok, dh, g_attn, ga.reshape(nc, nf, R, -1), ggm)
     at = lax.rem((lax.axis_index("ctx") * nf + lax.axis_index("fsdp")) * R, 128)
     gains = lax.dynamic_slice_in_dim(gains, at, R, 1)
 

time: 1190 us -> 875 us (0.74)
  Pallas kernels: 876 us -> 639 us
  local copies, waits for them, and re-layouts: 86.8 us -> 43 us
  matrix products: 151 us -> 112 us
    pallas_call x1, Pallas kernels: 248 us -> 173 us  [middle_call(): pl.pallas_call(functools.partial(middle_kernel, nc, nf, parts), in_specs=...]
    pallas_call x1, Pallas kernels: 255 us -> 185 us  [turn_call(): pl.pallas_call(functools.partial(turn_kernel, nc, nf, fold), in_specs=[AN...]
    pallas_call x1, Pallas kernels: 150 us -> 99.1 us  [open_call(): pl.pallas_call(functools.partial(open_kernel, nc, nf), in_specs=[ANY, ANY...]
    dot_general x4 -> x0, local copies, waits for them, and re-layouts: 49.3 us -> none  [dg(): lax.dot_general(a, b, (((ca,), (cb,)), ((), ())), preferred_element_type=...]
    pallas_call x1, Pallas kernels: 138 us -> 97.4 us  [close_call(): pl.pallas_call(functools.partial(close_kernel, nc, nf, parts), in_specs=[...]
    dot_general x12 -> x9, matrix products: 151 us -> 112 us  [dg(): lax.dot_general(a, b, (((ca,), (cb,)), ((), ())), preferred_element_type=...]
  transfers between devices with their start and end apart: 2 -> 2, of which waited for: 0 -> 0; matrix products, arithmetic and copies ran while one was open for 10% -> 11% of each run, Pallas kernels for 31% -> 21%
where the time goes in v3:
time: 875 us; the launch traced here: 862 us
  Pallas kernels  639 us (73%)
  matrix products  112 us (13%)
  other arithmetic  59.3 us (7%)
  local copies, waits for them, and re-layouts  43 us (5%)
    pallas_call x1, Pallas kernels, turn_call(): pl.pallas_call(functools.partial(turn_kernel, nc, nf, fold), in_specs=[AN...  185 us
    pallas_call x1, Pallas kernels, middle_call(): pl.pallas_call(functools.partial(middle_kernel, nc, nf, parts), in_specs=...  173 us
    dot_general x9, matrix products, dg(): lax.dot_general(a, b, (((ca,), (cb,)), ((), ())), preferred_element_type=...  112 us
    pallas_call x1, Pallas kernels, open_call(): pl.pallas_call(functools.partial(open_kernel, nc, nf), in_specs=[ANY, ANY...  99.1 us
    pallas_call x1, Pallas kernels, close_call(): pl.pallas_call(functools.partial(close_kernel, nc, nf, parts), in_specs=[...  97.4 us
    pallas_call x1, Pallas kernels, attn_bwd(): pl.pallas_call(functools.partial(attn_bwd_kernel, nh, tq, tk), grid=(S //...  43.2 us
    pallas_call x1, Pallas kernels, attn_fwd(): pl.pallas_call(functools.partial(attn_fwd_kernel, nh, tq, tk), grid=(S //...  41.3 us
  transfers between devices with their start and end apart: 2, of which 0 were waited for; matrix products, arithmetic and copies ran while one was open for 11% of the time, Pallas kernels for 21%

profile of v3, /device:TPU:0, one launch (start us, length us, event | category | flops | bytes accessed | tf_op | source)
XLA Modules:
  0.0 861.9 jit_solution(4878045773961531681)
XLA Ops:
  10.6 1.9 concatenate.23
  12.5 99.1 %open_row.1 = (bf16[8,256,2048]{2,1,0:T(8,128)(2,1)}, s32[8,8,256]{2,1,0:T(8,128)}, bf16[8,4,64,768]{3,2,1,0:T(8,128)(2,1)}) custom-call(bf16[256,2048]{1,0:T(8,128)(2,1)} %bitcast.104, s32[8,256]{1,0:T(8,128)} %pad.8.ids, bf16[8,64,768]{2,1,0:T(8,128)(2,1)} %bitcast.121), custom_call_target="tpu_custom_call" | custom-call | tf_op jit(solution)/shard_map/open_row/pallas_call | solution.py:529
  111.6 1.8 maximum_bitcast_fusion
  113.4 3.8 all-to-all-start
  117.2 2.7 fusion.16
  121.4 5.1 multiply_reduce_fusion
  126.5 8.6 %fusion.1 = bf16[2048,2048]{1,0:T(8,128)(2,1)} fusion(f32[2048]{0:T(1024)S(1)} %bitcast.147, f32[2048]{0:T(1024)S(1)} %bitcast.149, bf16[8,256,2048]{2,1,0:T(8,128)(2,1)} %get-tuple-element.36), kind=kLoop, calls=%fused_computation.2 | loop fusion | flops 16777216 | bytes 16793600 | tf_op jit(solution)/shard_map/convert_element_type | solution.py:1006
  135.2 6.4 fusion.6
  144.6 1.8 broadcast_multiply_fusion
  146.4 2.2 add_convert_fusion.1
  150.2 2.0 copy.91.k_ref
  153.2 1.9 copy.92.v_ref
  156.3 2.3 fusion.8
  159.2 41.3 %attn_fwd.1 = (f32[256,2048]{1,0:T(8,128)}, bf16[256,2048]{1,0:T(8,128)(2,1)}, f32[4,2048]{1,0:T(4,128)}) custom-call(bf16[256,2048]{1,0:T(8,128)(2,1)} %bitcast.139, bf16[2048,64]{1,0:T(8,128)(2,1)} %copy.91.k_ref, bf16[64,2048]{1,0:T(8,128)(2,1)} %copy.92.v_ref, s32[1,2048]{1,0:T(1,128)} %get-tuple-element.81.st_ref, s32[1,2048]{1,0:T(1,128)} %get-tuple-element.80.en_ref), custom_call_target="tpu_custom_call" | custom-call | flops 2147483648 | bytes 4194304 | tf_op jit(solution)/shard_map/attn_fwd/pallas_call | solution.py:71
  201.1 7.3 convolution_convert_fusion.2
  210.1 173.1 %attn_to_mlp.1 = (f32[256,2048]{1,0:T(8,128)}, bf16[8,256,2048]{2,1,0:T(8,128)(2,1)}, bf16[8,256,2048]{2,1,0:T(8,128)(2,1)}, bf16[8,4,64,3072]{3,2,1,0:T(8,128)(2,1)}) custom-call(bf16[8,256,2048]{2,1,0:T(8,128)(2,1)} %bitcast.100, bf16[256,2048]{1,0:T(8,128)(2,1)} %bitcast.105, bf16[256,2048]{1,0:T(8,128)(2,1)} %bitcast.115, ...), custom_call_target="tpu_custom_call" | custom-call | tf_op jit(solution)/shard_map/attn_to_mlp/pallas_call | solution.py:596
  383.1 24.2 %fusion.3 = f32[2048,2048]{1,0:T(8,128)} fusion(bf16[2048,2048]{1,0:T(8,128)(2,1)} %bitcast.110, bf16[2048,3072]{1,0:T(8,128)(2,1)} %bitcast.127), kind=kOutput, calls=%fused_computation.13 | convolution fusion | flops 17179869184 | bytes 33554432 | tf_op jit(solution)/shard_map/dot_general | solution.py:24
  407.3 23.4 %multiply_convert_fusion.2 = (bf16[2048,1024]{1,0:T(8,128)(2,1)}, bf16[2048,1024]{1,0:T(8,128)(2,1)}, bf16[2048,1024]{1,0:T(8,128)(2,1)}) fusion(f32[2048,2048]{1,0:T(8,128)} %fusion.3, bf16[2048,2048]{1,0:T(8,128)(2,1)} %bitcast.112, bf16[2048,3072]{1,0:T(8,128)(2,1)} %bitcast.128), kind=kOutput, calls=%fused_computation.7 | convolution fusion | flops 8623489024 | bytes 41943040 | tf_op jit(solution)/shard_map/dot_general | solution.py:24
  430.7 8.3 pad_maximum_fusion.refs_3_
  438.9 23.9 %convolution_convert_fusion.1 = bf16[2048,2048]{1,0:T(8,128)(2,1)} fusion(bf16[2048,3072]{1,0:T(8,128)(2,1)} %bitcast.129, bf16[2048,1024]{1,0:T(8,128)(2,1)} %get-tuple-element.58, bf16[2048,1024]{1,0:T(8,128)(2,1)} %get-tuple-element.57), kind=kOutput, calls=%fused_computation.10 | convolution fusion | flops 17200840704 | bytes 25165824 | tf_op jit(solution)/shard_map/dot_general | solution.py:24
  462.9 4.8 slice.131.refs_5_
  467.6 184.7 %mlp_to_attn.1 = (f32[256,2048]{1,0:T(8,128)}, bf16[8,256,2048]{2,1,0:T(8,128)(2,1)}, bf16[256,2048]{1,0:T(8,128)(2,1)}, f32[8,2048]{1,0:T(8,128)}, bf16[4,8,64,...) custom-call(bf16[8,256,2048]{2,1,0:T(8,128)(2,1)} %bitcast.114, ...), custom_call_target="tpu_custom_call" | custom-call | tf_op jit(solution)/shard_map/mlp_to_attn/pallas_call | solution.py:778
  652.3 9.9 %reduce_sum.40 = bf16[8,64,3072]{2,1,0:T(8,128)(2,1)} reduce(bf16[4,8,64,3072]{3,2,1,0:T(8,128)(2,1)} %get-tuple-element.56, bf16[]{:T(256)} %constant.10.clone.1), dimensions={0}, to_apply=%region_2.3 | reduce | flops 4718592 | bytes 15728642 | tf_op jit(solution)/shard_map/reduce_sum | solution.py:1036
  662.2 3.6 all-to-all-start.1
  665.9 7.1 convolution_convert_fusion.5.do_ref
  673.0 43.2 %attn_bwd.1 = (f32[256,2048]{1,0:T(8,128)}, f32[64,2048]{1,0:T(8,128)}, f32[64,2048]{1,0:T(8,128)}) custom-call(bf16[256,2048]{1,0:T(8,128)(2,1)} %bitcast.140, bf16[256,2048]{1,0:T(8,128)(2,1)} %convolution_convert_fusion.5.do_ref, f32[256,2048]{1,0:T(8,128)} %get-tuple-element.46.o_ref, f32[4,2048]{1,0:T(4,128)} %get-tuple-element.47.lse_ref, ...), custom_call_target="tpu_custom_call" | custom-call | flops 5368709120 | bytes 5242880 | tf_op jit(solution)/shard_map/attn_bwd/pallas_call | solution.py:140
  717.3 2.1 maximum_multiply_fusion
  720.6 6.5 convolution_convert_fusion.4
  727.2 3.5 convolution_convert_fusion.3
  732.4 4.6 copy.99
  737.0 9.8 %convolution_convert_fusion = bf16[2048,2048]{1,0:T(8,128)(2,1)} fusion(bf16[2048,768]{1,0:T(8,128)(2,1)} %bitcast.135, bf16[64,2048]{1,0:T(8,128)(2,1)S(1)} %convert_element_type.148, bf16[320,2048]{1,0:T(8,128)(2,1)} %bitcast.137), kind=kOutput, calls=%fused_computation.9 | convolution fusion | flops 3228565504 | bytes 11534336 | tf_op jit(solution)/shard_map/dot_general | solution.py:24
  746.8 97.4 %close_row.1 = (f32[256,2048]{1,0:T(8,128)}, bf16[8,64,640]{2,1,0:T(8,128)(2,1)}, f32[8,128]{1,0:T(8,128)}) custom-call(bf16[8,256,2048]{2,1,0:T(8,128)(2,1)} %bitcast.109, bf16[256,2048]{1,0:T(8,128)(2,1)} %bitcast.106, f32[256,2048]{1,0:T(8,128)} %get-tuple-element.51.dh, f32[1,2048]{1,0:T(1,128)} %bitcast.148, bf16[8,4,64,640]{3,2,1,0:T(8,128)(2,1)} %bitcast.103, ...), custom_call_target="tpu_custom_call" | custom-call | tf_op jit(solution)/shard_map/close_row/pallas_call | solution.py:908
  (99 shorter events, 42.6 us)
Async XLA Ops:
  0.6 6.0 copy-start.5
  5.9 1.6 copy-start.6
  5.9 2.3 copy-start.7
  7.5 1.6 copy-start.16
  7.5 1.6 copy-start.17
  7.5 1.6 copy-start.18
  113.4 95.0 %all-to-all-start = ((bf16[8,64,3072]{2,1,0:T(8,128)(2,1)}), bf16[8,64,3072]{2,1,0:T(8,128)(2,1)S(1)}, u32[]{:S(2)}, u32[]{:S(2)}) async-start(bf16[8,64,3072]{2,1,0:T(8,128)(2,1)} %maximum_bitcast_fusion), calls=%async_computation | async-start | bytes 6291456 | tf_op jit(solution)/shard_map/all_to_all | solution.py:981
  121.4 5.1 copy-start.13
  141.6 1.7 copy-start.14
  146.4 3.8 copy-start.3
  148.6 0.8 copy-start.1
  148.6 1.6 copy-start.2
  208.4 1.6 copy-start
  662.2 191.7 %all-to-all-start.1 = ((bf16[8,64,3072]{2,1,0:T(8,128)(2,1)}), bf16[8,64,3072]{2,1,0:T(8,128)(2,1)S(1)}, u32[]{:S(2)}, u32[]{:S(2)}) async-start(bf16[8,64,3072]{2,1,0:T(8,128)(2,1)} %reduce_sum.40), calls=%async_computation.1 | async-start | bytes 6291456 | tf_op jit(solution)/shard_map/all_to_all | solution.py:981
  716.2 3.2 copy-start.4
  716.2 3.2 copy-start.12
  719.4 1.2 copy-start.9
  719.4 7.8 slice-start
  720.6 6.6 copy-start.10
  720.6 6.6 slice-start.1
  844.2 9.1 %copy-start.15 = (f32[8,128]{1,0:T(8,128)S(1)}, f32[8,128]{1,0:T(8,128)}, u32[]{:S(2)}) copy-start(f32[8,128]{1,0:T(8,128)} %get-tuple-element.54) | copy-start | bytes 12292
  856.2 3.1 copy-start.11
  857.8 2.5 copy-start.8

commit v4 on v3

--- a/solution.py
+++ b/solution.py
@@ -24,43 +24,52 @@
     return lax.dot_general(a, b, (((ca,), (cb,)), ((), ())), preferred_element_type=f32)
 
 
-def attn_fwd_kernel(nh, tq, tk, q_ref, k_ref, v_ref, st_ref, en_ref, o_ref, ob_ref, l_ref):
-    st = st_ref[...]
-    en = en_ref[...]
-    lo = jnp.min(st) // tk
-    hi = (jnp.max(en) + tk - 1) // tk
-    qs = [q_ref[h * HD : (h + 1) * HD, :] for h in range(nh)]
+def lanes(v, heads):
+    return jnp.concatenate([v[h * HD : (h + 1) * HD, :] for h in range(heads)], axis=1)
+
+
+def turned_back(v, cos, sin):
+    half = HD // 2
+    out = []
+    for h in range(v.shape[0] // HD):
+        a, b = v[h * HD : h * HD + half, :], v[h * HD + half : (h + 1) * HD, :]
+        out += [a * cos + b * sin, b * cos - a * sin]
+    return jnp.concatenate(out, axis=0)
+
+
+def key_blocks(st, en, tk):
+    return jnp.min(st) // tk, (jnp.max(en) + tk - 1) // tk
+
+
+def attn_fwd_kernel(nh, tq, tk, q_ref, k_ref, v_ref, st_ref, en_ref, o_ref, ob_ref, l_ref, a_ref):
+    lo, hi = key_blocks(st_ref[...], en_ref[...], tk)
+    q = lanes(q_ref[...] * jnp.asarray(SCALE, bf16), nh)
+    st = jnp.concatenate([st_ref[...]] * nh, axis=1)
+    en = jnp.concatenate([en_ref[...]] * nh, axis=1)
+    W = nh * tq
+    a_ref[...] = jnp.zeros_like(a_ref)
 
     def body(j, c):
+        m, l = c
         off = pl.multiple_of(j * tk, tk)
-        kb = k_ref[pl.ds(off, tk), :]
-        vb = v_ref[:, pl.ds(off, tk)]
-        jj = off + lax.broadcasted_iota(jnp.int32, (tk, tq), 0)
-        vis = (jj >= st) & (jj < en)
-        out = []
-        for h in range(nh):
-            m, l, a = c[h]
-            s = dg(kb, qs[h], 1, 0) * SCALE
-            s = jnp.where(vis, s, NEG)
-            mn = jnp.maximum(m, jnp.max(s, axis=0, keepdims=True))
-            p = jnp.where(vis, jnp.exp(s - mn), 0.0)
-            sh = jnp.exp(m - mn)
-            l = l * sh + jnp.sum(p, axis=0, keepdims=True)
-            a = a * sh + dg(vb, p.astype(bf16), 1, 0)
-            out.append((mn, l, a))
-        return tuple(out)
-
-    init = tuple(
-        (jnp.full((1, tq), NEG, f32), jnp.zeros((1, tq), f32), jnp.zeros((HD, tq), f32))
-        for _ in range(nh)
-    )
-    res = lax.fori_loop(lo, hi, body, init)
+        jj = off + lax.broadcasted_iota(jnp.int32, (tk, W), 0)
+        s = dg(k_ref[pl.ds(off, tk), :], q, 1, 0)
+        s = jnp.where((jj >= st) & (jj < en), s, NEG)
+        mn = jnp.maximum(m, jnp.max(s, axis=0, keepdims=True))
+        p = jnp.exp(s - mn)
+        sh = jnp.exp(m - mn)
+        l = l * sh + jnp.sum(p, axis=0, keepdims=True)
+        a_ref[...] = a_ref[...] * sh + dg(v_ref[:, pl.ds(off, tk)], p.astype(bf16), 1, 0)
+        return mn, l
+
+    m, l = lax.fori_loop(lo, hi, body, (jnp.full((1, W), 0.1 * NEG, f32), jnp.zeros((1, W), f32)))
+    o = a_ref[...] / l
+    ls = m + jnp.log(l)
     for h in range(nh):
-        m, l, a = res[h]
-        o = a / l
-        o_ref[h * HD : (h + 1) * HD, :] = o
-        ob_ref[h * HD : (h + 1) * HD, :] = o.astype(bf16)
-        l_ref[h : h + 1, :] = m + jnp.log(l)
+        oh = o[:, h * tq : (h + 1) * tq]
+        o_ref[h * HD : (h + 1) * HD, :] = oh
+        ob_ref[h * HD : (h + 1) * HD, :] = oh.astype(bf16)
+        l_ref[h : h + 1, :] = ls[:, h * tq : (h + 1) * tq]
 
 
 def attn_fwd(qT, k, vT, st, en, tq=256, tk=256):
@@ -78,6 +87,7 @@
             jax.ShapeDtypeStruct((n, S), bf16),
             jax.ShapeDtypeStruct((nh, S), f32),
         ],
+        scratch_shapes=[pltpu.VMEM((HD, nh * tq), f32)],
         cost_estimate=pl.CostEstimate(
             flops=2 * S * S * n, bytes_accessed=8 * n * S, transcendentals=S * S * nh // 2
         ),
@@ -86,54 +96,54 @@
 
 
 def attn_bwd_kernel(
-    nh, tq, tk, q_ref, do_ref, o_ref, lse_ref, st_ref, en_ref, k_ref, kT_ref, v_ref, dq_ref, dk_ref, dv_ref
+    nh, tq, tk, q_ref, da_ref, wo_ref, o_ref, lse_ref, st_ref, en_ref, cos_ref, sin_ref, k_ref, kT_ref, v_ref,
+    out_ref, dk_ref, dv_ref, acc,
 ):
     i = pl.program_id(0)
+    n = nh * HD
 
     @pl.when(i == 0)
     def _():
         dk_ref[...] = jnp.zeros_like(dk_ref)
         dv_ref[...] = jnp.zeros_like(dv_ref)
 
-    st = st_ref[...]
-    en = en_ref[...]
-    lo = jnp.min(st) // tk
-    hi = (jnp.max(en) + tk - 1) // tk
-    qs = [q_ref[h * HD : (h + 1) * HD, :] for h in range(nh)]
-    dos = [do_ref[h * HD : (h + 1) * HD, :] for h in range(nh)]
-    dl = [
-        jnp.sum(dos[h].astype(f32) * o_ref[h * HD : (h + 1) * HD, :], axis=0, keepdims=True)
-        for h in range(nh)
-    ]
-    ls = [lse_ref[h : h + 1, :] for h in range(nh)]
-    dq_ref[...] = jnp.zeros_like(dq_ref)
+    here = pl.ds(pl.multiple_of(i * tq, tq), tq)
+    lo, hi = key_blocks(st_ref[...], en_ref[...], tk)
+    q = lanes(q_ref[...] * jnp.asarray(SCALE, bf16), nh)
+    do = lanes(dg(wo_ref[...], da_ref[...], 1, 1).astype(bf16), nh)
+    o = lanes(o_ref[...], nh)
+    dl = jnp.sum(do.astype(f32) * o, axis=0, keepdims=True)
+    ls = jnp.concatenate([lse_ref[h : h + 1, :] for h in range(nh)], axis=1)
+    st = jnp.concatenate([st_ref[...]] * nh, axis=1)
+    en = jnp.concatenate([en_ref[...]] * nh, axis=1)
+    acc[...] = jnp.zeros_like(acc)
 
     def body(j, _):
         off = pl.multiple_of(j * tk, tk)
-        kb = k_ref[pl.ds(off, tk), :]
-        kT = kT_ref[:, pl.ds(off, tk)]
-        vb = v_ref[pl.ds(off, tk), :]
-        jj = off + lax.broadcasted_iota(jnp.int32, (tk, tq), 0)
-        vis = (jj >= st) & (jj < en)
-        dk = jnp.zeros((HD, tk), f32)
-        dv = jnp.zeros((HD, tk), f32)
-        for h in range(nh):
-            s = dg(kb, qs[h], 1, 0) * SCALE
-            p = jnp.exp(jnp.where(vis, s - ls[h], NEG))
-            dp = dg(vb, dos[h], 1, 0)
-            dsc = (p * (dp - dl[h])).astype(bf16)
-            dq_ref[h * HD : (h + 1) * HD, :] += dg(kT, dsc, 1, 0)
-            dk = dk + dg(qs[h], dsc, 1, 1)
-            dv = dv + dg(dos[h], p.astype(bf16), 1, 1)
-        dk_ref[:, pl.ds(off, tk)] += dk
-        dv_ref[:, pl.ds(off, tk)] += dv
+        at = pl.ds(off, tk)
+        jj = off + lax.broadcasted_iota(jnp.int32, (tk, nh * tq), 0)
+        s = dg(k_ref[at, :], q, 1, 0)
+        dp = dg(v_ref[at, :], do, 1, 0)
+        p = jnp.exp(jnp.where((jj >= st) & (jj < en), s - ls, NEG))
+        ds = (p * (dp - dl)).astype(bf16)
+        acc[...] += dg(kT_ref[:, at], ds, 1, 0)
+        dk_ref[:, at] += dg(q, ds, 1, 1)
+        dv_ref[:, at] += dg(do, p.astype(bf16), 1, 1)
         return 0
 
     lax.fori_loop(lo, hi, body, 0)
-
-
-def attn_bwd(qT, doT, oT, lse, st, en, k, kT, v, tq=256, tk=256):
+    dq = jnp.concatenate([acc[:, h * tq : (h + 1) * tq] for h in range(nh)], axis=0) * SCALE
+    out_ref[pl.ds(0, n), here] = turned_back(dq, cos_ref[:, here], sin_ref[:, here]).astype(bf16)
+
+    @pl.when(i == pl.num_programs(0) - 1)
+    def _():
+        out_ref[pl.ds(n, HD), :] = turned_back(dk_ref[...], cos_ref[...], sin_ref[...]).astype(bf16)
+        out_ref[pl.ds(n + HD, HD), :] = dv_ref[...].astype(bf16)
+
+
+def attn_bwd(qT, da, woT, oT, lse, st, en, cos, sin, k, kT, v, tq=256, tk=256):
     n, S = qT.shape
+    E = da.shape[1]
     nh = n // HD
     blk = lambda r: pl.BlockSpec((r, tq), lambda i: (0, i))
     full = lambda s: pl.BlockSpec(s, lambda i: (0, 0))
@@ -141,20 +151,17 @@
         functools.partial(attn_bwd_kernel, nh, tq, tk),
         grid=(S // tq,),
         in_specs=[
-            blk(n), blk(n), blk(n), blk(nh), blk(1), blk(1),
-            full((S, HD)), full((HD, S)), full((S, HD)),
+            blk(n), pl.BlockSpec((tq, E), lambda i: (i, 0)), full((n, E)), blk(n), blk(nh), blk(1), blk(1),
+            full((HD // 2, S)), full((HD // 2, S)), full((S, HD)), full((HD, S)), full((S, HD)),
         ],
-        out_specs=[blk(n), full((HD, S)), full((HD, S))],
-        out_shape=[
-            jax.ShapeDtypeStruct((n, S), f32),
-            jax.ShapeDtypeStruct((HD, S), f32),
-            jax.ShapeDtypeStruct((HD, S), f32),
-        ],
+        out_specs=full((n + 2 * HD, S)),
+        out_shape=jax.ShapeDtypeStruct((n + 2 * HD, S), bf16),
+        scratch_shapes=[pltpu.VMEM((HD, S), f32), pltpu.VMEM((HD, S), f32), pltpu.VMEM((HD, nh * tq), f32)],
         cost_estimate=pl.CostEstimate(
             flops=5 * S * S * n, bytes_accessed=10 * n * S, transcendentals=S * S * nh // 2
         ),
         name="attn_bwd",
-    )(qT, doT, oT, lse, st, en, k, kT, v)
+    )(qT, da, woT, oT, lse, st, en, cos, sin, k, kT, v)
 
 
 MESH = pl.DeviceIdType.MESH
@@ -291,32 +298,24 @@
 
 
 class Scatter:
-    def __init__(self, p, part, a, x, ud, start, size, sems):
-        self.p, self.part, self.a, self.x, self.ud = p, part, a, x, ud
-        self.start, self.size, self.rows, self.sems = start, size, pl.ds(start, size), sems
-
-    def cross(self, y):
+    def __init__(self, p, a, x, ud, T, sems, part=None, make=None, stage=None):
+        self.p, self.a, self.x, self.ud, self.T, self.sems = p, a, x, ud, T, sems
+        self.part, self.make, self.stage = part, make, stage
+
+    def cross(self, y, slot=0):
         p = self.p
-        return remote(
-            self.part.at[2 * y + 1 - p.j, self.rows], self.x.at[y, self.rows],
-            self.sems.at[0, y], self.sems.at[1, y], "ctx", p.sib,
-        )
+        src = self.part.at[2 * y + 1 - p.j] if self.part is not None else self.stage.at[slot]
+        return remote(src, self.x.at[y], self.sems.at[0, y], self.sems.at[1, y], "ctx", p.sib)
 
     def load(self, y):
-        return pltpu.make_async_copy(
-            self.part.at[2 * y + self.p.j, self.rows], self.a.at[y, self.rows], self.sems.at[2, y]
-        )
+        return pltpu.make_async_copy(self.part.at[2 * y + self.p.j], self.a.at[y], self.sems.at[2, y])
 
     def go_up(self, y):
-        return remote(
-            self.a.at[y, self.rows], self.ud.at[y, self.rows], self.sems.at[3, y], self.sems.at[4, y], "ctx", self.p.c + 2
-        )
+        return remote(self.a.at[y], self.ud.at[y], self.sems.at[3, y], self.sems.at[4, y], "ctx", self.p.c + 2)
 
     def go_down(self, y, last=False):
         to = self.p.nz if last else y
-        return remote(
-            self.a.at[y, self.rows], self.ud.at[to, self.rows], self.sems.at[5, y], self.sems.at[6, y], "ctx", self.p.c - 2
-        )
+        return remote(self.a.at[y], self.ud.at[to], self.sems.at[5, y], self.sems.at[6, y], "ctx", self.p.c - 2)
 
     def begin(self, cross=True, load=True):
         nz = self.p.nz
@@ -329,8 +328,37 @@
             if load:
                 self.load(y).start()
 
+    def turn(self, i):
+        p = self.p
+        upper = p.z // (p.nz // 2)
+        return upper * i + (1 - upper) * (p.nz - 1 - i)
+
+    def compute(self, between=None):
+        p = self.p
+        for i in range(p.nz):
+            y, slot = self.turn(i), i % 2
+            if i > 1:
+                self.cross(self.turn(i - 2), slot).wait_send()
+            self.make(2 * y + 1 - p.j, self.stage.at[slot])
+            self.cross(y, slot).start()
+            self.make(2 * y + p.j, self.a.at[y])
+            if i > 0:
+                pl.when(p.z == 0)(functools.partial(self.edge, self.turn(i - 1), True, False))
+                pl.when(p.z == p.nz - 1)(functools.partial(self.edge, self.turn(i - 1), False, i == p.nz - 1))
+            if between is not None:
+                between(i)
+
+    def edge(self, y, up, last):
+        self.ready(y)
+        self.add(y, None)
+        if up:
+            self.go_up(y).start()
+        else:
+            self.go_down(y, last).start()
+
     def ready(self, y):
-        self.load(y).wait()
+        if self.part is not None:
+            self.load(y).wait()
         self.cross(y).wait_recv()
 
     def add(self, y, extra):
@@ -340,7 +368,7 @@
                 v = v + extra[y, r].astype(f32)
             self.a[y, r] = v.astype(bf16)
 
-        each(fn, self.start, self.size)
+        each(fn, 0, self.T)
 
     def edges(self):
         p = self.p
@@ -348,16 +376,12 @@
         @pl.when(p.z == 0)
         def _():
             for y in range(p.nz - 1, 0, -1):
-                self.ready(y)
-                self.add(y, None)
-                self.go_up(y).start()
+                self.edge(y, True, False)
 
         @pl.when(p.z == p.nz - 1)
         def _():
             for y in range(p.nz - 1):
-                self.ready(y)
-                self.add(y, None)
-                self.go_down(y, y == p.nz - 2).start()
+                self.edge(y, False, y == p.nz - 2)
 
     def step(self, t):
         p = self.p
@@ -399,16 +423,17 @@
                     v = v + self.ud[p.nz, r].astype(f32)
                 fn(r, v)
 
-            each(body, self.start, self.size)
+            each(body, 0, self.T)
 
         pl.when(p.low & p.high)(lambda: run(True, True))
         pl.when(p.z == 0)(lambda: run(False, p.nz > 1))
         pl.when(p.z == p.nz - 1)(lambda: run(True, False))
 
-    def finish(self):
+    def finish(self, staged=True):
         p = self.p
         for y in range(p.nz):
-            self.cross(y).wait_send()
+            if self.part is not None:
+                self.cross(y).wait_send()
 
             @pl.when(p.z < y)
             def _(y=y):
@@ -418,8 +443,20 @@
             def _(y=y):
                 self.go_down(y).wait_send()
 
+        if self.part is None and staged:
+            for i in range(max(p.nz - 2, 0), p.nz):
+                self.cross(self.turn(i), i % 2).wait_send()
+
     def all_steps(self):
         return [functools.partial(self.step, i) for i in range(1, self.p.nz - 1)]
+
+
+def strips(fn, width, step):
+    def body(i, _):
+        fn(pl.ds(pl.multiple_of(i * step, step), step))
+        return 0
+
+    lax.fori_loop(0, width // step, body, 0)
 
 
 def interleave(first, second):
@@ -465,7 +502,7 @@
 
 
 def params(cid):
-    return pltpu.CompilerParams(collective_id=cid, has_side_effects=True, vmem_limit_bytes=60 * 1024 * 1024)
+    return pltpu.CompilerParams(collective_id=cid, has_side_effects=True, vmem_limit_bytes=62 * 1024 * 1024)
 
 
 ANY = pl.BlockSpec(memory_space=pl.ANY)
@@ -543,59 +580,57 @@
 
 
 def middle_kernel(
-    nc, nf, parts, part, tok, og, g, wl, hid, n2, dm, w,
-    a, x, ud, own, dmo, rsem, nss, nrs, nls, dss, drs, dls, fss, frs, fls,
+    nc, nf, oT, wo, tok, og, g, wl, hid, n2, dm, w,
+    a, x, ud, stage, oblk, own, dmo, rsem, nss, nrs, nls, dss, drs, dls, fss, frs, fls,
 ):
     p = Place(nc, nf)
     greet(p, fsdp=True)
-    T = tok.shape[0]
-    size = T // parts
-    rs = [Scatter(p, part, a, x, ud, q * size, size, rsem.at[q]) for q in range(parts)]
-    ag = [
-        Gather(p, own, n2, pl.ds(q * size, size), nss.at[q], nrs.at[q], nls.at[q]) for q in range(parts)
-    ]
+    T, E = tok.shape
+
+    def make(d, ref):
+        oblk[...] = oT[:, pl.ds(pl.multiple_of(d * T, T), T)].T
+
+        def fn(r):
+            ref[:, r] = dg(oblk[...], wo[r, :], 1, 1).astype(bf16)
+
+        strips(fn, E, 512)
+
+    rs = Scatter(p, a, x, ud, T, rsem, make=make, stage=stage)
+    ag = Gather(p, own, n2, pl.ds(0, T), nss, nrs, nls)
     dmg = Gather(p, dmo, dm, pl.ds(0, T), dss, drs, dls)
     peers = Peers(p, lambda to: (wl, w.at[:, p.f]), fss, frs, (wl, w.at[:, p.f]), fls)
-    for q in range(parts):
-        rs[q].begin()
+    peers.start()
 
     def dm_rows(r):
         dmo[r] = (RES * og[r].astype(f32)).astype(bf16)
 
     each(dm_rows, 0, T)
     dmg.first()
-    rs[0].edges()
-    peers.start()
+    rs.compute()
 
     def rows(r, v):
         h = tok[r].astype(f32) + RES * v
         hid[r] = h
         own[r] = (h * lax.rsqrt(jnp.mean(h * h, axis=-1, keepdims=True) + EPS) * g[...]).astype(bf16)
 
-    pending = dmg.all_steps()[1:]
-    for q in range(parts):
-        interleave(pending, rs[q].all_steps())
-        if q + 1 < parts:
-            rs[q + 1].edges()
-        rs[q].total(rows)
-        ag[q].first()
-        pending = ag[q].all_steps()[1:]
-    for s in pending:
+    interleave(dmg.all_steps()[1:], rs.all_steps())
+    rs.total(rows)
+    ag.first()
+    for s in ag.all_steps()[1:]:
         s()
-    for q in range(parts):
-        ag[q].finish()
-        rs[q].finish()
+    ag.finish()
+    rs.finish()
     dmg.finish()
     peers.wait()
 
 
-def middle_call(nc, nf, parts, part, tok, og, g, wl):
+def middle_call(nc, nf, oT, wo, tok, og, g, wl):
     T, E = tok.shape
     _, R, M = wl.shape
     nz = nc // 2
     return pl.pallas_call(
-        functools.partial(middle_kernel, nc, nf, parts),
-        in_specs=[ANY, VM, VM, VM, ANY],
+        functools.partial(middle_kernel, nc, nf),
+        in_specs=[VM, VM, VM, VM, VM, ANY],
         out_specs=[VM, ANY, ANY, ANY],
         out_shape=[
             jax.ShapeDtypeStruct((T, E), f32),
@@ -604,50 +639,71 @@
             jax.ShapeDtypeStruct((nc, nf, R, M), bf16),
         ],
         scratch_shapes=scatter_scratch(nz, T, E)
-        + [pltpu.VMEM((T, E), bf16), pltpu.VMEM((T, E), bf16), DMA((parts, 7, nz))]
-        + [DMA((parts, 3, nc)), DMA((parts, nc)), DMA((parts,))]
+        + [pltpu.VMEM((2, T, E), bf16), pltpu.VMEM((T, oT.shape[0]), bf16)]
+        + [pltpu.VMEM((T, E), bf16), pltpu.VMEM((T, E), bf16), DMA((7, nz))]
+        + gather_sems(nc)
         + gather_sems(nc)
         + [DMA((nf,)), DMA((nf,)), DMA],
         compiler_params=params(2),
         name="attn_to_mlp",
-    )(part, tok, og, g, wl)
+    )(oT, wo, tok, og, g, wl)
 
 
 def turn_kernel(nc, nf, fold, *refs):
     it = iter(refs)
     take = lambda n: [next(it) for _ in range(n)]
-    part, n2, dm, dgu, act = take(5)
-    wd = next(it) if fold else None
+    n2, dm, dga, dup, act, wm = take(6)
     hid, og, g, dh, da = take(5)
     lay = next(it) if fold else None
-    gg, y, gbuf = take(3)
+    gg, gs, y, gbuf = take(4)
     mpart = next(it) if fold else None
     a, x, ud, own, rsem = take(5)
     nss, nrs, nls, fss, frs, fls = take(6)
-    dguv, actv, nb, db, nt, go, lsem, ssem = take(8)
+    dguv, actv, wide, nt, go, mp, lsem, ssem = take(8)
     p = Place(nc, nf)
+    nz = p.nz
     greet(p, fsdp=True)
     T, E = hid.shape
-    S, F2 = dgu.shape
-    F = act.shape[1]
+    S, F = act.shape
+    F2 = 2 * F
     R = E // (nc * nf)
     B = nf * R
-    rs = Scatter(p, part, a, x, ud, 0, T, rsem)
+
+    def fetch(src, dst, i):
+        return pltpu.make_async_copy(src, dst, lsem.at[4 + i])
+
+    big = [
+        fetch(wm.at[:, pl.ds(0, F2)], wide.at[pl.ds(0, E), pl.ds(0, F2)], 0),
+        fetch(dga, dguv.at[:, pl.ds(0, F)], 1),
+        fetch(dup, dguv.at[:, pl.ds(F, F)], 2),
+        fetch(act, actv, 3),
+    ]
+
+    def make(d, ref):
+        tok = dguv[pl.ds(pl.multiple_of(d * T, T), T), :]
+
+        def fn(r):
+            ref[:, r] = dg(tok, wide[r, pl.ds(0, F2)], 1, 1).astype(bf16)
+
+        strips(fn, E, 512)
+
+    rs = Scatter(p, a, x, ud, T, rsem, make=make, stage=mp)
     ag = Gather(p, own, da, pl.ds(0, T), nss, nrs, nls)
-    rs.begin()
-    big = [pltpu.make_async_copy(dgu, dguv, lsem.at[4]), pltpu.make_async_copy(act, actv, lsem.at[5])]
     if fold:
-        x2, ud2, wdv, mp, msem, wsem, psem = take(7)
-        ms = Scatter(p, mpart, a, x2, ud2, 0, T, msem)
-        big.append(pltpu.make_async_copy(wd, wdv, wsem))
+        x2, ud2, wdv, msem, psem = take(5)
+        ms = Scatter(p, a, x2, ud2, T, msem, part=mpart)
+        big.append(fetch(wm.at[:, pl.ds(F2, F)], wdv, 4))
     for cp in big:
         cp.start()
 
+    def spot(i):
+        return pl.ds(pl.multiple_of(i * B, B), B)
+
     def column(b, slot):
-        at = pl.ds(pl.multiple_of(b * B, B), B)
+        at = spot(b)
         return (
-            pltpu.make_async_copy(n2.at[:, at], nb.at[slot], lsem.at[slot]),
-            pltpu.make_async_copy(dm.at[:, at], db.at[slot], lsem.at[2 + slot]),
+            pltpu.make_async_copy(n2.at[:, at], wide.at[pl.ds(0, S), spot(slot)], lsem.at[slot]),
+            pltpu.make_async_copy(dm.at[:, at], wide.at[pl.ds(0, S), spot(2 + slot)], lsem.at[2 + slot]),
         )
 
     def keep(b, slot):
@@ -658,15 +714,42 @@
         at = pl.ds(pl.multiple_of(to * R, R), R)
         return remote(gbuf.at[b, at], y.at[p.f, b], fss.at[k, b], frs.at[k, b], "fsdp", to)
 
-    def mine(b):
+    def terms(b, slot):
         at = pl.ds(pl.multiple_of(p.f * R, R), R)
-        return pltpu.make_async_copy(gbuf.at[b, at], y.at[p.f, b], fls.at[b])
+        srcs = [gbuf.at[b, at]] + [y.at[lax.rem(p.f + k, nf), b] for k in range(1, nf)]
+        return [
+            pltpu.make_async_copy(src, go.at[slot, pl.ds(i * R, R)], fls.at[slot, i]) for i, src in enumerate(srcs)
+        ]
+
+    def stored(b, slot):
+        return pltpu.make_async_copy(go.at[slot, pl.ds(0, R)], gs.at[b], ssem.at[slot])
+
+    def sums(first, last):
+        for b in range(first, last):
+            slot = b % 2
+            for k in range(1, nf):
+                peer(b, k).wait()
+            if b > 1:
+                stored(b - 2, slot).wait()
+            cps = terms(b, slot)
+            for cp in cps:
+                cp.start()
+            for cp in cps:
+                cp.wait()
+
+            def fn(r, slot=slot):
+                v = go[slot, r].astype(f32)
+                for i in range(1, nf):
+                    v = v + go[slot, pl.ds(r.start + i * R, CH)].astype(f32)
+                go[slot, r] = v.astype(bf16)
+
+            each(fn, 0, R)
+            stored(b, slot).start()
 
     def send(b):
         keep(b, b % 2).wait()
         for k in range(1, nf):
             peer(b, k).start()
-        mine(b).start()
 
     def grads(b, _):
         slot = b % 2
@@ -677,9 +760,9 @@
                 cp.start()
 
         now = column(b, slot)
-        for src, val, base, width, cp in ((nb, dguv, 0, F2, now[0]), (db, actv, F2, F, now[1])):
+        for at, val, base, width, cp in ((slot, dguv, 0, F2, now[0]), (2 + slot, actv, F2, F, now[1])):
             cp.wait()
-            nt[...] = src[slot].T
+            nt[...] = wide[pl.ds(0, S), spot(at)].T
             step = min(512, width)
 
             def dots(i, _, val=val, base=base, step=step):
@@ -716,17 +799,14 @@
         out.start()
         return 0
 
+    gg[...] = jnp.zeros_like(gg)
+    for cp in big[:3]:
+        cp.wait()
+    rs.compute()
     for cp in column(0, 0):
         cp.start()
-    gg[...] = jnp.zeros_like(gg)
-    rs.edges()
-    for cp in big:
+    for cp in big[3:]:
         cp.wait()
-    if fold:
-        lax.fori_loop(0, nc, mlp, 0)
-        for slot in range(2):
-            pltpu.make_async_copy(mp.at[slot], mpart.at[slot], psem.at[slot]).wait()
-        ms.begin(load=False)
     steps = rs.all_steps()
     bounds = [nc * i // (len(steps) + 1) for i in range(len(steps) + 2)]
     for i in range(len(steps) + 1):
@@ -734,6 +814,13 @@
         if i < len(steps):
             steps[i]()
     send(nc - 1)
+    if fold:
+        for i in range(max(nz - 2, 0), nz):
+            rs.cross(rs.turn(i), i % 2).wait_send()
+        lax.fori_loop(0, nc, mlp, 0)
+        for slot in range(2):
+            pltpu.make_async_copy(mp.at[slot], mpart.at[slot], psem.at[slot]).wait()
+        ms.begin(load=False)
 
     def rows(r, dn):
         h = hid[r]
@@ -747,11 +834,20 @@
 
     rs.total(rows)
     ag.first()
-    rs.finish()
+    rs.finish(not fold)
     if fold:
         ms.begin(cross=False)
         ms.edges()
-    interleave(ag.all_steps()[1:], ms.all_steps() if fold else [])
+    sums(0, nc // 4)
+    more = ms.all_steps() if fold else []
+    done = nc // 4
+    for i, s in enumerate(ag.all_steps()[1:]):
+        s()
+        if i < len(more):
+            more[i]()
+        upto = min(nc - 1, done + max(1, nc // 4))
+        sums(done, upto)
+        done = upto
     if fold:
 
         def out(r, v):
@@ -760,29 +856,28 @@
         ms.total(out)
         ms.finish()
     ag.finish()
-    for b in range(nc):
-        for k in range(1, nf):
-            peer(b, k).wait()
-        mine(b).wait()
-
-
-def turn_call(nc, nf, fold, part, n2, dm, dgu, act, wd, hid, og, g):
+    sums(done, nc)
+    for b in range(nc - 2, nc):
+        stored(b, b % 2).wait()
+
+
+def turn_call(nc, nf, fold, n2, dm, dga, dup, act, wm, hid, og, g):
     T, E = hid.shape
-    S, F2 = dgu.shape
-    F = act.shape[1]
-    M = F2 + F
+    S, F = act.shape
+    F2, M = 2 * F, 3 * F
     R = E // (nc * nf)
     B = nf * R
     nz = nc // 2
     VMEM = pltpu.VMEM
     return pl.pallas_call(
         functools.partial(turn_kernel, nc, nf, fold),
-        in_specs=[ANY] * (5 + fold) + [VM, VM, VM],
-        out_specs=[VM, ANY] + [VM] * fold + [VM, ANY, ANY] + [ANY] * fold,
+        in_specs=[ANY] * 6 + [VM, VM, VM],
+        out_specs=[VM, ANY] + [VM] * fold + [VM, ANY, ANY, ANY] + [ANY] * fold,
         out_shape=[jax.ShapeDtypeStruct((T, E), f32), jax.ShapeDtypeStruct((nc, T, E), bf16)]
         + [jax.ShapeDtypeStruct((T, E), bf16)] * fold
         + [
             jax.ShapeDtypeStruct((8, E), f32),
+            jax.ShapeDtypeStruct((nc, R, M), bf16),
             jax.ShapeDtypeStruct((nf, nc, R, M), bf16),
             jax.ShapeDtypeStruct((nc, B, M), bf16),
         ]
@@ -790,33 +885,54 @@
         scratch_shapes=scatter_scratch(nz, T, E)
         + [VMEM((T, E), bf16), DMA((7, nz))]
         + gather_sems(nc)
-        + [DMA((nf, nc)), DMA((nf, nc)), DMA((nc,))]
-        + [VMEM((S, F2), bf16), VMEM((S, F), bf16), VMEM((2, S, B), bf16), VMEM((2, S, B), bf16)]
-        + [VMEM((B, S), bf16), VMEM((2, B, M), bf16), DMA((6,)), DMA((2,))]
-        + [
-            VMEM((nz, T, E), bf16), VMEM((nz + 1, T, E), bf16), VMEM((E, F), bf16), VMEM((2, T, E), bf16),
-            DMA((7, nz)), DMA, DMA((2,)),
-        ]
-        * fold,
+        + [DMA((nf, nc)), DMA((nf, nc)), DMA((2, nf))]
+        + [VMEM((S, F2), bf16), VMEM((S, F), bf16), VMEM((max(E, S), max(F2, 4 * B)), bf16)]
+        + [VMEM((B, S), bf16), VMEM((2, B, M), bf16), VMEM((2, T, E), bf16), DMA((9,)), DMA((2,))]
+        + [VMEM((nz, T, E), bf16), VMEM((nz + 1, T, E), bf16), VMEM((E, F), bf16), DMA((7, nz)), DMA((2,))] * fold,
         compiler_params=params(3),
         name="mlp_to_attn",
-    )(part, n2, dm, dgu, act, *([wd] if fold else []), hid, og, g)
+    )(n2, dm, dga, dup, act, wm, hid, og, g)
 
 
 def close_kernel(
-    nc, nf, parts, part, tok, dh, g, gw, ggm, dx, gout, ggout,
-    a, x, ud, y, zb, gg, gbuf, gsum, gfin, rsem, fss, frs, fls, css, crs, cls, s1, r1, s2, r2, l2,
+    nc, nf, dqkv, wq, oT, n1, da, tok, dh, g, ggm, dx, gout, ggout,
+    a, x, ud, stage, dblk, wqv, big, gt, gb, y, zb, gg, gbuf, gsum, gfin, rsem, lsem,
+    fss, frs, fls, css, crs, cls, s1, r1, s2, r2, l2,
 ):
     p = Place(nc, nf)
     greet(p, ctx=True, fsdp=True)
     T, E = tok.shape
-    R = gw.shape[2]
-    size = T // parts
-    rs = [Scatter(p, part, a, x, ud, q * size, size, rsem.at[q]) for q in range(parts)]
-    peers = Peers(p, lambda to: (gw.at[:, to], y.at[p.f]), fss, frs, (gw.at[:, p.f], y.at[p.f]), fls)
-    for q in range(parts):
-        rs[q].begin()
-    peers.start()
+    Q = dqkv.shape[0]
+    H = oT.shape[0]
+    R = E // (nc * nf)
+    B = nf * R
+    weights = pltpu.make_async_copy(wq.at[:, pl.ds(0, Q)], wqv, lsem.at[4])
+    weights.start()
+
+    def column(b, slot):
+        at = pl.ds(pl.multiple_of(b * B, B), B)
+        return (
+            pltpu.make_async_copy(n1.at[:, at], big.at[0, slot], lsem.at[slot]),
+            pltpu.make_async_copy(da.at[:, at], big.at[1, slot], lsem.at[2 + slot]),
+        )
+
+    for cp in column(0, 0):
+        cp.start()
+
+    def make(d, ref):
+        dblk[...] = dqkv[:, pl.ds(pl.multiple_of(d * T, T), T)].T
+
+        def fn(r):
+            ref[:, r] = dg(dblk[...], wqv[r, :], 1, 1).astype(bf16)
+
+        strips(fn, E, 512)
+
+    rs = Scatter(p, a, x, ud, T, rsem, make=make, stage=stage)
+
+    def pieces(to):
+        return gb.at[:, pl.ds(pl.multiple_of(to * R, R), R)], y.at[p.f]
+
+    peers = Peers(p, pieces, fss, frs, pieces(p.f), fls)
     gg[...] = jnp.zeros_like(gg)
 
     def piece(k):
@@ -848,14 +964,30 @@
         dx[r] = dh[r] + inv * (e - xn * jnp.mean(e * xn, axis=-1, keepdims=True))
         gg[...] += jnp.sum((xn * dn).reshape(CH // 8, 8, E), axis=0)
 
-    for q in range(parts):
-        rs[q].edges()
-    for q in range(parts):
-        for s in rs[q].all_steps():
-            s()
-        if q == 0:
-            grads()
-        rs[q].total(rows)
+    weights.wait()
+    rs.compute()
+
+    def products(b, _):
+        slot = b % 2
+
+        @pl.when(b + 1 < nc)
+        def _():
+            for cp in column(b + 1, 1 - slot):
+                cp.start()
+
+        for cp in column(b, slot):
+            cp.wait()
+        gt[pl.ds(0, Q), :] = dg(dqkv[...], big[0, slot], 1, 0)
+        gt[pl.ds(Q, H), :] = dg(oT[...], big[1, slot], 1, 0)
+        gb[b] = gt[...].T.astype(bf16)
+        return 0
+
+    lax.fori_loop(0, nc, products, 0)
+    peers.start()
+    for s in rs.all_steps():
+        s()
+    grads()
+    rs.total(rows)
 
     groups = E // 128
     sa = jnp.sum(gg[...], axis=0, keepdims=True)
@@ -897,17 +1029,20 @@
     for k in range(1, nc):
         piece(k).wait()
     mine.wait()
-    for q in range(parts):
-        rs[q].finish()
-
-
-def close_call(nc, nf, parts, part, tok, dh, g, gw, ggm):
+    rs.finish()
+
+
+def close_call(nc, nf, dqkv, wq, oT, n1, da, tok, dh, g, ggm):
     T, E = tok.shape
-    _, _, R, A = gw.shape
+    S = n1.shape[0]
+    Q, H = dqkv.shape[0], oT.shape[0]
+    A = Q + H
+    R = E // (nc * nf)
     nz = nc // 2
+    VMEM = pltpu.VMEM
     return pl.pallas_call(
-        functools.partial(close_kernel, nc, nf, parts),
-        in_specs=[ANY, VM, VM, VM, ANY, VM],
+        functools.partial(close_kernel, nc, nf),
+        in_specs=[VM, ANY, VM, ANY, ANY, VM, VM, VM, VM],
         out_specs=[VM, ANY, VM],
         out_shape=[
             jax.ShapeDtypeStruct((T, E), f32),
@@ -915,20 +1050,23 @@
             jax.ShapeDtypeStruct((8, 128), f32),
         ],
         scratch_shapes=scatter_scratch(nz, T, E)
+        + [VMEM((2, T, E), bf16), VMEM((T, Q), bf16), VMEM((E, Q), bf16), VMEM((2, 2, S, nf * R), bf16)]
+        + [VMEM((A, nf * R), f32), VMEM((nc, nf * R, A), bf16)]
         + [
-            pltpu.VMEM((nf, nc, R, A), bf16),
-            pltpu.VMEM((nc, R, A), bf16),
-            pltpu.VMEM((8, E), f32),
-            pltpu.VMEM((nf, E // 128, 8, 128), f32),
-            pltpu.VMEM((E // 128, 8, 128), f32),
-            pltpu.VMEM((nc, 8, 128), f32),
-            DMA((parts, 7, nz)),
+            VMEM((nf, nc, R, A), bf16),
+            VMEM((nc, R, A), bf16),
+            VMEM((8, E), f32),
+            VMEM((nf, E // 128, 8, 128), f32),
+            VMEM((E // 128, 8, 128), f32),
+            VMEM((nc, 8, 128), f32),
+            DMA((7, nz)),
+            DMA((5,)),
         ]
         + [DMA((nf,)), DMA((nf,)), DMA, DMA((nc,)), DMA((nc,)), DMA]
         + [DMA((nf,)), DMA((nf,)), DMA((nc,)), DMA((nc,)), DMA],
         compiler_params=params(4),
         name="close_row",
-    )(part, tok, dh, g, gw, ggm)
+    )(dqkv, wq, oT, n1, da, tok, dh, g, ggm)
 
 
 def rms(v):
@@ -946,9 +1084,6 @@
     a, b = v[:, 0], v[:, 1]
     s = sign * sin
     return jnp.stack([a * cos - b * s, b * cos + a * s], axis=1).reshape(heads * HD, -1)
-
-
-PB, PD = 1, 2
 
 
 def local(
@@ -1011,9 +1146,8 @@
     vT = qkv[VO:].astype(bf16)
     k, v = kT.T, vT.T
     oT, oTb, lse = attn_fwd(qT, k, vT, st, en)
-    attn = dg(oTb, w_o, 0, 1).astype(bf16).reshape(nc, T, E)
-
-    hidden, n2, dm, wm = middle_call(nc, nf, PB, attn, tok, og, g_mlp, wm)
+
+    hidden, n2, dm, wm = middle_call(nc, nf, oTb, w_o, tok, og, g_mlp, wm)
     n2, dm, wm = n2.reshape(S, E), dm.reshape(S, E), wm.reshape(E, -1)
     w_gu, w_d = wm[:, : 2 * FFL], wm[:, 2 * FFL :]
     gu = dg(n2, w_gu, 1, 0)
@@ -1023,25 +1157,19 @@
     d_act = dg(dm, w_d, 1, 0)
     d_gate = (d_act * up * sg * (1.0 + gate * (1.0 - sg))).astype(bf16)
     d_up = (d_act * gate * sg).astype(bf16)
-    d_gu = jnp.concatenate([d_gate, d_up], axis=1)
-    dn2 = dg(d_gu, w_gu, 1, 1).astype(bf16).reshape(nc, T, E)
+    turn = (n2, dm, d_gate, d_up, act, wm, hidden, og, g_mlp)
     if nz <= 4:
-        dh, da, layer_out, ggm, gm = turn_call(nc, nf, True, dn2, n2, dm, d_gu, act, w_d, hidden, og, g_mlp)[:5]
+        dh, da, layer_out, ggm, gm = turn_call(nc, nf, True, *turn)[:5]
     else:
-        dh, da, ggm, gm = turn_call(nc, nf, False, dn2, n2, dm, d_gu, act, None, hidden, og, g_mlp)[:4]
+        dh, da, ggm, gm = turn_call(nc, nf, False, *turn)[:4]
         mlp = dg(act, w_d, 1, 1).astype(bf16)
         mlp = lax.psum_scatter(mlp, "ctx", scatter_dimension=0, tiled=True)
         layer_out = (hidden + RES * mlp.astype(f32)).astype(bf16)
     da = da.reshape(S, E)
-    gm = exchange(jnp.sum(gm.astype(f32), axis=0).astype(bf16))
-
-    doT = dg(w_o, da, 0, 1).astype(bf16)
-    dqT, dkT, dvT = attn_bwd(qT, doT, oT, lse, st, en, k, kT, v)
-    dqk = rotate(jnp.concatenate([dqT, dkT], axis=0) * SCALE, cos, sin, -1.0).astype(bf16)
-    dqkv = jnp.concatenate([dqk, dvT.astype(bf16)], axis=0)
-    dn1 = dg(dqkv, w_qkv, 0, 1).astype(bf16).reshape(nc, T, E)
-    ga = jnp.concatenate([dg(dqkv, n1, 1, 0), dg(oTb, da, 1, 0)], axis=0).astype(bf16).T
-    input_grad, ga, gains = close_call(nc, nf, PD, dn1, tok, dh, g_attn, ga.reshape(nc, nf, R, -1), ggm)
+    gm = exchange(gm)
+
+    dqkv = attn_bwd(qT, da, w_o.T, oT, lse, st, en, cos, sin, k, kT, v)
+    input_grad, ga, gains = close_call(nc, nf, dqkv, wa, oTb, n1, da, tok, dh, g_attn, ggm)
     at = lax.rem((lax.axis_index("ctx") * nf + lax.axis_index("fsdp")) * R, 128)
     gains = lax.dynamic_slice_in_dim(gains, at, R, 1)
 

time: 875 us -> 789 us (0.902); the launches traced: 862 us -> 785 us
  matrix products: 112 us -> 53.6 us
  other arithmetic: 59.3 us -> 35.7 us
  local copies, waits for them, and re-layouts: 43 us -> 25.5 us
  waiting for transfers between devices: 0.01 us -> 13.1 us
    dot_general x9 -> x3, matrix products: 112 us -> 53.6 us  [dg(): lax.dot_general(a, b, (((ca,), (cb,)), ((), ())), preferred_element_type=...]
    pallas_call x1, Pallas kernels: 185 us -> 205 us  [turn_call(): pl.pallas_call(functools.partial(turn_kernel, nc, nf, fold), in_specs=[AN...]
    pallas_call x1, Pallas kernels: 41.3 us -> 22.5 us  [attn_fwd(): pl.pallas_call(functools.partial(attn_fwd_kernel, nh, tq, tk), grid=(S //...]
    pallas_call x2, Pallas kernels: 270 us -> 284 us  [the longest x1 172 us: middle_call(): pl.pallas_call(functools.partial(middle_kernel, nc, nf), in_specs=[VM, VM...]
    all_to_all x2, waiting for transfers between devices: 0.01 us -> 13.1 us  [exchange(): return lax.all_to_all(w, 'ctx', 0, 0, tiled=True)]
    reduce_sum x1 -> x0, other arithmetic: 9.9 us -> none  [local(): gm = exchange(jnp.sum(gm.astype(f32), axis=0).astype(bf16))]
  transfers between devices with their start and end apart: 2 -> 2, of which waited for: 0 -> 1; matrix products, arithmetic and copies ran while one was open for 11% -> 5% of each run, Pallas kernels for 21% -> 22%
where the time goes in v4:
time: 789 us; the launch traced here: 785 us
  Pallas kernels  646 us (82%)
  matrix products  53.6 us (7%)
  other arithmetic  35.7 us (5%)
  local copies, waits for them, and re-layouts  25.5 us (3%)
  waiting for transfers between devices  13.1 us (2%)
  starting transfers between devices  9.69 us (1%)
    pallas_call x1, Pallas kernels, turn_call(): pl.pallas_call(functools.partial(turn_kernel, nc, nf, fold), in_specs=[AN...  205 us
    pallas_call x1, Pallas kernels, middle_call(): pl.pallas_call(functools.partial(middle_kernel, nc, nf), in_specs=[VM, VM...  172 us
    pallas_call x1, Pallas kernels, close_call(): pl.pallas_call(functools.partial(close_kernel, nc, nf), in_specs=[VM, ANY...  112 us
    pallas_call x1, Pallas kernels, open_call(): pl.pallas_call(functools.partial(open_kernel, nc, nf), in_specs=[ANY, ANY...  99.1 us
    dot_general x3, matrix products, dg(): lax.dot_general(a, b, (((ca,), (cb,)), ((), ())), preferred_element_type=...  53.6 us
    pallas_call x1, Pallas kernels, attn_bwd(): pl.pallas_call(functools.partial(attn_bwd_kernel, nh, tq, tk), grid=(S //...  35.8 us
    pallas_call x1, Pallas kernels, attn_fwd(): pl.pallas_call(functools.partial(attn_fwd_kernel, nh, tq, tk), grid=(S //...  22.5 us
  transfers between devices with their start and end apart: 2, of which 1 were waited for; matrix products, arithmetic and copies ran while one was open for 5% of the time, Pallas kernels for 22%

profile of v4, /device:TPU:0, one launch (start us, length us, event | category | flops | bytes accessed | tf_op | source)
XLA Modules:
  0.0 785.0 jit_solution(15514601422207099147)
XLA Ops:
  1.6 1.1 convert_element_type.101
  2.7 1.1 convert_element_type.104
  6.0 1.8 convert_element_type.106
  9.0 1.5 copy_bitcast_fusion
  11.6 99.1 %open_row.1 = (bf16[8,256,2048]{2,1,0:T(8,128)(2,1)}, s32[8,8,256]{2,1,0:T(8,128)}, bf16[8,4,64,768]{3,2,1,0:T(8,128)(2,1)}) custom-call(bf16[256,2048]{1,0:T(8,128)(2,1)} %bitcast.90, s32[8,256]{1,0:T(8,128)} %pad.8.ids, bf16[8,64,768]{2,1,0:T(8,128)(2,1)} %bitcast.109), custom_call_target="tpu_custom_call" | custom-call | tf_op jit(solution)/shard_map/open_row/pallas_call | solution.py:566
  110.7 3.0 maximum_bitcast_fusion
  113.7 4.9 all-to-all-start
  118.7 5.1 multiply_reduce_fusion
  124.8 8.6 %fusion.1.n1 = bf16[2048,2048]{1,0:T(8,128)(2,1)} fusion(f32[2048]{0:T(1024)S(1)} %get-tuple-element.52, f32[2048]{0:T(1024)S(1)} %bitcast.127, bf16[8,256,2048]{2,1,0:T(8,128)(2,1)} %get-tuple-element.33), kind=kLoop, calls=%fused_computation.2 | loop fusion | flops 16777216 | bytes 16793600 | tf_op jit(solution)/shard_map/convert_element_type | solution.py:1141
  133.4 5.9 fusion.6
  144.5 2.0 copy.40.k_ref
  146.5 2.0 copy.52
  148.4 1.9 copy.41.v_ref
  150.4 2.3 fusion.8
  153.2 22.5 %attn_fwd.1 = (f32[256,2048]{1,0:T(8,128)}, bf16[256,2048]{1,0:T(8,128)(2,1)}, f32[4,2048]{1,0:T(4,128)}) custom-call(bf16[256,2048]{1,0:T(8,128)(2,1)} %bitcast.116, bf16[2048,64]{1,0:T(8,128)(2,1)} %copy.40.k_ref, bf16[64,2048]{1,0:T(8,128)(2,1)} %copy.41.v_ref, s32[1,2048]{1,0:T(1,128)} %get-tuple-element.74.st_ref, s32[1,2048]{1,0:T(1,128)} %get-tuple-element.73.en_ref), custom_call_target="tpu_custom_call" | custom-call | flops 2147483648 | bytes 4194304 | tf_op jit(solution)/shard_map/attn_fwd/pallas_call | solution.py:80
  175.7 1.5 slice_bitcast_fusion.2
  177.2 13.1 %all-to-all-done.wl = bf16[8,64,3072]{2,1,0:T(8,128)(2,1)} async-done(((bf16[8,64,3072]{2,1,0:T(8,128)(2,1)}), bf16[8,64,3072]{2,1,0:T(8,128)(2,1)}, u32[]{:S(2)}, u32[]{:S(2)}) %all-to-all-start) | async-done | bytes 3145760 | tf_op jit(solution)/shard_map/all_to_all | solution.py:1116
  190.2 172.3 %attn_to_mlp.1 = (f32[256,2048]{1,0:T(8,128)}, bf16[8,256,2048]{2,1,0:T(8,128)(2,1)}, bf16[8,256,2048]{2,1,0:T(8,128)(2,1)}, bf16[8,4,64,3072]{3,2,1,0:T(8,128)(2,1)}) custom-call(bf16[256,2048]{1,0:T(8,128)(2,1)} %get-tuple-element.35.oT, bf16[2048,256]{1,0:T(8,128)(2,1)} %get-tuple-element.60.wo, bf16[256,2048]{1,0:T(8,128)(2,1)} %bitcast.91, ...), custom_call_target="tpu_custom_call" | custom-call | tf_op jit(solution)/shard_map/attn_to_mlp/pallas_call | solution.py:631
  362.5 24.2 %fusion.2 = f32[2048,2048]{1,0:T(8,128)} fusion(bf16[2048,2048]{1,0:T(8,128)(2,1)} %bitcast.99, bf16[2048,3072]{1,0:T(8,128)(2,1)} %bitcast.86), kind=kOutput, calls=%fused_computation.4 | convolution fusion | flops 17179869184 | bytes 33554432 | tf_op jit(solution)/shard_map/dot_general | solution.py:24
  386.6 23.5 %multiply_convert_fusion.1 = (bf16[2048,1024]{1,0:T(8,128)(2,1)}, bf16[2048,1024]{1,0:T(8,128)(2,1)}, bf16[2048,1024]{1,0:T(8,128)(2,1)}) fusion(f32[2048,2048]{1,0:T(8,128)} %fusion.2, bf16[2048,2048]{1,0:T(8,128)(2,1)} %bitcast.101, bf16[2048,3072]{1,0:T(8,128)(2,1)} %bitcast.87), kind=kOutput, calls=%fused_computation.7 | convolution fusion | flops 8623489024 | bytes 41943040 | tf_op jit(solution)/shard_map/dot_general | solution.py:24
  410.1 204.9 %mlp_to_attn.1 = (f32[256,2048]{1,0:T(8,128)}, bf16[8,256,2048]{2,1,0:T(8,128)(2,1)}, bf16[256,2048]{1,0:T(8,128)(2,1)}, f32[8,2048]{1,0:T(8,128)}, bf16[8,64,30...) custom-call(bf16[2048,2048]{1,0:T(8,128)(2,1)} %bitcast.100, ...), custom_call_target="tpu_custom_call" | custom-call | tf_op jit(solution)/shard_map/mlp_to_attn/pallas_call | solution.py:872
  615.1 4.8 all-to-all-start.1
  619.8 1.4 copy.42.wo_ref
  621.3 35.8 %attn_bwd.1.dqkv = bf16[384,2048]{1,0:T(8,128)(2,1)} custom-call(bf16[256,2048]{1,0:T(8,128)(2,1)} %bitcast.117, bf16[2048,2048]{1,0:T(8,128)(2,1)} %bitcast.97, bf16[256,2048]{1,0:T(8,128)(2,1)} %copy.42.wo_ref, f32[256,2048]{1,0:T(8,128)} %get-tuple-element.43.o_ref, f32[4,2048]{1,0:T(4,128)} %get-tuple-element.44.lse_ref, ...), custom_call_target="tpu_custom_call" | custom-call | flops 5368709120 | bytes 5242880 | tf_op jit(solution)/shard_map/attn_bwd/pallas_call | solution.py:150
  657.1 111.7 %close_row.1 = (f32[256,2048]{1,0:T(8,128)}, bf16[8,64,640]{2,1,0:T(8,128)(2,1)}, f32[8,128]{1,0:T(8,128)}) custom-call(bf16[384,2048]{1,0:T(8,128)(2,1)} %attn_bwd.1.dqkv, bf16[2048,768]{1,0:T(8,128)(2,1)} %bitcast.93, bf16[256,2048]{1,0:T(8,128)(2,1)} %get-tuple-element.35.oT, bf16[2048,2048]{1,0:T(8,128)(2,1)} %fusion.1.n1, bf16[2048,2048]{1,0:T(8,128)(2,1)} %bitcast.98, ...), custom_call_target="tpu_custom_call" | custom-call | tf_op jit(solution)/shard_map/close_row/pallas_call | solution.py:1043
  768.8 1.1 convert_bitcast_fusion.3
  771.6 1.1 convert_bitcast_fusion.5
  775.2 2.6 convert_bitcast_fusion
  777.8 1.6 copy.60
  779.4 1.6 copy.61
  780.9 1.6 copy.62
  783.5 1.3 copy.73
  (72 shorter events, 17.3 us)
Async XLA Ops:
  0.6 7.2 copy-start.4
  5.9 2.2 copy-start.5
  5.9 2.5 copy-start.13
  5.9 2.5 copy-start.14
  6.0 2.5 copy-start.15
  113.7 10.1 %copy-start = (bf16[8,4,64,768]{3,2,1,0:T(8,128)(2,1)S(1)}, bf16[8,4,64,768]{3,2,1,0:T(8,128)(2,1)}, u32[]{:S(2)}) copy-start(bf16[8,4,64,768]{3,2,1,0:T(8,128)(2,1)} %get-tuple-element.31) | copy-start | bytes 9437188
  113.7 76.5 %all-to-all-start = ((bf16[8,64,3072]{2,1,0:T(8,128)(2,1)}), bf16[8,64,3072]{2,1,0:T(8,128)(2,1)}, u32[]{:S(2)}, u32[]{:S(2)}) async-start(bf16[8,64,3072]{2,1,0:T(8,128)(2,1)} %maximum_bitcast_fusion), calls=%async_computation | async-start | bytes 6291456 | tf_op jit(solution)/shard_map/all_to_all | solution.py:1116
  124.8 8.6 %copy-start.10 = (f32[2048]{0:T(1024)}, f32[2048]{0:T(1024)S(1)}, u32[]{:S(2)}) copy-start(f32[2048]{0:T(1024)S(1)} %get-tuple-element.52) | copy-start | bytes 24580
  133.4 6.9 copy-start.11
  142.5 2.0 copy-start.8
  142.6 33.1 %copy-start.7 = (f32[32,2048]{1,0:T(8,128)}, f32[32,2048]{1,0:T(8,128)S(1)}, u32[]{:S(2)}) copy-start(f32[32,2048]{1,0:T(8,128)S(1)} %get-tuple-element.71.cos_ref) | copy-start | bytes 786436
  143.0 0.8 copy-start.1
  143.0 1.6 copy-start.2
  615.0 4.8 copy-start.3
  615.1 160.1 %all-to-all-start.1 = ((bf16[8,64,3072]{2,1,0:T(8,128)(2,1)}), bf16[8,64,3072]{2,1,0:T(8,128)(2,1)}, u32[]{:S(2)}, u32[]{:S(2)}) async-start(bf16[8,64,3072]{2,1,0:T(8,128)(2,1)} %get-tuple-element.50), calls=%async_computation.1 | async-start | bytes 6291456 | tf_op jit(solution)/shard_map/all_to_all | solution.py:1116
  768.8 5.8 copy-start.12
  777.8 4.7 copy-start.9
  779.4 4.1 copy-start.6

commit v5 on v4

--- a/solution.py
+++ b/solution.py
@@ -236,7 +236,7 @@
 
     def first(self):
         p = self.p
-        src = self.own.at[self.rows]
+        src = None if self.own is None else self.own.at[self.rows]
 
         @pl.when(p.high)
         def _():
@@ -247,7 +247,8 @@
             self.copy(1, p.c, p.c - 2, src).start()
 
         self.copy(2, p.c, p.sib, src).start()
-        pltpu.make_async_copy(src, self.slot(p.c), self.ls).start()
+        if src is not None:
+            pltpu.make_async_copy(src, self.slot(p.c), self.ls).start()
 
     def step(self, t):
         p = self.p
@@ -274,11 +275,14 @@
 
             self.copy(2, k, p.sib).start()
 
-    def finish(self):
+    def arrived(self, k):
+        self.copy(2, k, self.p.sib).wait_recv()
+
+    def finish(self, arrived=False):
         p = self.p
-        src = self.own.at[self.rows]
-        for y in range(p.nz):
-            self.copy(2, 2 * y + 1 - p.j, p.sib).wait_recv()
+        if not arrived:
+            for y in range(p.nz):
+                self.arrived(2 * y + 1 - p.j)
         for y in range(p.nz):
             k = 2 * y + p.j
             self.copy(2, k, p.sib).wait_send()
@@ -291,7 +295,8 @@
             def _(k=k):
                 self.copy(1, k, p.c - 2).wait_send()
 
-        pltpu.make_async_copy(src, self.slot(p.c), self.ls).wait()
+        if self.own is not None:
+            pltpu.make_async_copy(self.own.at[self.rows], self.slot(p.c), self.ls).wait()
 
     def all_steps(self):
         return [self.first] + [functools.partial(self.step, t) for t in range(1, self.p.nz)]
@@ -301,21 +306,25 @@
     def __init__(self, p, a, x, ud, T, sems, part=None, make=None, stage=None):
         self.p, self.a, self.x, self.ud, self.T, self.sems = p, a, x, ud, T, sems
         self.part, self.make, self.stage = part, make, stage
+        self.size = T // CUTS
 
     def cross(self, y, slot=0):
         p = self.p
         src = self.part.at[2 * y + 1 - p.j] if self.part is not None else self.stage.at[slot]
-        return remote(src, self.x.at[y], self.sems.at[0, y], self.sems.at[1, y], "ctx", p.sib)
+        return remote(src, self.x.at[y], self.sems.at[0, y, 0], self.sems.at[1, y, 0], "ctx", p.sib)
 
     def load(self, y):
-        return pltpu.make_async_copy(self.part.at[2 * y + self.p.j], self.a.at[y], self.sems.at[2, y])
-
-    def go_up(self, y):
-        return remote(self.a.at[y], self.ud.at[y], self.sems.at[3, y], self.sems.at[4, y], "ctx", self.p.c + 2)
-
-    def go_down(self, y, last=False):
-        to = self.p.nz if last else y
-        return remote(self.a.at[y], self.ud.at[to], self.sems.at[5, y], self.sems.at[6, y], "ctx", self.p.c - 2)
+        return pltpu.make_async_copy(self.part.at[2 * y + self.p.j], self.a.at[y], self.sems.at[2, y, 0])
+
+    def go_up(self, y, h):
+        at = pl.ds(h * self.size, self.size)
+        ss, rs = self.sems.at[3, y, h], self.sems.at[4, y, h]
+        return remote(self.a.at[y, at], self.ud.at[y, at], ss, rs, "ctx", self.p.c + 2)
+
+    def go_down(self, y, h, last=False):
+        at = pl.ds(h * self.size, self.size)
+        ss, rs = self.sems.at[5, y, h], self.sems.at[6, y, h]
+        return remote(self.a.at[y, at], self.ud.at[self.p.nz if last else y, at], ss, rs, "ctx", self.p.c - 2)
 
     def begin(self, cross=True, load=True):
         nz = self.p.nz
@@ -333,7 +342,7 @@
         upper = p.z // (p.nz // 2)
         return upper * i + (1 - upper) * (p.nz - 1 - i)
 
-    def compute(self, between=None):
+    def compute(self):
         p = self.p
         for i in range(p.nz):
             y, slot = self.turn(i), i % 2
@@ -342,33 +351,32 @@
             self.make(2 * y + 1 - p.j, self.stage.at[slot])
             self.cross(y, slot).start()
             self.make(2 * y + p.j, self.a.at[y])
-            if i > 0:
-                pl.when(p.z == 0)(functools.partial(self.edge, self.turn(i - 1), True, False))
-                pl.when(p.z == p.nz - 1)(functools.partial(self.edge, self.turn(i - 1), False, i == p.nz - 1))
-            if between is not None:
-                between(i)
+            if i < p.nz - 1:
+                pl.when(p.z == 0)(functools.partial(self.edge, y, True, False))
+                pl.when(p.z == p.nz - 1)(functools.partial(self.edge, y, False, i == p.nz - 2))
 
     def edge(self, y, up, last):
         self.ready(y)
-        self.add(y, None)
-        if up:
-            self.go_up(y).start()
-        else:
-            self.go_down(y, last).start()
+        for h in range(CUTS):
+            self.add(y, h, None)
+            if up:
+                self.go_up(y, h).start()
+            else:
+                self.go_down(y, h, last).start()
 
     def ready(self, y):
         if self.part is not None:
             self.load(y).wait()
         self.cross(y).wait_recv()
 
-    def add(self, y, extra):
+    def add(self, y, h, extra):
         def fn(r):
             v = self.a[y, r].astype(f32) + self.x[y, r].astype(f32)
             if extra is not None:
                 v = v + extra[y, r].astype(f32)
             self.a[y, r] = v.astype(bf16)
 
-        each(fn, 0, self.T)
+        each(fn, h * self.size, self.size)
 
     def edges(self):
         p = self.p
@@ -383,22 +391,24 @@
             for y in range(p.nz - 1):
                 self.edge(y, False, y == p.nz - 2)
 
-    def step(self, t):
+    def step(self, t, h):
         p = self.p
 
         def upward():
             y = p.nz - 1 - t + p.z
-            self.ready(y)
-            self.go_up(y).wait_recv()
-            self.add(y, self.ud)
-            self.go_up(y).start()
+            if h == 0:
+                self.ready(y)
+            self.go_up(y, h).wait_recv()
+            self.add(y, h, self.ud)
+            self.go_up(y, h).start()
 
         def downward():
             y = t - (p.nz - 1 - p.z)
-            self.ready(y)
-            self.go_down(y).wait_recv()
-            self.add(y, self.ud)
-            self.go_down(y, t == p.nz - 2).start()
+            if h == 0:
+                self.ready(y)
+            self.go_down(y, h).wait_recv()
+            self.add(y, h, self.ud)
+            self.go_down(y, h, t == p.nz - 2).start()
 
         half = p.nz // 2
         goes_up = p.low & p.high & (p.z <= t)
@@ -407,27 +417,30 @@
         pl.when(goes_down)(downward)
         pl.when(goes_up & (p.z >= half))(upward)
 
-    def total(self, fn):
+    def total(self, fn, after=None):
         p = self.p
         z = p.z
         self.ready(z)
-        pl.when(p.low)(lambda: self.go_up(z).wait_recv())
-        pl.when(p.high)(lambda: self.go_down(z, True).wait_recv())
-
-        def run(low, high):
-            def body(r):
-                v = self.a[z, r].astype(f32) + self.x[z, r].astype(f32)
-                if low:
-                    v = v + self.ud[z, r].astype(f32)
-                if high:
-                    v = v + self.ud[p.nz, r].astype(f32)
-                fn(r, v)
-
-            each(body, 0, self.T)
-
-        pl.when(p.low & p.high)(lambda: run(True, True))
-        pl.when(p.z == 0)(lambda: run(False, p.nz > 1))
-        pl.when(p.z == p.nz - 1)(lambda: run(True, False))
+        for h in range(CUTS):
+            pl.when(p.low)(lambda: self.go_up(z, h).wait_recv())
+            pl.when(p.high)(lambda: self.go_down(z, h, True).wait_recv())
+
+            def run(low, high):
+                def body(r):
+                    v = self.a[z, r].astype(f32) + self.x[z, r].astype(f32)
+                    if low:
+                        v = v + self.ud[z, r].astype(f32)
+                    if high:
+                        v = v + self.ud[p.nz, r].astype(f32)
+                    fn(r, v)
+
+                each(body, h * self.size, self.size)
+
+            pl.when(p.low & p.high)(lambda: run(True, True))
+            pl.when(p.z == 0)(lambda: run(False, p.nz > 1))
+            pl.when(p.z == p.nz - 1)(lambda: run(True, False))
+            if after is not None:
+                after(h)
 
     def finish(self, staged=True):
         p = self.p
@@ -437,26 +450,50 @@
 
             @pl.when(p.z < y)
             def _(y=y):
-                self.go_up(y).wait_send()
+                for h in range(CUTS):
+                    self.go_up(y, h).wait_send()
 
             @pl.when(p.z > y)
             def _(y=y):
-                self.go_down(y).wait_send()
+                for h in range(CUTS):
+                    self.go_down(y, h).wait_send()
 
         if self.part is None and staged:
-            for i in range(max(p.nz - 2, 0), p.nz):
-                self.cross(self.turn(i), i % 2).wait_send()
+            self.sent()
+
+    def sent(self):
+        for i in range(max(self.p.nz - 2, 0), self.p.nz):
+            self.cross(self.turn(i), i % 2).wait_send()
 
     def all_steps(self):
-        return [functools.partial(self.step, i) for i in range(1, self.p.nz - 1)]
-
-
-def strips(fn, width, step):
-    def body(i, _):
-        fn(pl.ds(pl.multiple_of(i * step, step), step))
-        return 0
-
-    lax.fori_loop(0, width // step, body, 0)
+        return [functools.partial(self.step, i, h) for i in range(1, self.p.nz - 1) for h in range(CUTS)]
+
+
+class Gathers:
+    def __init__(self, p, own, full, T, ss, rs, ls):
+        n = T // CUTS
+        self.all = [Gather(p, own, full, pl.ds(h * n, n), ss.at[h], rs.at[h], ls.at[h]) for h in range(CUTS)]
+
+    def first(self, h):
+        self.all[h].first()
+
+    def step(self, t):
+        for g in self.all:
+            g.step(t)
+
+    def all_steps(self):
+        return [functools.partial(g.step, t) for t in range(1, self.all[0].p.nz) for g in self.all]
+
+    def arrived(self, k):
+        for g in self.all:
+            g.arrived(k)
+
+    def finish(self, arrived=False):
+        for g in self.all:
+            g.finish(arrived)
+
+
+CUTS = 2
 
 
 def interleave(first, second):
@@ -467,6 +504,22 @@
             second[i]()
 
 
+def strips(fn, width, step):
+    def body(i, _):
+        fn(pl.ds(pl.multiple_of(i * step, step), step))
+        return 0
+
+    lax.fori_loop(0, width // step, body, 0)
+
+
+def interleave(first, second):
+    for i in range(max(len(first), len(second))):
+        if i < len(first):
+            first[i]()
+        if i < len(second):
+            second[i]()
+
+
 class Peers:
     def __init__(self, p, pick, ss, rs, keep, ls):
         self.p, self.pick, self.ss, self.rs, self.keep, self.ls = p, pick, ss, rs, keep, ls
@@ -497,6 +550,10 @@
     return [DMA((3, nc)), DMA((nc,)), DMA]
 
 
+def gathers_sems(nc):
+    return [DMA((CUTS, 3, nc)), DMA((CUTS, nc)), DMA((CUTS,))]
+
+
 def scatter_scratch(nz, T, E):
     return [pltpu.VMEM((nz, T, E), bf16)] * 2 + [pltpu.VMEM((nz + 1, T, E), bf16)]
 
@@ -509,11 +566,26 @@
 VM = pl.BlockSpec(memory_space=pltpu.VMEM)
 
 
-def open_kernel(nc, nf, tok, ids, wl, row, ids_row, w, gss, grs, gls, iss, irs, ils, ass, ars, fss, frs, als):
+def open_kernel(
+    nc, nf, tok, ids, gains, wq, wk, wv, wo, wg, wu, wd, row, ids_row, w, wm,
+    qv, kv, vv, ov, gv, bigv, wl, wmv, lsem, msem,
+    gss, grs, gls, iss, irs, ils, ass, ars, fss, frs, als,
+):
     p = Place(nc, nf)
+    T = tok.shape[0]
+    R, QW = wq.shape[0], wq.shape[1] // nc
+    F = wg.shape[1] // nc
+    rep = nc * HD // wk.shape[1]
+    small = [
+        pltpu.make_async_copy(src, dst, lsem.at[i])
+        for i, (src, dst) in enumerate(((wq, qv), (wk, kv), (wv, vv), (wo, ov), (gains, gv)))
+    ]
+    large = [pltpu.make_async_copy(src, bigv.at[i], lsem.at[5 + i]) for i, src in enumerate((wg, wu, wd))]
+    for cp in small + large:
+        cp.start()
     greet(p, ctx=True, fsdp=True)
-    T = tok.shape[0]
     g = Gather(p, tok, row, pl.ds(0, T), gss, grs, gls)
+    g.first()
 
     def id_copy(k):
         to = lax.rem(p.c + k, nc)
@@ -530,6 +602,15 @@
     def source(k):
         return lax.rem(p.c + nc - k, nc)
 
+    for cp in small:
+        cp.wait()
+    for c in range(nc):
+        h = c // rep
+        at = 0
+        for src, i, width in ((qv, c, QW), (kv, h, HD), (vv, h, HD), (ov, c, QW)):
+            wl[c, :, pl.ds(at, width)] = src[:, i * width : (i + 1) * width].astype(bf16)
+            at += width
+        wl[c, :, pl.ds(at, 128)] = gv[...]
     keep_ids = pltpu.make_async_copy(ids, ids_row.at[p.c], ils)
     keep_w = pltpu.make_async_copy(wl.at[p.c], w.at[p.c, p.f], als)
     keep_w.start()
@@ -537,7 +618,6 @@
     for k in range(1, nc):
         block(k).start()
         id_copy(k).start()
-    g.first()
     keep_w.wait()
 
     def spread(k):
@@ -545,6 +625,16 @@
             onward(source(k), k, m).start()
 
     spread(0)
+    for i, cp in enumerate(large):
+        cp.wait()
+
+        def cast(c, _, i=i):
+            wmv[c, :, pl.ds(i * F, F)] = bigv[i, :, pl.ds(pl.multiple_of(c * F, F), F)].astype(bf16)
+            return 0
+
+        lax.fori_loop(0, nc, cast, 0)
+    keep_m = pltpu.make_async_copy(wmv, wm, msem)
+    keep_m.start()
     for k in range(1, nc):
         block(k).wait_recv()
         spread(k)
@@ -552,6 +642,7 @@
         g.step(t)
     g.finish()
     keep_ids.wait()
+    keep_m.wait()
     for k in range(1, nc):
         block(k).wait_send()
         id_copy(k).wait()
@@ -560,32 +651,71 @@
             onward(source(k), k, m).wait()
 
 
-def open_call(nc, nf, tok, ids, wl):
+def open_call(nc, nf, tok, ids, gains, wq, wk, wv, wo, wg, wu, wd):
     T, E = tok.shape
-    _, R, A = wl.shape
+    R = wq.shape[0]
+    A = 2 * wq.shape[1] // nc + 2 * HD + 128
+    M = 3 * wg.shape[1] // nc
+    VMEM = pltpu.VMEM
     return pl.pallas_call(
         functools.partial(open_kernel, nc, nf),
-        in_specs=[ANY, ANY, ANY],
-        out_specs=[ANY, ANY, ANY],
+        in_specs=[ANY] * 10,
+        out_specs=[ANY] * 4,
         out_shape=[
             jax.ShapeDtypeStruct((nc, T, E), bf16),
             jax.ShapeDtypeStruct((nc,) + ids.shape, jnp.int32),
             jax.ShapeDtypeStruct((nc, nf, R, A), bf16),
+            jax.ShapeDtypeStruct((nc, R, M), bf16),
         ],
-        scratch_shapes=gather_sems(nc)
+        scratch_shapes=[VMEM(v.shape, f32) for v in (wq, wk, wv, wo)]
+        + [VMEM((R, 128), bf16), VMEM((3,) + wg.shape, f32), VMEM((nc, R, A), bf16), VMEM((nc, R, M), bf16)]
+        + [DMA((8,)), DMA]
+        + gather_sems(nc)
         + [DMA((nc,)), DMA((nc,)), DMA, DMA((nc,)), DMA((nc,)), DMA((nc, nf)), DMA((nc, nf)), DMA],
         compiler_params=params(1),
         name="open_row",
-    )(tok, ids, wl)
-
-
-def middle_kernel(
-    nc, nf, oT, wo, tok, og, g, wl, hid, n2, dm, w,
-    a, x, ud, stage, oblk, own, dmo, rsem, nss, nrs, nls, dss, drs, dls, fss, frs, fls,
-):
+    )(tok, ids, gains, wq, wk, wv, wo, wg, wu, wd)
+
+
+def finish_kernel(F, QW, gm, ga, gg, gu, gd, gq, go):
+    gg[...] = gm[0, :, pl.ds(0, F)].astype(f32)
+    gu[...] = gm[0, :, pl.ds(F, F)].astype(f32)
+    gd[...] = gm[0, :, pl.ds(2 * F, F)].astype(f32)
+    gq[...] = ga[0, :, pl.ds(0, QW)].astype(f32)
+    go[...] = ga[0, :, pl.ds(QW + 2 * HD, QW)].astype(f32)
+
+
+def finish_call(gm, ga):
+    nc, R, M = gm.shape
+    A = ga.shape[2]
+    F, QW = M // 3, (A - 2 * HD) // 2
+    out = lambda n: pl.BlockSpec((R, n), lambda c: (0, c))
+    widths = (F, F, F, QW, QW)
+    return pl.pallas_call(
+        functools.partial(finish_kernel, F, QW),
+        grid=(nc,),
+        in_specs=[pl.BlockSpec((1, R, M), lambda c: (c, 0, 0)), pl.BlockSpec((1, R, A), lambda c: (c, 0, 0))],
+        out_specs=[out(n) for n in widths],
+        out_shape=[jax.ShapeDtypeStruct((R, nc * n), f32) for n in widths],
+        name="finish_rows",
+    )(gm, ga)
+
+
+def middle_kernel(nc, nf, fold, *refs):
+    it = iter(refs)
+    take = lambda n: [next(it) for _ in range(n)]
+    oT, wo, tok, og, g, wl = take(6)
+    hid, n2, dm, w = take(4)
+    outs = take(3) if fold else None
+    a, x, ud, stage, oblk, own, dmo, rsem = take(8)
+    nss, nrs, nls, dss, drs, dls, fss, frs, fls = take(9)
     p = Place(nc, nf)
     greet(p, fsdp=True)
     T, E = tok.shape
+    M = wl.shape[2]
+    F, F2 = M // 3, 2 * M // 3
+    R = wl.shape[1]
+    S = nc * T
 
     def make(d, ref):
         oblk[...] = oT[:, pl.ds(pl.multiple_of(d * T, T), T)].T
@@ -596,57 +726,169 @@
         strips(fn, E, 512)
 
     rs = Scatter(p, a, x, ud, T, rsem, make=make, stage=stage)
-    ag = Gather(p, own, n2, pl.ds(0, T), nss, nrs, nls)
-    dmg = Gather(p, dmo, dm, pl.ds(0, T), dss, drs, dls)
-    peers = Peers(p, lambda to: (wl, w.at[:, p.f]), fss, frs, (wl, w.at[:, p.f]), fls)
-    peers.start()
+    dmg = Gathers(p, dmo, dm, T, dss, drs, dls)
+    if fold:
+        n2v, wguv, wdv, dact, dmb, out, osem, dsem, csem, wsem = take(10)
+        ag = Gathers(p, None, n2v, T, nss, nrs, nls)
+        low, high = wl.at[:, :, pl.ds(0, F2)], wl.at[:, :, pl.ds(F2, F)]
+        last = Peers(p, lambda to: (high, wdv.at[:, p.f]), fss.at[0], frs.at[0], (high, wdv.at[:, p.f]), fls.at[0])
+        firsts = Peers(p, lambda to: (low, wguv.at[:, p.f]), fss.at[1], frs.at[1], (low, wguv.at[:, p.f]), fls.at[1])
+        last.start()
+        firsts.start()
+        saves = [
+            pltpu.make_async_copy(wdv, w.at[:, :, :, pl.ds(F2, F)], wsem.at[0]),
+            pltpu.make_async_copy(wguv, w.at[:, :, :, pl.ds(0, F2)], wsem.at[1]),
+        ]
+    else:
+        ag = Gathers(p, own, n2, T, nss, nrs, nls)
+        every = Peers(p, lambda to: (wl, w.at[:, p.f]), fss.at[0], frs.at[0], (wl, w.at[:, p.f]), fls.at[0])
+        every.start()
 
     def dm_rows(r):
         dmo[r] = (RES * og[r].astype(f32)).astype(bf16)
 
     each(dm_rows, 0, T)
-    dmg.first()
+    for h in range(CUTS):
+        dmg.first(h)
     rs.compute()
 
     def rows(r, v):
         h = tok[r].astype(f32) + RES * v
         hid[r] = h
-        own[r] = (h * lax.rsqrt(jnp.mean(h * h, axis=-1, keepdims=True) + EPS) * g[...]).astype(bf16)
-
-    interleave(dmg.all_steps()[1:], rs.all_steps())
-    rs.total(rows)
-    ag.first()
-    for s in ag.all_steps()[1:]:
+        v = (h * lax.rsqrt(jnp.mean(h * h, axis=-1, keepdims=True) + EPS) * g[...]).astype(bf16)
+        if fold:
+            n2v[p.c, r] = v
+        else:
+            own[r] = v
+
+    interleave(dmg.all_steps(), rs.all_steps())
+    rs.total(rows, ag.first)
+    dmg.finish()
+    steps = [functools.partial(ag.step, t) for t in range(1, p.nz)]
+    if not fold:
+        for s in steps:
+            s()
+        ag.finish()
+        rs.finish()
+        every.wait()
+        return
+
+    def dm_load(k, slot):
+        return pltpu.make_async_copy(dm.at[k], dmb.at[slot], dsem.at[slot])
+
+    def back(k, _):
+        slot = k % 2
+
+        @pl.when(k + 1 < nc)
+        def _():
+            dm_load(k + 1, 1 - slot).start()
+
+        dm_load(k, slot).wait()
+
+        def fn(at):
+            v = jnp.dot(dmb[slot], wdv[:, :, :, at].reshape(E, -1), preferred_element_type=f32)
+            dact[pl.ds(pl.multiple_of(k * T, T), T), at] = v
+
+        strips(fn, F, min(512, F))
+        return 0
+
+    dm_load(0, 0).start()
+    last.wait()
+    saves[0].start()
+    lax.fori_loop(0, nc, back, 0)
+
+    def results(k, slot):
+        rows_ = pl.ds(pl.multiple_of(k * T, T), T)
+        return [pltpu.make_async_copy(out.at[slot, i], outs[i].at[rows_], osem.at[slot, i]) for i in range(3)]
+
+    def block(q, _):
+        dist, sign, slot = q // 4, (q // 2) % 2, q % 2
+        y = p.z + (2 * sign - 1) * dist
+
+        @pl.when((y >= 0) & (y < nc // 2) & (dist + 1 - sign > 0))
+        def _():
+            k = 2 * y + p.j + slot * (1 - 2 * p.j)
+            pl.when(slot == 1)(lambda: ag.arrived(k))
+            pltpu.make_async_copy(n2v.at[k], n2.at[k], csem.at[k]).start()
+
+            @pl.when(dist > 0)
+            def _():
+                for cp in results(k, slot):
+                    cp.wait()
+
+            def fn(at):
+                up_at = pl.ds(pl.multiple_of(at.start + F, 128), at.size)
+                gate = jnp.dot(n2v[k], wguv[:, :, :, at].reshape(E, -1), preferred_element_type=f32)
+                up = jnp.dot(n2v[k], wguv[:, :, :, up_at].reshape(E, -1), preferred_element_type=f32)
+                d = dact[pl.ds(pl.multiple_of(k * T, T), T), at]
+                sg = 1.0 / (1.0 + jnp.exp(-gate))
+                silu = gate * sg
+                out[slot, 0, :, at] = (d * up * sg * (1.0 + gate * (1.0 - sg))).astype(bf16)
+                out[slot, 1, :, at] = (d * silu).astype(bf16)
+                out[slot, 2, :, at] = (silu * up).astype(bf16)
+
+            strips(fn, F, min(STRIP, F))
+            for cp in results(k, slot):
+                cp.start()
+
+        return 0
+
+    nz = nc // 2
+    for t, s in enumerate(steps, 1):
         s()
-    ag.finish()
+        if t == 2:
+            firsts.wait()
+            saves[1].start()
+            lax.fori_loop(0, 8, block, 0)
+    lax.fori_loop(8, 4 * nz, block, 0)
+    ag.finish(True)
     rs.finish()
-    dmg.finish()
-    peers.wait()
-
-
-def middle_call(nc, nf, oT, wo, tok, og, g, wl):
+    for slot in range(2):
+        for cp in results(0, slot):
+            cp.wait()
+    for cp in saves:
+        cp.wait()
+    for k in range(nc):
+        pltpu.make_async_copy(n2v.at[k], n2.at[k], csem.at[k]).wait()
+
+
+STRIP = 512
+
+
+def middle_call(nc, nf, fold, oT, wo, tok, og, g, wl):
     T, E = tok.shape
     _, R, M = wl.shape
     nz = nc // 2
+    F, S = M // 3, nc * T
+    VMEM = pltpu.VMEM
     return pl.pallas_call(
-        functools.partial(middle_kernel, nc, nf),
+        functools.partial(middle_kernel, nc, nf, fold),
         in_specs=[VM, VM, VM, VM, VM, ANY],
-        out_specs=[VM, ANY, ANY, ANY],
+        out_specs=[VM, ANY, ANY, ANY] + [ANY] * 3 * fold,
         out_shape=[
             jax.ShapeDtypeStruct((T, E), f32),
             jax.ShapeDtypeStruct((nc, T, E), bf16),
             jax.ShapeDtypeStruct((nc, T, E), bf16),
             jax.ShapeDtypeStruct((nc, nf, R, M), bf16),
-        ],
+        ]
+        + [jax.ShapeDtypeStruct((S, F), bf16)] * 3 * fold,
         scratch_shapes=scatter_scratch(nz, T, E)
-        + [pltpu.VMEM((2, T, E), bf16), pltpu.VMEM((T, oT.shape[0]), bf16)]
-        + [pltpu.VMEM((T, E), bf16), pltpu.VMEM((T, E), bf16), DMA((7, nz))]
-        + gather_sems(nc)
-        + gather_sems(nc)
-        + [DMA((nf,)), DMA((nf,)), DMA],
+        + [VMEM((2, T, E), bf16), VMEM((T, oT.shape[0]), bf16)]
+        + [VMEM((8, 128) if fold else (T, E), bf16), VMEM((T, E), bf16), DMA((7, nz, CUTS))]
+        + gathers_sems(nc)
+        + gathers_sems(nc)
+        + [DMA((2, nf)), DMA((2, nf)), DMA((2,))]
+        + [
+            VMEM((nc, T, E), bf16), VMEM((nc, nf, R, 2 * F), bf16), VMEM((nc, nf, R, F), bf16), VMEM((S, F), f32),
+            VMEM((2, T, E), bf16), VMEM((2, 3, T, F), bf16), DMA((2, 3)), DMA((2,)), DMA((nc,)), DMA((2,)),
+        ]
+        * fold,
         compiler_params=params(2),
         name="attn_to_mlp",
     )(oT, wo, tok, og, g, wl)
+
+
+EARLY, MLP_LATE = 8, True
 
 
 def turn_kernel(nc, nf, fold, *refs):
@@ -688,7 +930,7 @@
         strips(fn, E, 512)
 
     rs = Scatter(p, a, x, ud, T, rsem, make=make, stage=mp)
-    ag = Gather(p, own, da, pl.ds(0, T), nss, nrs, nls)
+    ag = Gathers(p, own, da, T, nss, nrs, nls)
     if fold:
         x2, ud2, wdv, msem, psem = take(5)
         ms = Scatter(p, a, x2, ud2, T, msem, part=mpart)
@@ -808,19 +1050,21 @@
     for cp in big[3:]:
         cp.wait()
     steps = rs.all_steps()
-    bounds = [nc * i // (len(steps) + 1) for i in range(len(steps) + 2)]
+    early = EARLY * nc // 8 if fold else nc
+    bounds = [early * i // (len(steps) + 1) for i in range(len(steps) + 2)]
     for i in range(len(steps) + 1):
         lax.fori_loop(bounds[i], bounds[i + 1], grads, 0)
         if i < len(steps):
             steps[i]()
-    send(nc - 1)
     if fold:
-        for i in range(max(nz - 2, 0), nz):
-            rs.cross(rs.turn(i), i % 2).wait_send()
-        lax.fori_loop(0, nc, mlp, 0)
-        for slot in range(2):
-            pltpu.make_async_copy(mp.at[slot], mpart.at[slot], psem.at[slot]).wait()
-        ms.begin(load=False)
+        rs.sent()
+
+    def mlp_terms():
+        if fold:
+            lax.fori_loop(0, nc, mlp, 0)
+            for slot in range(2):
+                pltpu.make_async_copy(mp.at[slot], mpart.at[slot], psem.at[slot]).wait()
+            ms.begin(load=False)
 
     def rows(r, dn):
         h = hid[r]
@@ -832,22 +1076,31 @@
         own[r] = (RES * v).astype(bf16)
         gg[...] += jnp.sum((xn * dn).reshape(CH // 8, 8, E), axis=0)
 
-    rs.total(rows)
-    ag.first()
+    if not MLP_LATE:
+        mlp_terms()
+    rs.total(rows, ag.first)
+    if MLP_LATE:
+        mlp_terms()
     rs.finish(not fold)
     if fold:
         ms.begin(cross=False)
         ms.edges()
-    sums(0, nc // 4)
     more = ms.all_steps() if fold else []
-    done = nc // 4
-    for i, s in enumerate(ag.all_steps()[1:]):
+    made, done = early, 0
+    late = ag.all_steps()
+    for i, s in enumerate(late):
+        upto = min(nc, made + max(1, nc // 8))
+        lax.fori_loop(made, upto, grads, 0)
+        if made < nc and upto == nc:
+            send(nc - 1)
+        made = upto
         s()
         if i < len(more):
             more[i]()
-        upto = min(nc - 1, done + max(1, nc // 4))
-        sums(done, upto)
-        done = upto
+    if early == nc:
+        send(nc - 1)
+    sums(0, nc // 2)
+    done = nc // 2
     if fold:
 
         def out(r, v):
@@ -883,12 +1136,12 @@
         ]
         + [jax.ShapeDtypeStruct((nc, T, E), bf16)] * fold,
         scratch_shapes=scatter_scratch(nz, T, E)
-        + [VMEM((T, E), bf16), DMA((7, nz))]
-        + gather_sems(nc)
+        + [VMEM((T, E), bf16), DMA((7, nz, CUTS))]
+        + gathers_sems(nc)
         + [DMA((nf, nc)), DMA((nf, nc)), DMA((2, nf))]
         + [VMEM((S, F2), bf16), VMEM((S, F), bf16), VMEM((max(E, S), max(F2, 4 * B)), bf16)]
         + [VMEM((B, S), bf16), VMEM((2, B, M), bf16), VMEM((2, T, E), bf16), DMA((9,)), DMA((2,))]
-        + [VMEM((nz, T, E), bf16), VMEM((nz + 1, T, E), bf16), VMEM((E, F), bf16), DMA((7, nz)), DMA((2,))] * fold,
+        + [VMEM((nz, T, E), bf16), VMEM((nz + 1, T, E), bf16), VMEM((E, F), bf16), DMA((7, nz, CUTS)), DMA((2,))] * fold,
         compiler_params=params(3),
         name="mlp_to_attn",
     )(n2, dm, dga, dup, act, wm, hid, og, g)
@@ -1059,7 +1312,7 @@
             VMEM((nf, E // 128, 8, 128), f32),
             VMEM((E // 128, 8, 128), f32),
             VMEM((nc, 8, 128), f32),
-            DMA((7, nz)),
+            DMA((7, nz, CUTS)),
             DMA((5,)),
         ]
         + [DMA((nf,)), DMA((nf,)), DMA, DMA((nc,)), DMA((nc,)), DMA]
@@ -1103,29 +1356,18 @@
     KO, VO, OO, GO = QW, QW + HD, QW + 2 * HD, 2 * QW + 2 * HD
     tok, og = tokens[0], out_grad[0]
 
-    def cols(w):
-        return w.astype(bf16).reshape(R, nc, -1)
-
-    def kv_cols(w):
-        return jnp.repeat(w.astype(bf16).reshape(R, KEY_VALUE_HEADS, HD), rep, axis=1)
-
-    def blocks(parts):
-        return jnp.transpose(jnp.concatenate(parts, axis=2), (1, 0, 2))
-
     def exchange(w):
         return lax.all_to_all(w, "ctx", 0, 0, tiled=True)
 
-    gains = jnp.stack([gain_attn, gain_mlp], axis=1).astype(bf16)
-    gains = jnp.broadcast_to(jnp.pad(gains, ((0, 0), (0, 126)))[:, None], (R, nc, 128))
-    wl = blocks([cols(w_query), kv_cols(w_key), kv_cols(w_value), cols(w_out), gains])
+
+    gains = jnp.pad(jnp.stack([gain_attn, gain_mlp], axis=1).astype(bf16), ((0, 0), (0, 126)))
     ids = jnp.pad(jnp.concatenate([seq_ids, positions, block_ids], axis=0), ((0, 5), (0, 0)))
-    row_tok, ids, wa = open_call(nc, nf, tok, ids, wl)
+    row_tok, ids, wa, wm = open_call(
+        nc, nf, tok, ids, gains, w_query, w_key, w_value, w_out, w_gate, w_up, w_down
+    )
+    wm = exchange(wm)
     wa = wa.reshape(E, -1)
     g_attn, g_mlp = wa[:, GO].astype(f32)[None], wa[:, GO + 1].astype(f32)[None]
-
-    wm = blocks([cols(w_gate), cols(w_up), cols(w_down)])
-    row_tok, wm = lax.optimization_barrier((row_tok, wm))
-    wm = exchange(wm)
 
     seq, pos, blk = (ids[:, i].reshape(S) for i in range(3))
     place = jnp.arange(S, dtype=jnp.int32)
@@ -1147,16 +1389,21 @@
     k, v = kT.T, vT.T
     oT, oTb, lse = attn_fwd(qT, k, vT, st, en)
 
-    hidden, n2, dm, wm = middle_call(nc, nf, oTb, w_o, tok, og, g_mlp, wm)
-    n2, dm, wm = n2.reshape(S, E), dm.reshape(S, E), wm.reshape(E, -1)
-    w_gu, w_d = wm[:, : 2 * FFL], wm[:, 2 * FFL :]
-    gu = dg(n2, w_gu, 1, 0)
-    gate, up = gu[:, :FFL], gu[:, FFL:]
-    sg = jax.nn.sigmoid(gate)
-    act = (gate * sg * up).astype(bf16)
-    d_act = dg(dm, w_d, 1, 0)
-    d_gate = (d_act * up * sg * (1.0 + gate * (1.0 - sg))).astype(bf16)
-    d_up = (d_act * gate * sg).astype(bf16)
+    middle = (oTb, w_o, tok, og, g_mlp, wm)
+    if nz <= 4:
+        hidden, n2, dm, wm, d_gate, d_up, act = middle_call(nc, nf, True, *middle)
+        n2, dm, wm = n2.reshape(S, E), dm.reshape(S, E), wm.reshape(E, -1)
+    else:
+        hidden, n2, dm, wm = middle_call(nc, nf, False, *middle)
+        n2, dm, wm = n2.reshape(S, E), dm.reshape(S, E), wm.reshape(E, -1)
+        w_d = wm[:, 2 * FFL :]
+        gu = dg(n2, wm[:, : 2 * FFL], 1, 0)
+        gate, up = gu[:, :FFL], gu[:, FFL:]
+        sg = jax.nn.sigmoid(gate)
+        act = (gate * sg * up).astype(bf16)
+        d_act = dg(dm, w_d, 1, 0)
+        d_gate = (d_act * up * sg * (1.0 + gate * (1.0 - sg))).astype(bf16)
+        d_up = (d_act * gate * sg).astype(bf16)
     turn = (n2, dm, d_gate, d_up, act, wm, hidden, og, g_mlp)
     if nz <= 4:
         dh, da, layer_out, ggm, gm = turn_call(nc, nf, True, *turn)[:5]
@@ -1173,25 +1420,21 @@
     at = lax.rem((lax.axis_index("ctx") * nf + lax.axis_index("fsdp")) * R, 128)
     gains = lax.dynamic_slice_in_dim(gains, at, R, 1)
 
-    def rows(g):
-        return jnp.transpose(g.astype(f32), (1, 0, 2)).reshape(R, -1)
-
     def kv_rows(g):
         g = g.astype(f32).reshape(KEY_VALUE_HEADS, rep, R, HD)
         return jnp.transpose(jnp.sum(g, axis=1), (1, 0, 2)).reshape(R, -1)
 
+    grads = finish_call(gm, ga)
     return (
         layer_out[None],
         input_grad[None],
         gains[0],
-        rows(ga[:, :, :KO]),
+        grads[3],
         kv_rows(ga[:, :, KO:VO]),
         kv_rows(ga[:, :, VO:OO]),
-        rows(ga[:, :, OO:]),
+        grads[4],
         gains[1],
-        rows(gm[:, :, :FFL]),
-        rows(gm[:, :, FFL : 2 * FFL]),
-        rows(gm[:, :, 2 * FFL :]),
+        *grads[:3],
     )
 
 

time: 789 us -> 712 us (0.902)
  matrix products: 53.6 us -> 5.89 us
  Pallas kernels: 646 us -> 632 us
  other arithmetic: 35.7 us -> 23.6 us
  local copies, waits for them, and re-layouts: 25.5 us -> 17.2 us
    dot_general x3 -> x1, matrix products: 53.6 us -> 5.89 us  [dg(): lax.dot_general(a, b, (((ca,), (cb,)), ((), ())), preferred_element_type=...]
    pallas_call x1, Pallas kernels: 205 us -> 189 us  [turn_call(): pl.pallas_call(functools.partial(turn_kernel, nc, nf, fold), in_specs=[AN...]
    pallas_call x2 -> x3, Pallas kernels: 271 us -> 286 us  [the longest x1 181 us: middle_call(): pl.pallas_call(functools.partial(middle_kernel, nc, nf, fold), in_specs=[...]
    pallas_call x1, Pallas kernels: 112 us -> 99 us  [close_call(): pl.pallas_call(functools.partial(close_kernel, nc, nf), in_specs=[VM, ANY...]
    reshape x8 -> x0, local copies, waits for them, and re-layouts: 7.99 us -> none  [the longest x5 6.38 us: rows(): return jnp.transpose(g.astype(f32), (1, 0, 2)).reshape(R, -1)]
  transfers between devices with their start and end apart: 2 -> 2, of which waited for: 1 -> 1; matrix products, arithmetic and copies ran while one was open for 5% -> 6% of each run, Pallas kernels for 22% -> 22%
where the time goes in v5:
time: 712 us; the launch traced here: 702 us
  Pallas kernels  632 us (89%)
  other arithmetic  23.6 us (3%)
  local copies, waits for them, and re-layouts  17.2 us (2%)
  waiting for transfers between devices  13 us (2%)
  starting transfers between devices  9.31 us (1%)
    pallas_call x1, Pallas kernels, turn_call(): pl.pallas_call(functools.partial(turn_kernel, nc, nf, fold), in_specs=[AN...  189 us
    pallas_call x1, Pallas kernels, middle_call(): pl.pallas_call(functools.partial(middle_kernel, nc, nf, fold), in_specs=[...  181 us
    pallas_call x1, Pallas kernels, close_call(): pl.pallas_call(functools.partial(close_kernel, nc, nf), in_specs=[VM, ANY...  99 us
    pallas_call x1, Pallas kernels, open_call(): pl.pallas_call(functools.partial(open_kernel, nc, nf), in_specs=[ANY] * 1...  98 us
    pallas_call x1, Pallas kernels, attn_bwd(): pl.pallas_call(functools.partial(attn_bwd_kernel, nh, tq, tk), grid=(S //...  35.8 us
    pallas_call x1, Pallas kernels, attn_fwd(): pl.pallas_call(functools.partial(attn_fwd_kernel, nh, tq, tk), grid=(S //...  22.5 us
  transfers between devices with their start and end apart: 2, of which 1 were waited for; matrix products, arithmetic and copies ran while one was open for 6% of the time, Pallas kernels for 22%

profile of v5, /device:TPU:0, one launch (start us, length us, event | category | flops | bytes accessed | tf_op | source)
XLA Modules:
  0.0 702.1 jit_solution(3512374021267778600)
XLA Ops:
  0.6 0.7 convert_bitcast_fusion.2
  2.1 0.7 pad_add_fusion
  3.4 98.0 %open_row.1 = (bf16[8,256,2048]{2,1,0:T(8,128)(2,1)}, s32[8,8,256]{2,1,0:T(8,128)}, bf16[8,4,64,768]{3,2,1,0:T(8,128)(2,1)}, bf16[8,64,3072]{2,1,0:T(8,128)(2,1)}) custom-call(bf16[256,2048]{1,0:T(8,128)(2,1)} %bitcast.47, s32[8,256]{1,0:T(8,128)} %pad.8.ids, bf16[64,128]{1,0:T(8,128)(2,1)} %pad.9.gains, f32[64,2048]{1,0:T(8,128)} %wq.1, f32[64,512]{1,0:T(8,128)} %wk.1, ...), custom_call_target="tpu_custom_call" | custom-call | tf_op jit(solution)/shard_map/open_row/pallas_call | solution.py:660
  101.4 4.5 all-to-all-start
  105.9 5.2 multiply_reduce_fusion
  111.2 1.0 convert_reduce_fusion
  112.2 8.5 %fusion.1.n1 = bf16[2048,2048]{1,0:T(8,128)(2,1)} fusion(f32[2048]{0:T(1024)S(1)} %get-tuple-element.66, f32[2048]{0:T(1024)S(1)} %bitcast.70, bf16[8,256,2048]{2,1,0:T(8,128)(2,1)} %get-tuple-element.39), kind=kLoop, calls=%fused_computation.2 | loop fusion | flops 16777216 | bytes 16793600 | tf_op jit(solution)/shard_map/convert_element_type | solution.py:1383
  120.7 5.9 fusion.2
  126.8 0.7 slice.84
  128.9 1.0 multiply_cosine_fusion
  130.3 0.8 copy-done.1
  131.1 0.7 pad_maximum_fusion
  131.8 2.0 copy.43.k_ref
  133.8 2.0 copy.49
  135.8 1.9 copy.44.v_ref
  137.7 2.3 fusion.4
  140.6 22.5 %attn_fwd.1 = (f32[256,2048]{1,0:T(8,128)}, bf16[256,2048]{1,0:T(8,128)(2,1)}, f32[4,2048]{1,0:T(4,128)}) custom-call(bf16[256,2048]{1,0:T(8,128)(2,1)} %bitcast.63, bf16[2048,64]{1,0:T(8,128)(2,1)} %copy.43.k_ref, bf16[64,2048]{1,0:T(8,128)(2,1)} %copy.44.v_ref, s32[1,2048]{1,0:T(1,128)} %get-tuple-element.80.st_ref, s32[1,2048]{1,0:T(1,128)} %get-tuple-element.79.en_ref), custom_call_target="tpu_custom_call" | custom-call | flops 2147483648 | bytes 4194304 | tf_op jit(solution)/shard_map/attn_fwd/pallas_call | solution.py:80
  163.0 1.5 slice_bitcast_fusion.2
  164.5 13.0 %all-to-all-done.refs_5_ = bf16[8,64,3072]{2,1,0:T(8,128)(2,1)} async-done(((bf16[8,64,3072]{2,1,0:T(8,128)(2,1)}), bf16[8,64,3072]{2,1,0:T(8,128)(2,1)}, u32[]{:S(2)}, u32[]{:S(2)}) %all-to-all-start) | async-done | bytes 3145760 | tf_op jit(solution)/shard_map/all_to_all | solution.py:1360
  177.4 180.8 %attn_to_mlp.1 = (f32[256,2048]{1,0:T(8,128)}, bf16[8,256,2048]{2,1,0:T(8,128)(2,1)}, bf16[8,256,2048]{2,1,0:T(8,128)(2,1)}, bf16[8,4,64,3072]{3,2,1,0:T(8,128)(...) custom-call(bf16[256,2048]{1,0:T(8,128)(2,1)} %get-tuple-element.41.refs_0_.oT, ...), custom_call_target="tpu_custom_call" | custom-call | tf_op jit(solution)/shard_map/attn_to_mlp/pallas_call | solution.py:864
  358.2 188.8 %mlp_to_attn.1 = (f32[256,2048]{1,0:T(8,128)}, bf16[8,256,2048]{2,1,0:T(8,128)(2,1)}, bf16[256,2048]{1,0:T(8,128)(2,1)}, f32[8,2048]{1,0:T(8,128)}, bf16[8,64,30...) custom-call(bf16[2048,2048]{1,0:T(8,128)(2,1)} %bitcast.56, ...), custom_call_target="tpu_custom_call" | custom-call | tf_op jit(solution)/shard_map/mlp_to_attn/pallas_call | solution.py:1125
  547.1 4.8 all-to-all-start.1
  552.0 1.4 copy.45.wo_ref
  553.4 35.8 %attn_bwd.1.dqkv = bf16[384,2048]{1,0:T(8,128)(2,1)} custom-call(bf16[256,2048]{1,0:T(8,128)(2,1)} %bitcast.64, bf16[2048,2048]{1,0:T(8,128)(2,1)} %bitcast.54, bf16[256,2048]{1,0:T(8,128)(2,1)} %copy.45.wo_ref, f32[256,2048]{1,0:T(8,128)} %get-tuple-element.52.o_ref, f32[4,2048]{1,0:T(4,128)} %get-tuple-element.53.lse_ref, ...), custom_call_target="tpu_custom_call" | custom-call | flops 5368709120 | bytes 5242880 | tf_op jit(solution)/shard_map/attn_bwd/pallas_call | solution.py:150
  589.2 99.0 %close_row.1 = (f32[256,2048]{1,0:T(8,128)}, bf16[8,64,640]{2,1,0:T(8,128)(2,1)}, f32[8,128]{1,0:T(8,128)}) custom-call(bf16[384,2048]{1,0:T(8,128)(2,1)} %attn_bwd.1.dqkv, bf16[2048,768]{1,0:T(8,128)(2,1)} %bitcast.50, bf16[256,2048]{1,0:T(8,128)(2,1)} %get-tuple-element.41.refs_0_.oT, bf16[2048,2048]{1,0:T(8,128)(2,1)} %fusion.1.n1, ...), custom_call_target="tpu_custom_call" | custom-call | tf_op jit(solution)/shard_map/close_row/pallas_call | solution.py:1296
  688.2 1.2 convert_bitcast_fusion
  689.6 0.8 reshape.252
  690.5 0.8 reshape.254
  691.3 0.8 constant_dynamic-slice_fusion
  692.5 6.8 finish_rows.1
  699.3 1.0 copy.53
  700.3 1.3 copy.54
  (35 shorter events, 4.8 us)
Async XLA Ops:
  101.4 76.0 %all-to-all-start = ((bf16[8,64,3072]{2,1,0:T(8,128)(2,1)}), bf16[8,64,3072]{2,1,0:T(8,128)(2,1)}, u32[]{:S(2)}, u32[]{:S(2)}) async-start(bf16[8,64,3072]{2,1,0:T(8,128)(2,1)} %get-tuple-element.42), calls=%async_computation | async-start | bytes 6291456 | tf_op jit(solution)/shard_map/all_to_all | solution.py:1360
  105.9 5.3 copy-start
  112.2 8.5 %copy-start.8 = (f32[2048]{0:T(1024)}, f32[2048]{0:T(1024)S(1)}, u32[]{:S(2)}) copy-start(f32[2048]{0:T(1024)S(1)} %get-tuple-element.66) | copy-start | bytes 24580
  126.6 0.9 copy-start.9
  129.9 2.0 copy-start.6
  129.9 3.9 copy-start.5
  130.3 0.8 copy-start.1
  130.3 1.6 copy-start.2
  547.1 4.9 copy-start.3
  547.1 145.5 %all-to-all-start.1 = ((bf16[8,64,3072]{2,1,0:T(8,128)(2,1)}), bf16[8,64,3072]{2,1,0:T(8,128)(2,1)}, u32[]{:S(2)}, u32[]{:S(2)}) async-start(bf16[8,64,3072]{2,1,0:T(8,128)(2,1)} %get-tuple-element.58), calls=%async_computation.1 | async-start | bytes 6291456 | tf_op jit(solution)/shard_map/all_to_all | solution.py:1360
  688.2 11.1 %copy-start.7 = (bf16[256,2048]{1,0:T(8,128)(2,1)S(1)}, bf16[256,2048]{1,0:T(8,128)(2,1)}, u32[]{:S(2)}) copy-start(bf16[256,2048]{1,0:T(8,128)(2,1)} %get-tuple-element.50) | copy-start | bytes 3145732
  690.5 9.8 %copy-start.4 = (f32[256,2048]{1,0:T(8,128)S(1)}, f32[256,2048]{1,0:T(8,128)}, u32[]{:S(2)}) copy-start(f32[256,2048]{1,0:T(8,128)} %get-tuple-element.56) | copy-start | bytes 6291460

commit v6 on v5

--- a/solution.py
+++ b/solution.py
@@ -344,16 +344,24 @@
 
     def compute(self):
         p = self.p
-        for i in range(p.nz):
+
+        def body(i, _):
             y, slot = self.turn(i), i % 2
-            if i > 1:
+
+            @pl.when(i > 1)
+            def _():
                 self.cross(self.turn(i - 2), slot).wait_send()
+
             self.make(2 * y + 1 - p.j, self.stage.at[slot])
             self.cross(y, slot).start()
             self.make(2 * y + p.j, self.a.at[y])
-            if i < p.nz - 1:
-                pl.when(p.z == 0)(functools.partial(self.edge, y, True, False))
-                pl.when(p.z == p.nz - 1)(functools.partial(self.edge, y, False, i == p.nz - 2))
+            inner = i < p.nz - 1
+            pl.when((p.z == 0) & inner)(functools.partial(self.edge, y, True, False))
+            pl.when((p.z == p.nz - 1) & (i < p.nz - 2))(functools.partial(self.edge, y, False, False))
+            pl.when((p.z == p.nz - 1) & (i == p.nz - 2))(functools.partial(self.edge, y, False, True))
+            return 0
+
+        lax.fori_loop(0, p.nz, body, 0)
 
     def edge(self, y, up, last):
         self.ready(y)
@@ -584,8 +592,9 @@
     for cp in small + large:
         cp.start()
     greet(p, ctx=True, fsdp=True)
-    g = Gather(p, tok, row, pl.ds(0, T), gss, grs, gls)
-    g.first()
+    g = Gathers(p, tok, row, T, gss, grs, gls)
+    for h in range(CUTS):
+        g.first(h)
 
     def id_copy(k):
         to = lax.rem(p.c + k, nc)
@@ -670,33 +679,48 @@
         scratch_shapes=[VMEM(v.shape, f32) for v in (wq, wk, wv, wo)]
         + [VMEM((R, 128), bf16), VMEM((3,) + wg.shape, f32), VMEM((nc, R, A), bf16), VMEM((nc, R, M), bf16)]
         + [DMA((8,)), DMA]
-        + gather_sems(nc)
+        + gathers_sems(nc)
         + [DMA((nc,)), DMA((nc,)), DMA, DMA((nc,)), DMA((nc,)), DMA((nc, nf)), DMA((nc, nf)), DMA],
         compiler_params=params(1),
         name="open_row",
     )(tok, ids, gains, wq, wk, wv, wo, wg, wu, wd)
 
 
-def finish_kernel(F, QW, gm, ga, gg, gu, gd, gq, go):
-    gg[...] = gm[0, :, pl.ds(0, F)].astype(f32)
-    gu[...] = gm[0, :, pl.ds(F, F)].astype(f32)
-    gd[...] = gm[0, :, pl.ds(2 * F, F)].astype(f32)
-    gq[...] = ga[0, :, pl.ds(0, QW)].astype(f32)
-    go[...] = ga[0, :, pl.ds(QW + 2 * HD, QW)].astype(f32)
-
-
-def finish_call(gm, ga):
+def finish_kernel(F, QW, rep, gm, ga, gg, gu, gd, gq, go, gk, gv):
+    each_step = gm.shape[0]
+    for i in range(each_step):
+        for ref, at in ((gg, 0), (gu, F), (gd, 2 * F)):
+            ref[:, i * F : (i + 1) * F] = gm[i, :, pl.ds(at, F)].astype(f32)
+        for ref, at in ((gq, 0), (go, QW + 2 * HD)):
+            ref[:, i * QW : (i + 1) * QW] = ga[i, :, pl.ds(at, QW)].astype(f32)
+    steps = gk.shape[1] * rep // (HD * each_step)
+    for step in range(steps):
+
+        @pl.when(pl.program_id(0) == step)
+        def _(step=step):
+            for i in range(each_step):
+                c = step * each_step + i
+                at = slice((c // rep) * HD, (c // rep + 1) * HD)
+                for ref, lane in ((gk, QW), (gv, QW + HD)):
+                    v = ga[i, :, lane : lane + HD].astype(f32)
+                    ref[:, at] = v if c % rep == 0 else ref[:, at] + v
+
+
+def finish_call(gm, ga, rep):
     nc, R, M = gm.shape
     A = ga.shape[2]
     F, QW = M // 3, (A - 2 * HD) // 2
-    out = lambda n: pl.BlockSpec((R, n), lambda c: (0, c))
+    n = 2
+    out = lambda width: pl.BlockSpec((R, n * width), lambda c: (0, c))
+    whole = pl.BlockSpec((R, nc * HD // rep), lambda c: (0, 0))
     widths = (F, F, F, QW, QW)
     return pl.pallas_call(
-        functools.partial(finish_kernel, F, QW),
-        grid=(nc,),
-        in_specs=[pl.BlockSpec((1, R, M), lambda c: (c, 0, 0)), pl.BlockSpec((1, R, A), lambda c: (c, 0, 0))],
-        out_specs=[out(n) for n in widths],
-        out_shape=[jax.ShapeDtypeStruct((R, nc * n), f32) for n in widths],
+        functools.partial(finish_kernel, F, QW, rep),
+        grid=(nc // n,),
+        in_specs=[pl.BlockSpec((n, R, M), lambda c: (c, 0, 0)), pl.BlockSpec((n, R, A), lambda c: (c, 0, 0))],
+        out_specs=[out(width) for width in widths] + [whole, whole],
+        out_shape=[jax.ShapeDtypeStruct((R, nc * width), f32) for width in widths]
+        + [jax.ShapeDtypeStruct((R, nc * HD // rep), f32)] * 2,
         name="finish_rows",
     )(gm, ga)
 
@@ -935,7 +959,7 @@
         x2, ud2, wdv, msem, psem = take(5)
         ms = Scatter(p, a, x2, ud2, T, msem, part=mpart)
         big.append(fetch(wm.at[:, pl.ds(F2, F)], wdv, 4))
-    for cp in big:
+    for cp in big[:3]:
         cp.start()
 
     def spot(i):
@@ -1044,6 +1068,8 @@
     gg[...] = jnp.zeros_like(gg)
     for cp in big[:3]:
         cp.wait()
+    for cp in big[3:]:
+        cp.start()
     rs.compute()
     for cp in column(0, 0):
         cp.start()
@@ -1420,18 +1446,14 @@
     at = lax.rem((lax.axis_index("ctx") * nf + lax.axis_index("fsdp")) * R, 128)
     gains = lax.dynamic_slice_in_dim(gains, at, R, 1)
 
-    def kv_rows(g):
-        g = g.astype(f32).reshape(KEY_VALUE_HEADS, rep, R, HD)
-        return jnp.transpose(jnp.sum(g, axis=1), (1, 0, 2)).reshape(R, -1)
-
-    grads = finish_call(gm, ga)
+    grads = finish_call(gm, ga, rep)
     return (
         layer_out[None],
         input_grad[None],
         gains[0],
         grads[3],
-        kv_rows(ga[:, :, KO:VO]),
-        kv_rows(ga[:, :, VO:OO]),
+        grads[5],
+        grads[6],
         grads[4],
         gains[1],
         *grads[:3],

time: 712 us -> 699 us (0.982); the launches traced: 702 us -> 698 us
  transfers between devices with their start and end apart: 2 -> 2, of which waited for: 1 -> 1; matrix products, arithmetic and copies ran while one was open for 6% -> 5% of each run, Pallas kernels for 22% -> 23%
where the time goes in v6:
time: 699 us; the launch traced here: 698 us
  Pallas kernels  631 us (90%)
  other arithmetic  22.5 us (3%)
  local copies, waits for them, and re-layouts  15.5 us (2%)
  waiting for transfers between devices  12.9 us (2%)
  starting transfers between devices  9.06 us (1%)
    pallas_call x1, Pallas kernels, turn_call(): pl.pallas_call(functools.partial(turn_kernel, nc, nf, fold), in_specs=[AN...  189 us
    pallas_call x1, Pallas kernels, middle_call(): pl.pallas_call(functools.partial(middle_kernel, nc, nf, fold), in_specs=[...  180 us
    pallas_call x1, Pallas kernels, close_call(): pl.pallas_call(functools.partial(close_kernel, nc, nf), in_specs=[VM, ANY...  101 us
    pallas_call x1, Pallas kernels, open_call(): pl.pallas_call(functools.partial(open_kernel, nc, nf), in_specs=[ANY] * 1...  97.3 us
    pallas_call x1, Pallas kernels, attn_bwd(): pl.pallas_call(functools.partial(attn_bwd_kernel, nh, tq, tk), grid=(S //...  35.8 us
    pallas_call x1, Pallas kernels, attn_fwd(): pl.pallas_call(functools.partial(attn_fwd_kernel, nh, tq, tk), grid=(S //...  22.5 us
  transfers between devices with their start and end apart: 2, of which 1 were waited for; matrix products, arithmetic and copies ran while one was open for 5% of the time, Pallas kernels for 23%

profile of v6, /device:TPU:0, one launch (start us, length us, event | category | flops | bytes accessed | tf_op | source)
XLA Modules:
  0.0 697.8 jit_solution(3429355081472235713)
XLA Ops:
  0.6 0.7 convert_bitcast_fusion
  1.4 0.6 pad.9.gains
  2.1 0.7 pad_add_fusion
  3.4 97.3 %open_row.1 = (bf16[8,256,2048]{2,1,0:T(8,128)(2,1)}, s32[8,8,256]{2,1,0:T(8,128)}, bf16[8,4,64,768]{3,2,1,0:T(8,128)(2,1)}, bf16[8,64,3072]{2,1,0:T(8,128)(2,1)}) custom-call(bf16[256,2048]{1,0:T(8,128)(2,1)} %bitcast.43, s32[8,256]{1,0:T(8,128)} %pad.8.ids, bf16[64,128]{1,0:T(8,128)(2,1)} %pad.9.gains, f32[64,2048]{1,0:T(8,128)} %wq.1, f32[64,512]{1,0:T(8,128)} %wk.1, ...), custom_call_target="tpu_custom_call" | custom-call | tf_op jit(solution)/shard_map/open_row/pallas_call | solution.py:669
  100.7 4.5 all-to-all-start
  105.1 5.2 multiply_reduce_fusion
  110.4 1.0 convert_reduce_fusion
  111.4 8.5 %fusion.1.n1 = bf16[2048,2048]{1,0:T(8,128)(2,1)} fusion(f32[2048]{0:T(1024)S(1)} %get-tuple-element.70, f32[2048]{0:T(1024)S(1)} %bitcast.66, bf16[8,256,2048]{2,1,0:T(8,128)(2,1)} %get-tuple-element.41), kind=kLoop, calls=%fused_computation.2 | loop fusion | flops 16777216 | bytes 16793600 | tf_op jit(solution)/shard_map/convert_element_type | solution.py:1409
  119.9 5.9 fusion.2
  126.0 0.7 slice.76
  126.8 0.7 fusion.5
  127.4 0.7 add_multiply_fusion
  128.1 1.0 multiply_cosine_fusion
  129.5 0.8 copy-done.1
  130.4 0.7 pad_maximum_fusion
  131.1 2.0 copy.41.k_ref
  133.0 2.0 copy.45
  135.0 1.9 copy.42.v_ref
  136.9 2.3 fusion.4
  139.8 22.5 %attn_fwd.1 = (f32[256,2048]{1,0:T(8,128)}, bf16[256,2048]{1,0:T(8,128)(2,1)}, f32[4,2048]{1,0:T(4,128)}) custom-call(bf16[256,2048]{1,0:T(8,128)(2,1)} %bitcast.59, bf16[2048,64]{1,0:T(8,128)(2,1)} %copy.41.k_ref, bf16[64,2048]{1,0:T(8,128)(2,1)} %copy.42.v_ref, s32[1,2048]{1,0:T(1,128)} %get-tuple-element.82.st_ref, s32[1,2048]{1,0:T(1,128)} %get-tuple-element.81.en_ref), custom_call_target="tpu_custom_call" | custom-call | flops 2147483648 | bytes 4194304 | tf_op jit(solution)/shard_map/attn_fwd/pallas_call | solution.py:80
  162.3 1.5 slice_bitcast_fusion.2
  163.7 12.9 %all-to-all-done.refs_5_ = bf16[8,64,3072]{2,1,0:T(8,128)(2,1)} async-done(((bf16[8,64,3072]{2,1,0:T(8,128)(2,1)}), bf16[8,64,3072]{2,1,0:T(8,128)(2,1)}, u32[]{:S(2)}, u32[]{:S(2)}) %all-to-all-start) | async-done | bytes 3145760 | tf_op jit(solution)/shard_map/all_to_all | solution.py:1386
  176.7 179.9 %attn_to_mlp.1 = (f32[256,2048]{1,0:T(8,128)}, bf16[8,256,2048]{2,1,0:T(8,128)(2,1)}, bf16[8,256,2048]{2,1,0:T(8,128)(2,1)}, bf16[8,4,64,3072]{3,2,1,0:T(8,128)(...) custom-call(bf16[256,2048]{1,0:T(8,128)(2,1)} %get-tuple-element.43.refs_0_.oT, ...), custom_call_target="tpu_custom_call" | custom-call | tf_op jit(solution)/shard_map/attn_to_mlp/pallas_call | solution.py:888
  356.6 188.5 %mlp_to_attn.1 = (f32[256,2048]{1,0:T(8,128)}, bf16[8,256,2048]{2,1,0:T(8,128)(2,1)}, bf16[256,2048]{1,0:T(8,128)(2,1)}, f32[8,2048]{1,0:T(8,128)}, bf16[8,64,30...) custom-call(bf16[2048,2048]{1,0:T(8,128)(2,1)} %bitcast.52, ...), custom_call_target="tpu_custom_call" | custom-call | tf_op jit(solution)/shard_map/mlp_to_attn/pallas_call | solution.py:1151
  545.1 4.6 all-to-all-start.1
  549.7 1.4 copy.43.wo_ref
  551.2 35.8 %attn_bwd.1.dqkv = bf16[384,2048]{1,0:T(8,128)(2,1)} custom-call(bf16[256,2048]{1,0:T(8,128)(2,1)} %bitcast.60, bf16[2048,2048]{1,0:T(8,128)(2,1)} %bitcast.50, bf16[256,2048]{1,0:T(8,128)(2,1)} %copy.43.wo_ref, f32[256,2048]{1,0:T(8,128)} %get-tuple-element.54.o_ref, f32[4,2048]{1,0:T(4,128)} %get-tuple-element.55.lse_ref, ...), custom_call_target="tpu_custom_call" | custom-call | flops 5368709120 | bytes 5242880 | tf_op jit(solution)/shard_map/attn_bwd/pallas_call | solution.py:150
  587.0 101.3 %close_row.1 = (f32[256,2048]{1,0:T(8,128)}, bf16[8,64,640]{2,1,0:T(8,128)(2,1)}, f32[8,128]{1,0:T(8,128)}) custom-call(bf16[384,2048]{1,0:T(8,128)(2,1)} %attn_bwd.1.dqkv, bf16[2048,768]{1,0:T(8,128)(2,1)} %bitcast.46, bf16[256,2048]{1,0:T(8,128)(2,1)} %get-tuple-element.43.refs_0_.oT, bf16[2048,2048]{1,0:T(8,128)(2,1)} %fusion.1.n1, ...), custom_call_target="tpu_custom_call" | custom-call | tf_op jit(solution)/shard_map/close_row/pallas_call | solution.py:1322
  688.4 0.9 constant_dynamic-slice_fusion
  689.8 5.7 finish_rows.1
  695.5 1.0 copy.49
  696.5 1.3 copy.50
  (30 shorter events, 2.5 us)
Async XLA Ops:
  100.7 76.0 %all-to-all-start = ((bf16[8,64,3072]{2,1,0:T(8,128)(2,1)}), bf16[8,64,3072]{2,1,0:T(8,128)(2,1)}, u32[]{:S(2)}, u32[]{:S(2)}) async-start(bf16[8,64,3072]{2,1,0:T(8,128)(2,1)} %get-tuple-element.44), calls=%async_computation | async-start | bytes 6291456 | tf_op jit(solution)/shard_map/all_to_all | solution.py:1386
  105.1 5.3 copy-start
  111.4 8.5 %copy-start.8 = (f32[2048]{0:T(1024)}, f32[2048]{0:T(1024)S(1)}, u32[]{:S(2)}) copy-start(f32[2048]{0:T(1024)S(1)} %get-tuple-element.70) | copy-start | bytes 24580
  125.8 0.9 copy-start.9
  129.1 2.0 copy-start.6
  129.1 3.9 copy-start.5
  129.5 0.8 copy-start.1
  129.5 1.6 copy-start.2
  545.1 4.6 copy-start.3
  545.1 144.7 %all-to-all-start.1 = ((bf16[8,64,3072]{2,1,0:T(8,128)(2,1)}), bf16[8,64,3072]{2,1,0:T(8,128)(2,1)}, u32[]{:S(2)}, u32[]{:S(2)}) async-start(bf16[8,64,3072]{2,1,0:T(8,128)(2,1)} %get-tuple-element.60), calls=%async_computation.1 | async-start | bytes 6291456 | tf_op jit(solution)/shard_map/all_to_all | solution.py:1386
  688.3 7.2 %copy-start.7 = (bf16[256,2048]{1,0:T(8,128)(2,1)S(1)}, bf16[256,2048]{1,0:T(8,128)(2,1)}, u32[]{:S(2)}) copy-start(bf16[256,2048]{1,0:T(8,128)(2,1)} %get-tuple-element.52) | copy-start | bytes 3145732
  688.3 8.1 %copy-start.4 = (f32[256,2048]{1,0:T(8,128)S(1)}, f32[256,2048]{1,0:T(8,128)}, u32[]{:S(2)}) copy-start(f32[256,2048]{1,0:T(8,128)} %get-tuple-element.58) | copy-start | bytes 6291460
